TPU v7x, 32 devices: a whole 2x2x4 slice. The times are simulated.
32 devices in a mesh: dp: 8 (over y, x, core), tensor: 4 (over z).
Axes of the slice: x: 2, y: 2, z: 4, core: 2. Of those that a mesh axis runs over, the one named last changes fastest.
Arguments:
- hidden_in: bfloat16 [4096, 1536], P(('dp', 'tensor')), may hold values from -6 to 6
- positions: int32 [4096], P(('dp', 'tensor')), may hold values from 0 to 511, as said below
- gain_attn: bfloat16 [1536], P(('dp', 'tensor')), may hold values from 0.5 to 1.5
- w_query: bfloat16 [1536, 1536], P(('dp', 'tensor')), may hold values from -0.15625 to 0.15625
- key_matrix: bfloat16 [1536, 768], P(('dp', 'tensor')), may hold values from -0.15625 to 0.15625
- value_matrix: bfloat16 [1536, 768], P(('dp', 'tensor')), may hold values from -0.15625 to 0.15625
- w_output: bfloat16 [1536, 1536], P(('dp', 'tensor')), may hold values from -3.5 to 3.5
- gain_mlp: bfloat16 [1536], P(('dp', 'tensor')), may hold values from 0.5 to 1.5
- w_gate: bfloat16 [1536, 4096], P(None, 'tensor'), may hold values from -0.15625 to 0.15625
- w_up: bfloat16 [1536, 4096], P(None, 'tensor'), may hold values from -0.15625 to 0.15625
- w_down: bfloat16 [4096, 1536], P('tensor'), may hold values from -0.09375 to 0.09375
- cotangent: bfloat16 [4096, 1536], P(('dp', 'tensor')), may hold values from -6 to 6
Outputs:
- layer_out: bfloat16 [4096, 1536], P(('dp', 'tensor'))
- grad_input: float32 [4096, 1536], P(('dp', 'tensor'))
- grad_gain_attn: float32 [1536], P(('dp', 'tensor'))
- grad_w_query: float32 [1536, 1536], P(('dp', 'tensor'))
- grad_w_key: float32 [1536, 768], P(('dp', 'tensor'))
- grad_w_value: float32 [1536, 768], P(('dp', 'tensor'))
- grad_w_output: float32 [1536, 1536], P(('dp', 'tensor'))
- grad_gain_mlp: float32 [1536], P(('dp', 'tensor'))
- grad_w_gate: float32 [1536, 4096], P('dp', 'tensor')
- grad_w_up: float32 [1536, 4096], P('dp', 'tensor')
- grad_w_down: float32 [4096, 1536], P('tensor', 'dp')
Inputs may be any that keep to these rules, and one draw needn't show every extreme that they name: positions is 0 at the first token of every document and at every sequence's first row (multiples of 512), and rises by one from each token to the next within a document; documents are runs of consecutive tokens; the first sequence is a single document of 512 tokens.
All inputs are finite; a program needn't handle non-finite values.
Results may differ from a plain program's by a relative error of at most 0.015.
Values may be sent and summed in bfloat16 or wider, within the bound.
A program may use at most 192 MiB of HBM per device.

v0:
```python
import math

import jax
import jax.numpy as jnp
from jax import lax
from jax.sharding import PartitionSpec as P

QUERY_HEADS = 16
KEY_VALUE_HEADS = 8
HEAD_DIMENSION = 96


EPSILON = 1e-05
ROPE_BASE = 100000.0
MASKED = -1e30


def angle_tables(pos_rows, head_size):
    half_size = head_size // 2
    freq_rates = ROPE_BASE ** (-(jnp.arange(half_size, dtype=jnp.float32) * 2.0) / head_size)
    turned = pos_rows.astype(jnp.float32)[:, None] * freq_rates[None, :]
    return (jnp.cos(turned)[:, None, :], jnp.sin(turned)[:, None, :])


def apply_rotary(tensor_in, cosine_table, sine_table):
    half_size = tensor_in.shape[-1] // 2
    lo_half = tensor_in[..., :half_size]
    hi_half = tensor_in[..., half_size:]
    return jnp.concatenate(
        [
            lo_half * cosine_table - hi_half * sine_table,
            hi_half * cosine_table + lo_half * sine_table,
        ],
        axis=-1,
    )


def shards(
    hidden_in,
    positions,
    gain_attn,
    w_query,
    key_matrix,
    value_matrix,
    w_output,
    gain_mlp,
    w_gate,
    w_up,
    w_down,
    cotangent,
):
    tok_rows = hidden_in.shape[0]
    model_width = hidden_in.shape[1]
    num_heads = QUERY_HEADS
    key_value_count = KEY_VALUE_HEADS
    head_size = HEAD_DIMENSION
    kv_width = key_value_count * head_size
    queries_per_group = num_heads // key_value_count
    seq_len = tok_rows * lax.axis_size("tensor")
    score_scale = 1.0 / math.sqrt(head_size)
    gathered = (
        lax.all_gather(gain_attn, ("dp", "tensor"), axis=0, tiled=True),
        lax.all_gather(w_query, ("dp", "tensor"), axis=0, tiled=True),
        lax.all_gather(key_matrix, ("dp", "tensor"), axis=0, tiled=True),
        lax.all_gather(value_matrix, ("dp", "tensor"), axis=0, tiled=True),
        lax.all_gather(w_output, ("dp", "tensor"), axis=0, tiled=True),
        lax.all_gather(gain_mlp, ("dp", "tensor"), axis=0, tiled=True),
    )
    gain_one, query_full, key_full, value_full, output_full, gain_two = gathered
    gain_one_f = gain_one.astype(jnp.float32)
    gain_two_f = gain_two.astype(jnp.float32)
    x_float = hidden_in.astype(jnp.float32)
    inv_one = lax.rsqrt(jnp.mean(x_float * x_float, axis=-1, keepdims=True) + EPSILON)
    normed_one = (x_float * inv_one * gain_one_f).astype(jnp.bfloat16)
    queries = jnp.dot(normed_one, query_full, preferred_element_type=jnp.float32)
    key_projected = jnp.dot(normed_one, key_full, preferred_element_type=jnp.float32)
    value_proj = jnp.dot(normed_one, value_full, preferred_element_type=jnp.float32)
    cosine_table, sine_table = angle_tables(positions, head_size)
    rotated_query_rows = apply_rotary(
        queries.reshape(tok_rows, num_heads, head_size), cosine_table, sine_table
    ).astype(jnp.bfloat16)
    rotated_key_rows = (
        apply_rotary(
            key_projected.reshape(tok_rows, key_value_count, head_size), cosine_table, sine_table
        )
        .astype(jnp.bfloat16)
        .reshape(tok_rows, kv_width)
    )
    value_rows_lowered = value_proj.astype(jnp.bfloat16)
    keys_all, values_all = (
        lax.all_gather(rotated_key_rows, "tensor", axis=0, tiled=True),
        lax.all_gather(value_rows_lowered, "tensor", axis=0, tiled=True),
    )
    offset = lax.axis_index("tensor") * tok_rows
    query_index = offset + jnp.arange(tok_rows, dtype=jnp.int32)
    key_index = jnp.arange(seq_len, dtype=jnp.int32)
    visible = (key_index[None, :] <= query_index[:, None]) & (
        key_index[None, :] >= (query_index - positions)[:, None]
    )
    visible = jnp.tile(visible, (queries_per_group, 1))

    def split_queries(tensor_in):
        return (
            tensor_in.reshape(tok_rows, key_value_count, queries_per_group, head_size)
            .transpose(1, 2, 0, 3)
            .reshape(key_value_count, queries_per_group * tok_rows, head_size)
        )

    def split_keys(tensor_in):
        return tensor_in.reshape(seq_len, key_value_count, head_size).transpose(1, 0, 2)

    def merge_heads(tensor_in):
        return (
            tensor_in.reshape(key_value_count, queries_per_group, tok_rows, head_size)
            .transpose(2, 0, 1, 3)
            .reshape(tok_rows, model_width)
        )

    query_heads = split_queries(rotated_query_rows)
    k_heads = split_keys(keys_all)
    value_heads = split_keys(values_all)

    def attend(head_items):
        q_block, k_block, v_block = head_items
        scores = (
            jnp.einsum("qd,kd->qk", q_block, k_block, preferred_element_type=jnp.float32)
            * score_scale
        )
        scores = jnp.where(visible, scores, MASKED)
        peak = jnp.max(scores, axis=-1, keepdims=True)
        exp_vals = jnp.exp(scores - peak)
        total = jnp.sum(exp_vals, axis=-1, keepdims=True)
        probs = exp_vals / total
        out_block = jnp.einsum(
            "qk,kd->qd", probs.astype(jnp.bfloat16), v_block, preferred_element_type=jnp.float32
        )
        return (out_block, peak[:, 0] + jnp.log(total[:, 0]))

    attended_rows, log_total = lax.map(attend, (query_heads, k_heads, value_heads))
    attended_low = merge_heads(attended_rows).astype(jnp.bfloat16)
    resid_sum = x_float + jnp.dot(attended_low, output_full, preferred_element_type=jnp.float32)
    inv_two = lax.rsqrt(jnp.mean(resid_sum * resid_sum, axis=-1, keepdims=True) + EPSILON)
    normed_two = (resid_sum * inv_two * gain_two_f).astype(jnp.bfloat16)
    rows_all = lax.all_gather(normed_two, "tensor", axis=0, tiled=True)
    gate_val = jnp.dot(rows_all, w_gate, preferred_element_type=jnp.float32)
    up_val = jnp.dot(rows_all, w_up, preferred_element_type=jnp.float32)
    sig_gate = jax.nn.sigmoid(gate_val)
    silu_gate = gate_val * sig_gate
    act_low = (silu_gate * up_val).astype(jnp.bfloat16)
    mlp_sum = lax.psum_scatter(
        jnp.dot(act_low, w_down, preferred_element_type=jnp.float32).astype(jnp.bfloat16),
        "tensor",
        scatter_dimension=0,
        tiled=True,
    ).astype(jnp.float32)
    layer_out = (resid_sum + mlp_sum).astype(jnp.bfloat16)
    grad_float = cotangent.astype(jnp.float32)
    grad_all = lax.all_gather(cotangent, "tensor", axis=0, tiled=True)
    grad_down = jnp.einsum("sf,sd->fd", act_low, grad_all, preferred_element_type=jnp.float32)
    g_act = jnp.einsum("sd,fd->sf", grad_all, w_down, preferred_element_type=jnp.float32)
    g_gate = (g_act * up_val * sig_gate * (1.0 + gate_val * (1.0 - sig_gate))).astype(jnp.bfloat16)
    g_up = (g_act * silu_gate).astype(jnp.bfloat16)
    grad_gate = jnp.einsum("sd,sf->df", rows_all, g_gate, preferred_element_type=jnp.float32)
    grad_up = jnp.einsum("sd,sf->df", rows_all, g_up, preferred_element_type=jnp.float32)
    g_norm_two = lax.psum_scatter(
        (
            jnp.einsum("sf,df->sd", g_gate, w_gate, preferred_element_type=jnp.float32)
            + jnp.einsum("sf,df->sd", g_up, w_up, preferred_element_type=jnp.float32)
        ).astype(jnp.bfloat16),
        "tensor",
        scatter_dimension=0,
        tiled=True,
    ).astype(jnp.float32)
    scaled_two = gain_two_f * g_norm_two
    grad_gain_two = jnp.sum(g_norm_two * resid_sum * inv_two, axis=0)
    g_resid = (
        grad_float
        + inv_two * scaled_two
        - resid_sum * inv_two**3 * jnp.mean(scaled_two * resid_sum, axis=-1, keepdims=True)
    )
    g_resid_low = g_resid.astype(jnp.bfloat16)
    grad_output = jnp.einsum(
        "tc,td->cd", attended_low, g_resid_low, preferred_element_type=jnp.float32
    )
    g_att = jnp.einsum(
        "td,cd->tc", g_resid_low, output_full, preferred_element_type=jnp.float32
    ).astype(jnp.bfloat16)
    g_heads = split_queries(g_att)

    def attend_back(head_items):
        q_block, k_block, v_block, log_block, g_block = head_items
        scores = (
            jnp.einsum("qd,kd->qk", q_block, k_block, preferred_element_type=jnp.float32)
            * score_scale
        )
        scores = jnp.where(visible, scores, MASKED)
        probs = jnp.exp(scores - log_block[:, None])
        g_probs = jnp.einsum("qd,kd->qk", g_block, v_block, preferred_element_type=jnp.float32)
        g_scores = (probs * (g_probs - jnp.sum(probs * g_probs, axis=-1, keepdims=True))).astype(
            jnp.bfloat16
        )
        g_rq = (
            jnp.einsum("qk,kd->qd", g_scores, k_block, preferred_element_type=jnp.float32)
            * score_scale
        )
        g_rk = (
            jnp.einsum("qk,qd->kd", g_scores, q_block, preferred_element_type=jnp.float32)
            * score_scale
        )
        g_val = jnp.einsum(
            "qk,qd->kd", probs.astype(jnp.bfloat16), g_block, preferred_element_type=jnp.float32
        )
        return (g_rq, g_rk, g_val)

    g_rq, g_rk, g_val = lax.map(
        attend_back, (query_heads, k_heads, value_heads, log_total, g_heads)
    )
    g_rk_flat = g_rk.transpose(1, 0, 2).reshape(seq_len, kv_width)
    g_val_flat = g_val.transpose(1, 0, 2).reshape(seq_len, kv_width)
    key_part, value_part = (
        lax.psum_scatter(
            g_rk_flat.astype(jnp.bfloat16), "tensor", scatter_dimension=0, tiled=True
        ).astype(jnp.float32),
        lax.psum_scatter(
            g_val_flat.astype(jnp.bfloat16), "tensor", scatter_dimension=0, tiled=True
        ).astype(jnp.float32),
    )
    g_queries = (
        apply_rotary(
            merge_heads(g_rq).reshape(tok_rows, num_heads, head_size), cosine_table, -sine_table
        )
        .reshape(tok_rows, model_width)
        .astype(jnp.bfloat16)
    )
    g_keys = (
        apply_rotary(
            key_part.reshape(tok_rows, key_value_count, head_size), cosine_table, -sine_table
        )
        .reshape(tok_rows, kv_width)
        .astype(jnp.bfloat16)
    )
    g_values = value_part.astype(jnp.bfloat16)
    grad_query = jnp.einsum("tc,td->cd", normed_one, g_queries, preferred_element_type=jnp.float32)
    grad_key = jnp.einsum("tc,td->cd", normed_one, g_keys, preferred_element_type=jnp.float32)
    grad_value = jnp.einsum("tc,td->cd", normed_one, g_values, preferred_element_type=jnp.float32)
    g_norm_one = (
        jnp.einsum("td,cd->tc", g_queries, query_full, preferred_element_type=jnp.float32)
        + jnp.einsum("td,cd->tc", g_keys, key_full, preferred_element_type=jnp.float32)
        + jnp.einsum("td,cd->tc", g_values, value_full, preferred_element_type=jnp.float32)
    )
    scaled_one = gain_one_f * g_norm_one
    grad_gain_one = jnp.sum(g_norm_one * x_float * inv_one, axis=0)
    grad_input = (
        g_resid
        + inv_one * scaled_one
        - x_float * inv_one**3 * jnp.mean(scaled_one * x_float, axis=-1, keepdims=True)
    )
    query_part, keyw_part, valuew_part, out_part, gain_one_part, gain_two_part = (
        lax.psum_scatter(grad_query, ("dp", "tensor"), scatter_dimension=0, tiled=True),
        lax.psum_scatter(grad_key, ("dp", "tensor"), scatter_dimension=0, tiled=True),
        lax.psum_scatter(grad_value, ("dp", "tensor"), scatter_dimension=0, tiled=True),
        lax.psum_scatter(grad_output, ("dp", "tensor"), scatter_dimension=0, tiled=True),
        lax.psum_scatter(grad_gain_one, ("dp", "tensor"), scatter_dimension=0, tiled=True),
        lax.psum_scatter(grad_gain_two, ("dp", "tensor"), scatter_dimension=0, tiled=True),
    )
    gate_sum, up_sum, down_sum = (
        lax.psum_scatter(grad_gate, "dp", scatter_dimension=0, tiled=True),
        lax.psum_scatter(grad_up, "dp", scatter_dimension=0, tiled=True),
        lax.psum_scatter(grad_down, "dp", scatter_dimension=1, tiled=True),
    )
    return (
        layer_out,
        grad_input,
        gain_one_part,
        query_part,
        keyw_part,
        valuew_part,
        out_part,
        gain_two_part,
        gate_sum,
        up_sum,
        down_sum,
    )


def solution(mesh):
    placed = (
        P(("dp", "tensor"), None),
        P(("dp", "tensor")),
        P(("dp", "tensor")),
        P(("dp", "tensor"), None),
        P(("dp", "tensor"), None),
        P(("dp", "tensor"), None),
        P(("dp", "tensor"), None),
        P(("dp", "tensor")),
        P(None, "tensor"),
        P(None, "tensor"),
        P("tensor", None),
        P(("dp", "tensor"), None),
    )
    return jax.shard_map(
        shards,
        mesh=mesh,
        in_specs=placed,
        out_specs=(
            P(("dp", "tensor"), None),
            P(("dp", "tensor"), None),
            P(("dp", "tensor")),
            P(("dp", "tensor"), None),
            P(("dp", "tensor"), None),
            P(("dp", "tensor"), None),
            P(("dp", "tensor"), None),
            P(("dp", "tensor")),
            P("dp", "tensor"),
            P("dp", "tensor"),
            P("tensor", "dp"),
        ),
        check_vma=False,
    )
```

profile of v0, /device:TPU:4, one launch (start us, length us, event | category | flops | bytes accessed | tf_op | source)
XLA Modules:
  0.0 1253.4 jit_solution(6569822728411166291)
XLA Ops:
  12.6 41.4 %all-reduce.5 = (bf16[1536]{0:T(1024)(128)(2,1)S(1)}, bf16[1536]{0:T(1024)(128)(2,1)S(1)}) all-reduce(bf16[1536]{0:T(1024)(128)(2,1)S(1)} %dynamic-update-slice, bf16[1536]{0:T(1024)(128)(2,1)S(1)} %dynamic-update-slice.1), channel_id=1, replica_groups=mesh['dp'=8,'tensor'=4] {'dp','tensor'}, use_global_device_ids=true, to_apply=%add | all-reduce | flops 3072 | bytes 12288
  58.0 11.1 all-gather.9.cloned.1.call-done
  72.1 19.5 %all_gather.33 = bf16[512,768]{0,1:T(8,128)(2,1)} all-gather(bf16[128,768]{0,1:T(8,128)(2,1)S(1)} %bitcast.215), channel_id=1, replica_groups=mesh['dp'=8,'tensor'=4] {'tensor'}, dimensions={0}, use_global_device_ids=true | all-gather | bytes 983040 | tf_op jit(solution)/shard_map/all_gather | solution.py:91
  93.8 35.9 %all-gather.11.cloned.1.call-done = bf16[1536,768]{1,0:T(8,128)(2,1)} async-done(((bf16[48,768]{1,0:T(8,128)(2,1)}), bf16[1536,768]{1,0:T(8,128)(2,1)}) %all-gather.11.cloned.1.call-update) | async-done | bytes 2359312 | tf_op jit(solution)/shard_map/all_gather | solution.py:65
  132.0 21.3 %all_gather.35 = bf16[512,768]{1,0:T(8,128)(2,1)} all-gather(bf16[128,768]{1,0:T(8,128)(2,1)S(1)} %convolution_convert_fusion.2), channel_id=1, replica_groups=mesh['dp'=8,'tensor'=4] {'tensor'}, dimensions={0}, use_global_device_ids=true | all-gather | bytes 983040 | tf_op jit(solution)/shard_map/all_gather | solution.py:92
  157.8 38.5 %all-gather.7.cloned.1.call-done = bf16[1536,1536]{1,0:T(8,128)(2,1)} async-done(((bf16[48,1536]{1,0:T(8,128)(2,1)}), bf16[1536,1536]{1,0:T(8,128)(2,1)}) %all-gather.7.cloned.1.call-update) | async-done | bytes 4718608 | tf_op jit(solution)/shard_map/all_gather | solution.py:63
  203.5 48.9 %while.30 = (s32[]{:T(128)}, bf16[8,256,96]{1,2,0:T(8,128)(2,1)}, f32[8,256]{1,0:T(8,128)}, bf16[8,256,96]{2,1,0:T(8,128)(2,1)}, bf16[8,512,96]{2,1,0:T(8,128)(2...) while((s32[]{:T(128)}, bf16[8,256,96]{1,2,0:T(8,128)(2,1)}, ...), condition=%wide.region_4.5_spmd.clone.clone, body=%wide.region_1.4_spmd.clone.sunk.clone | while | flops 51379968 | bytes 2338905 | solution.py:139
  266.9 34.8 %all-gather.15.cloned.1.call-done = bf16[512,1536]{1,0:T(8,128)(2,1)} async-done(((bf16[128,1536]{1,0:T(8,128)(2,1)}), bf16[512,1536]{1,0:T(8,128)(2,1)}) %all-gather.15.cloned.1.call-update) | async-done | bytes 1572880 | tf_op jit(solution)/shard_map/all_gather | solution.py:144
  310.5 28.6 %all-gather.17.cloned.1.call-done = bf16[512,1536]{1,0:T(8,128)(2,1)} async-done(((bf16[128,1536]{1,0:T(8,128)(2,1)}), bf16[512,1536]{1,0:T(8,128)(2,1)}) %all-gather.17.cloned.1.call-update) | async-done | bytes 1572880 | tf_op jit(solution)/shard_map/all_gather | solution.py:158
  339.0 6.3 multiply_convert_fusion.1
  355.4 30.1 %reduce-scatter.18.cloned.1.call-done = bf16[128,1536]{1,0:T(8,128)(2,1)} async-done(((bf16[512,1536]{1,0:T(8,128)(2,1)}), bf16[128,1536]{1,0:T(8,128)(2,1)}) %reduce-scatter.18.cloned.1.call-update) | async-done | bytes 393232 | tf_op jit(solution)/shard_map/reduce_scatter | solution.py:165
  387.6 34.5 %reduce-scatter.16.cloned.1.call-done = bf16[128,1536]{1,0:T(8,128)(2,1)} async-done(((bf16[512,1536]{1,0:T(8,128)(2,1)}), bf16[128,1536]{1,0:T(8,128)(2,1)}) %reduce-scatter.16.cloned.1.call-update) | async-done | bytes 393232 | tf_op jit(solution)/shard_map/reduce_scatter | solution.py:150
  429.1 61.5 %while.31 = (s32[]{:T(128)}, f32[8,256,96]{1,2,0:T(8,128)}, bf16[8,512,96]{1,2,0:T(8,128)(2,1)}, bf16[8,512,96]{1,2,0:T(8,128)(2,1)}, bf16[8,256,96]{2,1,0:T(8,1...) while((s32[]{:T(128)}, f32[8,256,96]{1,2,0:T(8,128)}, ...), condition=%wide.region_11.12_spmd.clone.clone, body=%wide.region_9.11_spmd.clone.sunk.clone | while | flops 127082240 | bytes 5417073 | solution.py:215
  501.7 5.9 fusion.86
  508.9 6.0 fusion.87
  519.7 20.4 %reduce-scatter.36.cloned.1.call-done = bf16[128,768]{1,0:T(8,128)(2,1)} async-done(((bf16[512,768]{1,0:T(8,128)(2,1)}), bf16[128,768]{1,0:T(8,128)(2,1)}) %reduce-scatter.36.cloned.1.call-update) | async-done | bytes 196624
  551.6 6.0 fusion.64
  566.1 41.8 %all-reduce.4 = (f32[1536]{0:T(1024)}, f32[1536]{0:T(1024)}) all-reduce(f32[1536]{0:T(1024)} %get-tuple-element.201, f32[1536]{0:T(1024)} %get-tuple-element.199), channel_id=6, replica_groups=mesh['dp'=8,'tensor'=4] {'dp','tensor'}, use_global_device_ids=true, to_apply=%region_16.17.clone | all-reduce | flops 3072 | bytes 24576
  613.0 59.3 %reduce-scatter.30.cloned.1.call-done = f32[192,1024]{1,0:T(8,128)} async-done(((f32[1536,1024]{1,0:T(8,128)}), f32[192,1024]{1,0:T(8,128)}) %reduce-scatter.30.cloned.1.call-update) | async-done | bytes 786448 | tf_op jit(solution)/shard_map/reduce_scatter | solution.py:268
  672.2 65.7 %reduce-scatter.32.cloned.1.call-done = f32[1024,192]{0,1:T(8,128)} async-done(((f32[1024,1536]{0,1:T(8,128)}), f32[1024,192]{0,1:T(8,128)}) %reduce-scatter.32.cloned.1.call-update) | async-done | bytes 786448 | tf_op jit(solution)/shard_map/reduce_scatter | solution.py:269
  738.0 113.3 %reduce-scatter.22.cloned.1.call-done = f32[48,768]{1,0:T(8,128)} async-done(((f32[1536,768]{1,0:T(8,128)}), f32[48,768]{1,0:T(8,128)}) %reduce-scatter.22.cloned.1.call-update) | async-done | bytes 147472 | tf_op jit(solution)/shard_map/reduce_scatter | solution.py:260
  851.3 112.5 %reduce-scatter.24.cloned.1.call-done = f32[48,768]{1,0:T(8,128)} async-done(((f32[1536,768]{1,0:T(8,128)}), f32[48,768]{1,0:T(8,128)}) %reduce-scatter.24.cloned.1.call-update) | async-done | bytes 147472 | tf_op jit(solution)/shard_map/reduce_scatter | solution.py:261
  963.7 141.7 %reduce-scatter.20.cloned.1.call-done = f32[48,1536]{1,0:T(8,128)} async-done(((f32[1536,1536]{1,0:T(8,128)}), f32[48,1536]{1,0:T(8,128)}) %reduce-scatter.20.cloned.1.call-update) | async-done | bytes 294928 | tf_op jit(solution)/shard_map/reduce_scatter | solution.py:259
  1105.4 141.5 %reduce-scatter.26.cloned.1.call-done = f32[48,1536]{1,0:T(8,128)} async-done(((f32[1536,1536]{1,0:T(8,128)}), f32[48,1536]{1,0:T(8,128)}) %reduce-scatter.26.cloned.1.call-update) | async-done | bytes 294928 | tf_op jit(solution)/shard_map/reduce_scatter | solution.py:262
  (282 shorter events, 222.9 us)
Async XLA Ops:
  7.2 331.9 %copy-start = (bf16[1024,1536]{1,0:T(8,128)(2,1)S(1)}, bf16[1024,1536]{1,0:T(8,128)(2,1)}, u32[]{:S(2)}) copy-start(bf16[1024,1536]{1,0:T(8,128)(2,1)} %param.26) | copy-start | bytes 9437188
  7.2 61.9 %all-gather.9.cloned.1.call-start = ((), (), s32[]{:S(2)}) async-start(), calls=%async_computation.12 | async-start | bytes 2433024 | tf_op jit(solution)/shard_map/all_gather | solution.py:64
  7.9 121.9 %all-gather.11.cloned.1.call-start = ((), (), s32[]{:S(2)}) async-start(), calls=%async_computation.13 | async-start | bytes 2433024 | tf_op jit(solution)/shard_map/all_gather | solution.py:65
  8.7 187.6 %all-gather.7.cloned.1.call-start = ((), (), s32[]{:S(2)}) async-start(), calls=%async_computation.11 | async-start | bytes 4866048 | tf_op jit(solution)/shard_map/all_gather | solution.py:63
  9.4 251.4 %all-gather.13.cloned.1.call-start = ((), (), s32[]{:S(2)}) async-start(), calls=%async_computation.14 | async-start | bytes 4866048 | tf_op jit(solution)/shard_map/all_gather | solution.py:66
  10.0 291.7 %all-gather.15.cloned.1.call-start = ((), (), s32[]{:S(2)}) async-start(), calls=%async_computation.15 | async-start | bytes 1966080 | tf_op jit(solution)/shard_map/all_gather | solution.py:144
  266.1 72.9 %all-gather.17.cloned.1.call-start = ((), (), s32[]{:S(2)}) async-start(), calls=%async_computation.17 | async-start | bytes 1966080 | tf_op jit(solution)/shard_map/all_gather | solution.py:158
  266.7 118.8 %reduce-scatter.18.cloned.1.call-start = ((), (), s32[]{:S(2)}) async-start(), calls=%async_computation.18 | async-start | bytes 1966080 | tf_op jit(solution)/shard_map/reduce_scatter | solution.py:165
  351.0 71.1 %reduce-scatter.16.cloned.1.call-start = ((), (), s32[]{:S(2)}) async-start(), calls=%async_computation.16 | async-start | bytes 1966080 | tf_op jit(solution)/shard_map/reduce_scatter | solution.py:150
  355.3 66.8 %copy-start.4 = (f32[128,1536]{1,0:T(8,128)S(1)}, f32[128,1536]{1,0:T(8,128)}, u32[]{:S(2)}) copy-start(f32[128,1536]{1,0:T(8,128)} %copy-done.3) | copy-start | bytes 2359300
  355.3 66.8 %copy-start.10 = (bf16[128,1536]{1,0:T(8,128)(2,1)S(1)}, bf16[128,1536]{1,0:T(8,128)(2,1)}, u32[]{:S(2)}) copy-start(bf16[128,1536]{1,0:T(8,128)(2,1)} %param.27) | copy-start | bytes 1179652
  355.3 66.8 %copy-start.23 = (f32[128]{0:T(128)S(1)}, f32[128]{0:T(128)}, u32[]{:S(2)}) copy-start(f32[128]{0:T(128)} %copy-done.22) | copy-start | bytes 1540
  355.3 66.8 %copy-start.24 = (f32[128]{0:T(128)S(1)}, f32[128]{0:T(128)}, u32[]{:S(2)}) copy-start(f32[128]{0:T(128)} %get-tuple-element.263) | copy-start | bytes 1540
  355.4 159.9 %reduce-scatter.34.cloned.1.call-start = ((), (), s32[]{:S(2)}) async-start(), calls=%async_computation.26 | async-start | bytes 983040
  424.3 126.6 %copy-start.5 = (f32[128,1536]{1,0:T(8,128)}, f32[128,1536]{1,0:T(8,128)S(1)}, u32[]{:S(2)}) copy-start(f32[128,1536]{1,0:T(8,128)S(1)} %get-tuple-element.252) | copy-start | bytes 2359300
  493.1 47.0 %reduce-scatter.36.cloned.1.call-start = ((), (), s32[]{:S(2)}) async-start(), calls=%async_computation.27 | async-start | bytes 983040
  494.3 118.6 %reduce-scatter.28.cloned.1.call-start = ((), (), s32[]{:S(2)}) async-start(), calls=%async_computation.23 | async-start | bytes 7077888 | tf_op jit(solution)/shard_map/reduce_scatter | solution.py:267
  500.5 171.7 %reduce-scatter.30.cloned.1.call-start = ((), (), s32[]{:S(2)}) async-start(), calls=%async_computation.24 | async-start | bytes 7077888 | tf_op jit(solution)/shard_map/reduce_scatter | solution.py:268
  507.7 230.3 %reduce-scatter.32.cloned.1.call-start = ((), (), s32[]{:S(2)}) async-start(), calls=%async_computation.25 | async-start | bytes 7077888 | tf_op jit(solution)/shard_map/reduce_scatter | solution.py:269
  514.9 336.4 %reduce-scatter.22.cloned.1.call-start = ((), (), s32[]{:S(2)}) async-start(), calls=%async_computation.20 | async-start | bytes 4866048 | tf_op jit(solution)/shard_map/reduce_scatter | solution.py:260
  519.6 444.1 %reduce-scatter.24.cloned.1.call-start = ((), (), s32[]{:S(2)}) async-start(), calls=%async_computation.21 | async-start | bytes 4866048 | tf_op jit(solution)/shard_map/reduce_scatter | solution.py:261
  544.0 561.4 %reduce-scatter.20.cloned.1.call-start = ((), (), s32[]{:S(2)}) async-start(), calls=%async_computation.19 | async-start | bytes 9732096 | tf_op jit(solution)/shard_map/reduce_scatter | solution.py:259
  550.6 696.3 %reduce-scatter.26.cloned.1.call-start = ((), (), s32[]{:S(2)}) async-start(), calls=%async_computation.22 | async-start | bytes 9732096 | tf_op jit(solution)/shard_map/reduce_scatter | solution.py:262
  563.6 683.3 %copy-start.1 = (bf16[1024,1536]{1,0:T(8,128)(2,1)S(1)}, bf16[1024,1536]{1,0:T(8,128)(2,1)}, u32[]{:S(2)}) copy-start(bf16[1024,1536]{1,0:T(8,128)(2,1)} %param.26) | copy-start | bytes 9437188
  (27 other events, 139.4 us)
Sparse Core Ops, SparseCore 0:
  10.8 58.2 all-gather.8
  71.9 57.8 all-gather.10
  132.6 63.6 all-gather.6
  198.9 61.8 all-gather.12
  266.2 35.3 all-gather.14
  303.1 35.8 all-gather.16
  351.1 34.2 reduce-scatter.17
  387.8 34.2 reduce-scatter.15
  493.2 21.9 reduce-scatter.33
  517.4 22.6 reduce-scatter.35
  544.1 62.3 reduce-scatter.27
  610.3 61.9 reduce-scatter.29
  676.2 61.7 reduce-scatter.31
  743.9 107.3 reduce-scatter.21
  857.2 106.5 reduce-scatter.23
  970.0 135.3 reduce-scatter.19
  1111.7 135.1 reduce-scatter.25
where the time goes:
time: 1260 us; the launch traced here: 1250 us
  waiting for transfers between devices  876 us (70%)
  matrix products  164 us (13%)
  blocking collectives  124 us (10%)
  local copies, waits for them, and re-layouts  51.5 us (4%)
  other arithmetic  21.6 us (2%)
  between operations  14.4 us (1%)
    reduce_scatter x1, waiting for transfers between devices, shards(): lax.psum_scatter(grad_query, ('dp', 'tensor'), scatter_dimension=0, tiled...  142 us
    reduce_scatter x1, waiting for transfers between devices, shards(): lax.psum_scatter(grad_output, ('dp', 'tensor'), scatter_dimension=0, tile...  141 us
    reduce_scatter x1, waiting for transfers between devices, shards(): lax.psum_scatter(grad_key, ('dp', 'tensor'), scatter_dimension=0, tiled=T...  113 us
    reduce_scatter x1, waiting for transfers between devices, shards(): lax.psum_scatter(grad_value, ('dp', 'tensor'), scatter_dimension=0, tiled...  112 us
    unnamed x2, blocking collectives  83.2 us
    reduce_scatter x1, waiting for transfers between devices, shards(): lax.psum_scatter(grad_down, 'dp', scatter_dimension=1, tiled=True)  65.7 us
    reduce_scatter x1, waiting for transfers between devices, shards(): lax.psum_scatter(grad_up, 'dp', scatter_dimension=0, tiled=True)  59.3 us
    all_gather x1, waiting for transfers between devices, shards(): lax.all_gather(w_query, ('dp', 'tensor'), axis=0, tiled=True)  38.5 us
  transfers between devices with their start and end apart: 17, of which 16 were waited for; matrix products, arithmetic and copies ran while one was open for 12% of the time, Pallas kernels for 0%

commit v1 on v0

--- a/solution.py
+++ b/solution.py
@@ -255,18 +255,28 @@
         + inv_one * scaled_one
         - x_float * inv_one**3 * jnp.mean(scaled_one * x_float, axis=-1, keepdims=True)
     )
-    query_part, keyw_part, valuew_part, out_part, gain_one_part, gain_two_part = (
-        lax.psum_scatter(grad_query, ("dp", "tensor"), scatter_dimension=0, tiled=True),
-        lax.psum_scatter(grad_key, ("dp", "tensor"), scatter_dimension=0, tiled=True),
-        lax.psum_scatter(grad_value, ("dp", "tensor"), scatter_dimension=0, tiled=True),
-        lax.psum_scatter(grad_output, ("dp", "tensor"), scatter_dimension=0, tiled=True),
+    packed = jnp.concatenate([grad_query, grad_key, grad_value, grad_output], axis=1)
+    packed_part = lax.psum_scatter(
+        packed.astype(jnp.bfloat16), ("dp", "tensor"), scatter_dimension=0, tiled=True
+    ).astype(jnp.float32)
+    query_part = packed_part[:, :model_width]
+    keyw_part = packed_part[:, model_width : model_width + kv_width]
+    valuew_part = packed_part[:, model_width + kv_width : model_width + 2 * kv_width]
+    out_part = packed_part[:, model_width + 2 * kv_width :]
+    gain_one_part, gain_two_part = (
         lax.psum_scatter(grad_gain_one, ("dp", "tensor"), scatter_dimension=0, tiled=True),
         lax.psum_scatter(grad_gain_two, ("dp", "tensor"), scatter_dimension=0, tiled=True),
     )
     gate_sum, up_sum, down_sum = (
-        lax.psum_scatter(grad_gate, "dp", scatter_dimension=0, tiled=True),
-        lax.psum_scatter(grad_up, "dp", scatter_dimension=0, tiled=True),
-        lax.psum_scatter(grad_down, "dp", scatter_dimension=1, tiled=True),
+        lax.psum_scatter(
+            grad_gate.astype(jnp.bfloat16), "dp", scatter_dimension=0, tiled=True
+        ).astype(jnp.float32),
+        lax.psum_scatter(
+            grad_up.astype(jnp.bfloat16), "dp", scatter_dimension=0, tiled=True
+        ).astype(jnp.float32),
+        lax.psum_scatter(
+            grad_down.astype(jnp.bfloat16), "dp", scatter_dimension=1, tiled=True
+        ).astype(jnp.float32),
     )
     return (
         layer_out,

time: 1260 us -> 883 us (0.70)
  waiting for transfers between devices: 876 us -> 468 us
  local copies, waits for them, and re-layouts: 51.5 us -> 80.7 us
  other arithmetic: 21.6 us -> 35.5 us
    reduce_scatter x7 -> x3, waiting for transfers between devices: 634 us -> 64.6 us  [the longest x1 47.5 us: shards(): lax.psum_scatter(grad_gate.astype(jnp.bfloat16), 'dp', scatter_dimension=...]
    unnamed x19 -> x17, waiting for transfers between devices: 24 us -> 184 us
    unnamed x80 -> x76, local copies, waits for them, and re-layouts: 19.9 us -> 44.9 us
  transfers between devices with their start and end apart: 17 -> 14, of which waited for: 16 -> 12; matrix products, arithmetic and copies ran while one was open for 12% -> 19% of each run, Pallas kernels for 0% -> 0%
where the time goes in v1:
time: 883 us; the launch traced here: 877 us
  waiting for transfers between devices  468 us (53%)
  matrix products  155 us (18%)
  blocking collectives  123 us (14%)
  local copies, waits for them, and re-layouts  80.7 us (9%)
  other arithmetic  35.5 us (4%)
  between operations  14.3 us (2%)
    unnamed x17, waiting for transfers between devices  184 us
    unnamed x2, blocking collectives  82.6 us
    reduce_scatter x1, waiting for transfers between devices, shards(): lax.psum_scatter(grad_gate.astype(jnp.bfloat16), 'dp', scatter_dimension=...  47.5 us
    unnamed x76, local copies, waits for them, and re-layouts  44.9 us
    all_gather x1, waiting for transfers between devices, shards(): lax.all_gather(w_query, ('dp', 'tensor'), axis=0, tiled=True)  38.4 us
    all_gather x1, waiting for transfers between devices, shards(): lax.all_gather(value_matrix, ('dp', 'tensor'), axis=0, tiled=True)  35.9 us
    reduce_scatter x1, waiting for transfers between devices, shards(): lax.psum_scatter(jnp.dot(act_low, w_down, preferred_element_type=jnp.floa...  35.1 us
    all_gather x1, waiting for transfers between devices, shards(): rows_all = lax.all_gather(normed_two, 'tensor', axis=0, tiled=True)  34.7 us
  transfers between devices with their start and end apart: 14, of which 12 were waited for; matrix products, arithmetic and copies ran while one was open for 19% of the time, Pallas kernels for 0%

profile of v1, /device:TPU:4, one launch (start us, length us, event | category | flops | bytes accessed | tf_op | source)
XLA Modules:
  0.0 877.2 jit_solution(17342453882744493003)
XLA Ops:
  12.5 41.5 %all-reduce.5 = (bf16[1536]{0:T(1024)(128)(2,1)S(1)}, bf16[1536]{0:T(1024)(128)(2,1)S(1)}) all-reduce(bf16[1536]{0:T(1024)(128)(2,1)S(1)} %dynamic-update-slice, bf16[1536]{0:T(1024)(128)(2,1)S(1)} %dynamic-update-slice.1), channel_id=1, replica_groups=mesh['dp'=8,'tensor'=4] {'dp','tensor'}, use_global_device_ids=true, to_apply=%add | all-reduce | flops 3072 | bytes 12288
  58.0 11.1 %all-gather.9.cloned.1.call-done = bf16[1536,768]{1,0:T(8,128)(2,1)} async-done(((bf16[48,768]{1,0:T(8,128)(2,1)}), bf16[1536,768]{1,0:T(8,128)(2,1)}) %all-gather.9.cloned.1.call-update) | async-done | bytes 2359312 | tf_op jit(solution)/shard_map/all_gather | solution.py:64
  72.2 19.5 %all_gather.33 = bf16[512,768]{0,1:T(8,128)(2,1)} all-gather(bf16[128,768]{0,1:T(8,128)(2,1)S(1)} %bitcast.216), channel_id=1, replica_groups=mesh['dp'=8,'tensor'=4] {'tensor'}, dimensions={0}, use_global_device_ids=true | all-gather | bytes 983040 | tf_op jit(solution)/shard_map/all_gather | solution.py:91
  93.8 35.9 %all-gather.11.cloned.1.call-done = bf16[1536,768]{1,0:T(8,128)(2,1)} async-done(((bf16[48,768]{1,0:T(8,128)(2,1)}), bf16[1536,768]{1,0:T(8,128)(2,1)}) %all-gather.11.cloned.1.call-update) | async-done | bytes 2359312 | tf_op jit(solution)/shard_map/all_gather | solution.py:65
  132.0 21.3 %all_gather.35 = bf16[512,768]{1,0:T(8,128)(2,1)} all-gather(bf16[128,768]{1,0:T(8,128)(2,1)S(1)} %convolution_convert_fusion.9), channel_id=1, replica_groups=mesh['dp'=8,'tensor'=4] {'tensor'}, dimensions={0}, use_global_device_ids=true | all-gather | bytes 983040 | tf_op jit(solution)/shard_map/all_gather | solution.py:92
  157.8 38.4 %all-gather.7.cloned.1.call-done = bf16[1536,1536]{1,0:T(8,128)(2,1)} async-done(((bf16[48,1536]{1,0:T(8,128)(2,1)}), bf16[1536,1536]{1,0:T(8,128)(2,1)}) %all-gather.7.cloned.1.call-update) | async-done | bytes 4718608 | tf_op jit(solution)/shard_map/all_gather | solution.py:63
  203.5 48.9 %while.30 = (s32[]{:T(128)}, bf16[8,256,96]{1,2,0:T(8,128)(2,1)}, f32[8,256]{1,0:T(8,128)}, bf16[8,256,96]{2,1,0:T(8,128)(2,1)}, bf16[8,512,96]{2,1,0:T(8,128)(2...) while((s32[]{:T(128)}, bf16[8,256,96]{1,2,0:T(8,128)(2,1)}, ...), condition=%wide.region_4.5_spmd.clone.clone, body=%wide.region_1.4_spmd.clone.sunk.clone | while | flops 51379968 | bytes 2338905 | solution.py:139
  267.0 34.7 %all-gather.15.cloned.1.call-done = bf16[512,1536]{1,0:T(8,128)(2,1)} async-done(((bf16[128,1536]{1,0:T(8,128)(2,1)}), bf16[512,1536]{1,0:T(8,128)(2,1)}) %all-gather.15.cloned.1.call-update) | async-done | bytes 1572880 | tf_op jit(solution)/shard_map/all_gather | solution.py:144
  301.6 5.7 fusion.80
  310.4 28.6 %all-gather.17.cloned.1.call-done = bf16[512,1536]{1,0:T(8,128)(2,1)} async-done(((bf16[128,1536]{1,0:T(8,128)(2,1)}), bf16[512,1536]{1,0:T(8,128)(2,1)}) %all-gather.17.cloned.1.call-update) | async-done | bytes 1572880 | tf_op jit(solution)/shard_map/all_gather | solution.py:158
  339.0 6.3 multiply_convert_fusion.1
  355.4 30.1 %reduce-scatter.17.cloned.1.call-done = bf16[128,1536]{1,0:T(8,128)(2,1)} async-done(((bf16[512,1536]{1,0:T(8,128)(2,1)}), bf16[128,1536]{1,0:T(8,128)(2,1)}) %reduce-scatter.17.cloned.1.call-update) | async-done | bytes 393232 | tf_op jit(solution)/shard_map/reduce_scatter | solution.py:165
  387.0 35.1 %reduce-scatter.15.cloned.1.call-done = bf16[128,1536]{1,0:T(8,128)(2,1)} async-done(((bf16[512,1536]{1,0:T(8,128)(2,1)}), bf16[128,1536]{1,0:T(8,128)(2,1)}) %reduce-scatter.15.cloned.1.call-update) | async-done | bytes 393232 | tf_op jit(solution)/shard_map/reduce_scatter | solution.py:150
  429.0 61.5 %while.31 = (s32[]{:T(128)}, f32[8,256,96]{1,2,0:T(8,128)}, bf16[8,512,96]{1,2,0:T(8,128)(2,1)}, bf16[8,512,96]{1,2,0:T(8,128)(2,1)}, bf16[8,256,96]{2,1,0:T(8,1...) while((s32[]{:T(128)}, f32[8,256,96]{1,2,0:T(8,128)}, ...), condition=%wide.region_11.12_spmd.clone.clone, body=%wide.region_9.11_spmd.clone.sunk.clone | while | flops 127082240 | bytes 5417073 | solution.py:215
  495.6 4.9 convolution_convert_fusion.2
  501.7 4.9 convolution_convert_fusion.3
  507.8 4.9 convolution_convert_fusion.4
  524.8 15.7 %reduce-scatter.27.cloned.1.call-done = bf16[128,768]{1,0:T(8,128)(2,1)} async-done(((bf16[512,768]{1,0:T(8,128)(2,1)}), bf16[128,768]{1,0:T(8,128)(2,1)}) %reduce-scatter.27.cloned.1.call-update) | async-done | bytes 196624
  542.5 9.8 %pad_maximum_fusion = bf16[1536,4608]{0,1:T(8,128)(2,1)} fusion(bf16[1536,1536]{0,1:T(8,128)(2,1)} %convolution_convert_fusion.1, bf16[1536,768]{0,1:T(8,128)(2,1)S(1)} %convolution_convert_fusion.5, bf16[1536,768]{0,1:T(8,128)(2,1)S(1)} %copy-done.5, bf16[1536,1536]{0,1:T(8,128)(2,1)} %convolution_convert_fusion), kind=kLoop, calls=%fused_computation.56 | loop fusion | flops 56623104 | bytes 28311552 | tf_op jit(solution)/shard_map/concatenate | solution.py:258
  552.3 17.6 %copy.88 = bf16[1536,4608]{1,0:T(8,128)(2,1)} copy(bf16[1536,4608]{0,1:T(8,128)(2,1)} %pad_maximum_fusion) | data formatting | bytes 28311552
  577.9 41.2 %all-reduce.4 = (f32[1536]{0:T(1024)S(1)}, f32[1536]{0:T(1024)S(1)}) all-reduce(f32[1536]{0:T(1024)S(1)} %get-tuple-element.245, f32[1536]{0:T(1024)S(1)} %get-tuple-element.243), channel_id=6, replica_groups=mesh['dp'=8,'tensor'=4] {'dp','tensor'}, use_global_device_ids=true, to_apply=%region_16.17.clone | all-reduce | flops 3072 | bytes 24576
  622.2 17.1 %reduce-scatter.21.cloned.1.call-done = bf16[192,1024]{1,0:T(8,128)(2,1)} async-done(((bf16[1536,1024]{1,0:T(8,128)(2,1)}), bf16[192,1024]{1,0:T(8,128)(2,1)}) %reduce-scatter.21.cloned.1.call-update) | async-done | bytes 393232 | tf_op jit(solution)/shard_map/reduce_scatter | solution.py:274
  641.3 47.5 %reduce-scatter.19.cloned.1.call-done = bf16[192,1024]{1,0:T(8,128)(2,1)} async-done(((bf16[1536,1024]{1,0:T(8,128)(2,1)}), bf16[192,1024]{1,0:T(8,128)(2,1)}) %reduce-scatter.19.cloned.1.call-update) | async-done | bytes 393232 | tf_op jit(solution)/shard_map/reduce_scatter | solution.py:271
  691.9 165.4 %reduce-scatter.29.cloned.1.call-done = bf16[48,4608]{1,0:T(8,128)(2,1)} async-done(((bf16[1536,4608]{1,0:T(8,128)(2,1)}), bf16[48,4608]{1,0:T(8,128)(2,1)}) %reduce-scatter.29.cloned.1.call-update) | async-done | bytes 442384
  (275 shorter events, 225.6 us)
Async XLA Ops:
  7.2 331.8 %copy-start = (bf16[1024,1536]{1,0:T(8,128)(2,1)S(1)}, bf16[1024,1536]{1,0:T(8,128)(2,1)}, u32[]{:S(2)}) copy-start(bf16[1024,1536]{1,0:T(8,128)(2,1)} %param.26) | copy-start | bytes 9437188
  7.2 61.9 %all-gather.9.cloned.1.call-start = ((), (), s32[]{:S(2)}) async-start(), calls=%async_computation.9 | async-start | bytes 2433024 | tf_op jit(solution)/shard_map/all_gather | solution.py:64
  7.9 121.9 %all-gather.11.cloned.1.call-start = ((), (), s32[]{:S(2)}) async-start(), calls=%async_computation.10 | async-start | bytes 2433024 | tf_op jit(solution)/shard_map/all_gather | solution.py:65
  8.7 187.6 %all-gather.7.cloned.1.call-start = ((), (), s32[]{:S(2)}) async-start(), calls=%async_computation.8 | async-start | bytes 4866048 | tf_op jit(solution)/shard_map/all_gather | solution.py:63
  9.4 251.4 %all-gather.13.cloned.1.call-start = ((), (), s32[]{:S(2)}) async-start(), calls=%async_computation.11 | async-start | bytes 4866048 | tf_op jit(solution)/shard_map/all_gather | solution.py:66
  10.0 291.7 %all-gather.15.cloned.1.call-start = ((), (), s32[]{:S(2)}) async-start(), calls=%async_computation.12 | async-start | bytes 1966080 | tf_op jit(solution)/shard_map/all_gather | solution.py:144
  69.1 60.7 %copy-start.2 = (bf16[128,1536]{1,0:T(8,128)(2,1)S(1)}, bf16[128,1536]{1,0:T(8,128)(2,1)}, u32[]{:S(2)}) copy-start(bf16[128,1536]{1,0:T(8,128)(2,1)} %param.16) | copy-start | bytes 1179652
  266.2 72.8 %all-gather.17.cloned.1.call-start = ((), (), s32[]{:S(2)}) async-start(), calls=%async_computation.14 | async-start | bytes 1966080 | tf_op jit(solution)/shard_map/all_gather | solution.py:158
  266.7 118.7 %reduce-scatter.17.cloned.1.call-start = ((), (), s32[]{:S(2)}) async-start(), calls=%async_computation.15 | async-start | bytes 1966080 | tf_op jit(solution)/shard_map/reduce_scatter | solution.py:165
  301.6 5.7 copy-start.20
  301.6 5.7 copy-start.23
  339.0 6.3 copy-start.21
  351.0 71.1 %reduce-scatter.15.cloned.1.call-start = ((), (), s32[]{:S(2)}) async-start(), calls=%async_computation.13 | async-start | bytes 1966080 | tf_op jit(solution)/shard_map/reduce_scatter | solution.py:150
  355.3 66.8 %copy-start.4 = (f32[128,1536]{1,0:T(8,128)S(1)}, f32[128,1536]{1,0:T(8,128)}, u32[]{:S(2)}) copy-start(f32[128,1536]{1,0:T(8,128)} %copy-done.3) | copy-start | bytes 2359300
  355.3 166.0 %reduce-scatter.25.cloned.1.call-start = ((), (), s32[]{:S(2)}) async-start(), calls=%async_computation.19 | async-start | bytes 983040
  424.5 4.5 copy-start.7
  490.5 5.0 copy-start.26
  492.9 47.6 %reduce-scatter.27.cloned.1.call-start = ((), (), s32[]{:S(2)}) async-start(), calls=%async_computation.20 | async-start | bytes 983040
  495.3 125.0 %reduce-scatter.23.cloned.1.call-start = ((), (), s32[]{:S(2)}) async-start(), calls=%async_computation.18 | async-start | bytes 3538944 | tf_op jit(solution)/shard_map/reduce_scatter | solution.py:277
  500.5 138.8 %reduce-scatter.21.cloned.1.call-start = ((), (), s32[]{:S(2)}) async-start(), calls=%async_computation.17 | async-start | bytes 3538944 | tf_op jit(solution)/shard_map/reduce_scatter | solution.py:274
  506.6 182.2 %reduce-scatter.19.cloned.1.call-start = ((), (), s32[]{:S(2)}) async-start(), calls=%async_computation.16 | async-start | bytes 3538944 | tf_op jit(solution)/shard_map/reduce_scatter | solution.py:271
  512.7 344.6 %reduce-scatter.29.cloned.1.call-start = ((), (), s32[]{:S(2)}) async-start(), calls=%async_computation.21 | async-start | bytes 14598144
  576.9 113.9 %copy-start.19 = (f32[128]{0:T(128)S(1)}, f32[128]{0:T(128)}, u32[]{:S(2)}) copy-start(f32[128]{0:T(128)} %get-tuple-element.309) | copy-start | bytes 1540
  859.6 11.1 %copy-start.1 = (bf16[1024,1536]{1,0:T(8,128)(2,1)S(1)}, bf16[1024,1536]{1,0:T(8,128)(2,1)}, u32[]{:S(2)}) copy-start(bf16[1024,1536]{1,0:T(8,128)(2,1)} %param.26) | copy-start | bytes 9437188
  (19 other events, 41.0 us)
Sparse Core Ops, SparseCore 0:
  10.8 58.2 all-gather.8
  71.9 57.8 all-gather.10
  132.6 63.6 all-gather.6
  198.9 61.8 all-gather.12
  266.3 35.3 all-gather.14
  303.1 35.8 all-gather.16
  351.1 34.2 reduce-scatter.16
  387.8 34.2 reduce-scatter.14
  493.0 21.9 reduce-scatter.24
  517.8 22.6 reduce-scatter.26
  543.9 45.9 reduce-scatter.22
  593.1 46.1 reduce-scatter.20
  642.7 46.0 reduce-scatter.18
  694.7 162.5 reduce-scatter.28

commit v2 on v1

--- a/solution.py
+++ b/solution.py
@@ -1,18 +1,472 @@
+import functools
 import math
 
 import jax
 import jax.numpy as jnp
+import numpy as np
 from jax import lax
+from jax.experimental import pallas as pl
+from jax.experimental.pallas import tpu as pltpu
 from jax.sharding import PartitionSpec as P
+
+F32 = jnp.float32
+BF16 = jnp.bfloat16
+MESH = pl.DeviceIdType.MESH
+EPSILON = 1e-05
+ROPE_BASE = 100000.0
+MASKED = -1e30
+HEAD = 96
+VMEM_LIMIT = 64 * 2**20 - 65536
+
+
+def rotary_tables(rows, shards_in_sequence):
+    half = HEAD // 2
+    lanes = np.arange(4 * HEAD) % half
+    rates = ROPE_BASE ** (-(lanes * 2.0) / HEAD)
+    near = np.arange(rows)[:, None] * rates[None, :]
+    far = (np.arange(shards_in_sequence) * rows)[:, None] * rates[None, :]
+    shift = np.concatenate([np.cos(far), np.sin(far)], axis=0)
+    return (
+        np.cos(near).astype(np.float32),
+        np.sin(near).astype(np.float32),
+        shift.astype(np.float32),
+    )
+
+
+def tensor_peer(t, m):
+    if m == 1:
+        return t + 1 - 2 * lax.rem(t, 2)
+    if m == 2:
+        return lax.rem(t + 2, 4)
+    return 3 - t
+
+
+def dp_peer(d, m):
+    if m & 1:
+        d = d + 1 - 2 * lax.rem(d, 2)
+    if m & 2:
+        d = d + 2 - 4 * lax.rem(lax.div(d, 2), 2)
+    if m & 4:
+        d = lax.rem(d + 4, 8)
+    return d
+
+
+class Links:
+    def __init__(self, tsend, trecv, dsend, drecv):
+        self.t = lax.axis_index("tensor")
+        self.d = lax.axis_index("dp")
+        self.mid = lax.rem(lax.div(self.t + 1, 2), 2)
+        self.tsend, self.trecv, self.dsend, self.drecv = tsend, trecv, dsend, drecv
+
+    def shard_at(self, i):
+        t, mid = self.t, self.mid
+        near, two, three = (tensor_peer(t, m) for m in (1, 2, 3))
+        if isinstance(i, int):
+            if i == 0:
+                return t, 0
+            if i == 1:
+                return near, 1
+            if i == 2:
+                return two + mid * (three - two), 2 + mid
+            return three + mid * (two - three), 3 - mid
+        one_if = [1 - jnp.minimum(jnp.abs(i - k), 1) for k in range(4)]
+        pairs = [self.shard_at(k) for k in range(4)]
+        return (
+            sum(f * p[0] for f, p in zip(one_if, pairs)),
+            sum(f * p[1] for f, p in zip(one_if, pairs)),
+        )
+
+    def over_tensor(self, kind, m, src, dst, recv=None):
+        peer = tensor_peer(self.t, m)
+        return pltpu.make_async_remote_copy(
+            src_ref=src,
+            dst_ref=dst,
+            send_sem=self.tsend.at[kind, m],
+            recv_sem=self.trecv.at[kind, m if recv is None else recv],
+            device_id={"dp": self.d, "tensor": peer},
+            device_id_type=MESH,
+        )
+
+    def over_dp(self, kind, m, src, dst, to=None):
+        peer = dp_peer(self.d, m if to is None else to)
+        return pltpu.make_async_remote_copy(
+            src_ref=src,
+            dst_ref=dst,
+            send_sem=self.dsend.at[kind, m],
+            recv_sem=self.drecv.at[kind, m],
+            device_id={"dp": peer, "tensor": self.t},
+            device_id_type=MESH,
+        )
+
+    def landed_tensor(self, kind, m, ref):
+        pltpu.make_async_copy(ref, ref, self.trecv.at[kind, m]).wait()
+
+    def landed_dp(self, kind, m, ref):
+        pltpu.make_async_copy(ref, ref, self.drecv.at[kind, m]).wait()
+
+    def gather_start(self, kind, src, at):
+        own = at(self.t)
+        self.over_tensor(kind, 1, src, own).start()
+
+        @pl.when(self.mid == 0)
+        def _():
+            self.over_tensor(kind, 2, src, own).start()
+
+        @pl.when(self.mid == 1)
+        def _():
+            self.over_tensor(kind, 3, src, own).start()
+
+    def gather_take(self, kind, i, at):
+        shard, m = self.shard_at(i)
+        block = at(shard)
+        self.landed_tensor(kind, m, block)
+
+        def hand_on():
+            pltpu.make_async_remote_copy(
+                src_ref=block,
+                dst_ref=block,
+                send_sem=self.tsend.at[kind, 2 + i],
+                recv_sem=self.trecv.at[kind, 5 - m],
+                device_id={"dp": self.d, "tensor": tensor_peer(self.t, 1)},
+                device_id_type=MESH,
+            ).start()
+
+        if isinstance(i, int):
+            if i >= 2:
+                pl.when(self.mid == 1)(hand_on)
+        else:
+            pl.when((self.mid == 1) & (i >= 2))(hand_on)
+
+    def gather_end(self, kind, src, at):
+        own = at(self.t)
+        self.over_tensor(kind, 1, src, own).wait_send()
+
+        @pl.when(self.mid == 0)
+        def _():
+            self.over_tensor(kind, 2, src, own).wait_send()
+
+        @pl.when(self.mid == 1)
+        def _():
+            self.over_tensor(kind, 3, src, own).wait_send()
+            for i in (2, 3):
+                shard, m = self.shard_at(i)
+                pltpu.make_async_copy(at(shard), at(shard), self.tsend.at[kind, 2 + i]).wait()
+
+    def barrier(self, tensor_peers, dp_peers):
+        sem = pltpu.get_barrier_semaphore()
+        for m in tensor_peers:
+            pl.semaphore_signal(
+                sem,
+                inc=1,
+                device_id={"dp": self.d, "tensor": tensor_peer(self.t, m)},
+                device_id_type=MESH,
+            )
+        for m in dp_peers:
+            pl.semaphore_signal(
+                sem,
+                inc=1,
+                device_id={"dp": dp_peer(self.d, m), "tensor": self.t},
+                device_id_type=MESH,
+            )
+        pl.semaphore_wait(sem, len(tensor_peers) + len(dp_peers))
+
+
+def mm(a, b, dims=((1,), (0,))):
+    return lax.dot_general(a, b, (dims, ((), ())), preferred_element_type=F32)
+
+
+NN = ((1,), (0,))
+NT = ((1,), (1,))
+TN = ((0,), (0,))
+
+
+def lane_roll(u, by):
+    return pltpu.roll(u, by % u.shape[-1], u.ndim - 1)
+
+
+def swap_halves(u):
+    lane = lax.broadcasted_iota(jnp.int32, u.shape, 1)
+    low = lax.rem(lane, HEAD) < HEAD // 2
+    return jnp.where(low, -lane_roll(u, -(HEAD // 2)), lane_roll(u, HEAD // 2))
+
+
+def turn_tables(near_cos, near_sin, shift, shard):
+    c = shift[pl.ds(shard, 1), :]
+    s = shift[pl.ds(shard + 4, 1), :]
+    a, b = near_cos[...], near_sin[...]
+    return a * c - b * s, b * c + a * s
+
+
+def front_kernel(
+    hid, cot, tile, wpack, wo, near_cos, near_sin, shift,
+    normed_out, w_out, wo_out, heads_out, lse_out, start_out, cot_out, rows_out, resid_out,
+    normed2_out, gains_out,
+    xall, nall, call, w, wof, tiles, qh, kh, vh, att, arow, outh, lse, start, gains, resid, normed2,
+    tsend, trecv, dsend, drecv, local, store,
+):
+    ln = Links(tsend, trecv, dsend, drecv)
+    t, d = ln.t, ln.d
+    rows = hid.shape[0]
+    width = hid.shape[1]
+    wrows = wo.shape[0]
+    srows = 4 * wrows
+    TILE, W, X, O, C, A = range(6)
+    DT, DW, FW, DO, FO = range(5)
+
+    def rows_at(ref, shard):
+        return ref.at[pl.ds(pl.multiple_of(shard * rows, rows), rows), :]
+
+    def w_at(ref, dd, tt=None):
+        if tt is None:
+            return ref.at[pl.ds(pl.multiple_of(dd * srows, 16), srows), :]
+        return ref.at[pl.ds(pl.multiple_of(dd * srows + tt * wrows, 16), wrows), :]
+
+    x_of = functools.partial(rows_at, xall)
+    c_of = functools.partial(rows_at, call)
+
+    def wo_of(tt):
+        return w_at(wof, d, tt)
+
+    mine = [
+        pltpu.make_async_copy(tile, tiles.at[d, t], local.at[0]),
+        pltpu.make_async_copy(wpack.at[t], w_at(w, d, t), local.at[1]),
+        pltpu.make_async_copy(wo, wo_of(t), local.at[2]),
+        pltpu.make_async_copy(hid, x_of(t), local.at[3]),
+        pltpu.make_async_copy(cot, c_of(t), local.at[4]),
+    ]
+    for c in mine:
+        c.start()
+    ln.barrier((1, 2, 3), (1, 2, 3, 4, 5, 6, 7))
+    for m in (1, 2, 3):
+        ln.over_tensor(TILE, m, tile, tiles.at[d, t]).start()
+    for m in (1, 2, 3):
+        ln.over_tensor(W, m, wpack.at[tensor_peer(t, m)], w_at(w, d, t)).start()
+    ln.gather_start(O, wo, wo_of)
+    ln.gather_start(X, hid, x_of)
+
+    mine[0].wait()
+    for m in (1, 2, 3):
+        ln.landed_tensor(TILE, m, tiles.at[d, tensor_peer(t, m)])
+    for m in range(1, 8):
+        ln.over_dp(DT, m, tiles.at[d], tiles.at[d]).start()
+    mine[1].wait()
+    for m in (1, 2, 3):
+        ln.landed_tensor(W, m, w_at(w, d, tensor_peer(t, m)))
+    for m in (2, 4, 6, 1):
+        ln.over_dp(DW, m, w_at(w, d), w_at(w, d)).start()
+    mine[2].wait()
+    for i in (1, 2, 3):
+        ln.gather_take(O, i, wo_of)
+    for m in (2, 4, 6, 1):
+        ln.over_dp(DO, m, w_at(wof, d), w_at(wof, d)).start()
+    for m in range(1, 8):
+        ln.landed_dp(DT, m, tiles.at[dp_peer(d, m)])
+    for m in (2, 4, 6):
+        dd = dp_peer(d, m)
+        ln.landed_dp(DW, m, w_at(w, dd))
+        ln.over_dp(FW, m, w_at(w, dd), w_at(w, dd), to=1).start()
+
+    for g in range(4):
+        acc = jnp.zeros((8, 8 * wrows), F32)
+        for j in range(8):
+            r = 8 * g + j
+            piece = jnp.concatenate(
+                [tiles[r // 4, r % 4], jnp.zeros((8, 8 * wrows - 128), F32)], axis=1
+            )
+            acc = acc + lane_roll(piece, wrows * j)
+        gains[:, g * 8 * wrows : (g + 1) * 8 * wrows] = acc
+    for s in range(4):
+        start[:, s * rows : (s + 1) * rows] = tiles[d, s, 2:3, :]
+
+    mine[3].wait()
+    for i in (1, 2, 3):
+        ln.gather_take(X, i, x_of)
+    mine[4].wait()
+    ln.gather_start(C, cot, c_of)
+    for m in (1,):
+        ln.landed_dp(DW, m, w_at(w, dp_peer(d, m)))
+    for m in (2, 4, 6):
+        ln.landed_dp(FW, m, w_at(w, dp_peer(d, m ^ 1)))
+
+    def project(s, carry):
+        at = pl.ds(pl.multiple_of(s * rows, rows), rows)
+        x = xall[at, :].astype(F32)
+        inv = lax.rsqrt(jnp.mean(x * x, axis=1, keepdims=True) + EPSILON)
+        normed = (x * inv * gains[0:1, :]).astype(BF16)
+        nall[at, :] = normed
+        cosine, sine = turn_tables(near_cos, near_sin, shift, s)
+        q = mm(normed, w[:, : 4 * HEAD])
+        q = q * cosine + swap_halves(q) * sine
+        kv = mm(normed, w[:, 4 * HEAD :])
+        lane = lax.broadcasted_iota(jnp.int32, kv.shape, 1)
+        kv = jnp.where(lane < 2 * HEAD, kv * cosine + swap_halves(kv) * sine, kv)
+        keep = lax.broadcasted_iota(jnp.int32, (rows, 128), 1) < HEAD
+        for h in range(4):
+            qh[h, at, :] = jnp.where(keep, lane_roll(q, -HEAD * h)[:, :128], 0.0).astype(BF16)
+        for c in range(2):
+            kh[c, at, :] = jnp.where(keep, lane_roll(kv, -HEAD * c)[:, :128], 0.0).astype(BF16)
+            vh[c, at, :] = jnp.where(keep, lane_roll(kv, -HEAD * (c + 2))[:, :128], 0.0).astype(BF16)
+        return carry
+
+    lax.fori_loop(0, 4, project, 0)
+
+    def forward_wo(m):
+        dd = dp_peer(d, m)
+        ln.landed_dp(DO, m, w_at(wof, dd))
+        ln.over_dp(FO, m, w_at(wof, dd), w_at(wof, dd), to=1).start()
+
+    scale = 1.0 / math.sqrt(HEAD)
+
+    def attend(h, carry):
+        c = lax.div(h, 2)
+        for b in range(4):
+            span = (b + 1) * rows
+            sc = mm(kh[c, :span, :], qh[h, b * rows : span, :], NT) * scale
+            key = lax.broadcasted_iota(jnp.int32, sc.shape, 0)
+            query = lax.broadcasted_iota(jnp.int32, sc.shape, 1) + b * rows
+            first = start[:, b * rows : span].astype(jnp.int32)
+            sc = jnp.where((key <= query) & (key >= first), sc, MASKED)
+            peak = jnp.max(sc, axis=0, keepdims=True)
+            e = jnp.exp(sc - peak)
+            total = jnp.sum(e, axis=0, keepdims=True)
+            p = (e * (1.0 / total)).astype(BF16)
+            outh[h, b * rows : span, :] = mm(p, vh[c, :span, :], TN)
+            lse[h, :, b * rows : span] = peak + jnp.log(total)
+        return carry
+
+    lax.fori_loop(0, 4, attend, 0)
+
+    def pack(b, carry):
+        at = pl.ds(pl.multiple_of(b * rows, rows), rows)
+        acc = jnp.zeros((rows, 4 * HEAD), F32)
+        for h in range(4):
+            piece = jnp.concatenate([outh[h, at, :], jnp.zeros((rows, 4 * HEAD - 128), F32)], axis=1)
+            acc = acc + lane_roll(piece, HEAD * h)
+        att[b] = acc.astype(BF16)
+        return carry
+
+    lax.fori_loop(0, 4, pack, 0)
+
+    def columns(tt):
+        return arow.at[:, pl.ds(pl.multiple_of(tt * 4 * HEAD, 128), 4 * HEAD)]
+
+    for m in (1, 2, 3):
+        ln.over_tensor(A, m, att.at[tensor_peer(t, m)], columns(t)).start()
+    own = pltpu.make_async_copy(att.at[t], columns(t), local.at[0])
+    own.start()
+    for m in (2, 4, 6):
+        forward_wo(m)
+    ln.landed_dp(DO, 1, w_at(wof, dp_peer(d, 1)))
+    for m in (2, 4, 6):
+        ln.landed_dp(FO, m, w_at(wof, dp_peer(d, m ^ 1)))
+    own.wait()
+    for m in (1, 2, 3):
+        ln.landed_tensor(A, m, columns(tensor_peer(t, m)))
+
+    at = pl.ds(pl.multiple_of(t * rows, rows), rows)
+    third = width // 3
+
+    def project_out(n, carry):
+        cols = pl.ds(pl.multiple_of(n * third, 128), third)
+        resid[:, cols] = xall[at, cols].astype(F32) + mm(arow[...], wof[:, cols])
+        return carry
+
+    lax.fori_loop(0, 3, project_out, 0)
+    r = resid[...]
+    inv = lax.rsqrt(jnp.mean(r * r, axis=1, keepdims=True) + EPSILON)
+    normed2[...] = (r * inv * gains[1:2, :]).astype(BF16)
+
+    for i in (1, 2, 3):
+        ln.gather_take(C, i, c_of)
+
+    results = [
+        (nall, normed_out), (w, w_out), (wof, wo_out), (qh, heads_out.at[0:4]),
+        (kh, heads_out.at[4:6]), (vh, heads_out.at[6:8]), (lse, lse_out), (start, start_out),
+        (call, cot_out), (arow, rows_out), (resid, resid_out), (normed2, normed2_out),
+        (gains, gains_out),
+    ]
+    stores = [pltpu.make_async_copy(a, b, store.at[i]) for i, (a, b) in enumerate(results)]
+    for c in stores:
+        c.start()
+    for m in (1, 2, 3):
+        ln.over_tensor(TILE, m, tile, tiles.at[d, t]).wait_send()
+        ln.over_tensor(W, m, wpack.at[tensor_peer(t, m)], w_at(w, d, t)).wait_send()
+        ln.over_tensor(A, m, att.at[tensor_peer(t, m)], columns(t)).wait_send()
+    ln.gather_end(O, wo, wo_of)
+    ln.gather_end(X, hid, x_of)
+    ln.gather_end(C, cot, c_of)
+    for m in range(1, 8):
+        ln.over_dp(DT, m, tiles.at[d], tiles.at[d]).wait_send()
+    for m in (2, 4, 6, 1):
+        ln.over_dp(DW, m, w_at(w, d), w_at(w, d)).wait_send()
+        ln.over_dp(DO, m, w_at(wof, d), w_at(wof, d)).wait_send()
+    for m in (2, 4, 6):
+        dd = dp_peer(d, m)
+        ln.over_dp(FW, m, w_at(w, dd), w_at(w, dd), to=1).wait_send()
+        ln.over_dp(FO, m, w_at(wof, dd), w_at(wof, dd), to=1).wait_send()
+    for c in stores:
+        c.wait()
+
+
+def front(hid, cot, positions, gain_attn, gain_mlp, wq, wk, wv, wo):
+    rows, width = hid.shape
+    wrows = wq.shape[0]
+    seq = 4 * rows
+    t = lax.axis_index("tensor")
+    index = t * rows + jnp.arange(rows, dtype=jnp.int32)
+    pad = (0, 128 - wrows)
+    tile = jnp.stack(
+        [
+            jnp.pad(gain_attn.astype(F32), pad),
+            jnp.pad(gain_mlp.astype(F32), pad),
+            (index - positions).astype(F32),
+        ]
+        + [jnp.zeros((128,), F32)] * 5
+    )
+    wpack = jnp.concatenate(
+        [a.reshape(wrows, 4, a.shape[1] // 4).transpose(1, 0, 2) for a in (wq, wk, wv)], axis=2
+    )
+    near_cos, near_sin, shift = rotary_tables(rows, 4)
+    hbm = pl.BlockSpec(memory_space=pl.ANY)
+    vmem = pl.BlockSpec(memory_space=pltpu.VMEM)
+    sds = jax.ShapeDtypeStruct
+    shapes = dict(
+        normed=((seq, width), BF16), w=((width, 8 * HEAD), BF16), wo=((width, width), BF16),
+        heads=((8, seq, 128), BF16), lse=((4, 1, seq), F32), start=((1, seq), F32),
+        cot=((seq, width), BF16), rows=((rows, width), BF16), resid=((rows, width), F32),
+        normed2=((rows, width), BF16), gains=((8, width), F32),
+    )
+    S = {k: pltpu.VMEM(*v) for k, v in shapes.items()}
+    outs = pl.pallas_call(
+        front_kernel,
+        out_shape=[sds(*v) for v in shapes.values()],
+        in_specs=[hbm] * 5 + [vmem] * 3,
+        out_specs=[hbm] * len(shapes),
+        scratch_shapes=[
+            pltpu.VMEM((seq, width), BF16),
+            S["normed"], S["cot"], S["w"], S["wo"],
+            pltpu.VMEM((8, 4, 8, 128), F32),
+            pltpu.VMEM((4, seq, 128), BF16), pltpu.VMEM((2, seq, 128), BF16),
+            pltpu.VMEM((2, seq, 128), BF16),
+            pltpu.VMEM((4, rows, 4 * HEAD), BF16),
+            S["rows"],
+            pltpu.VMEM((4, seq, 128), F32),
+            S["lse"], S["start"], S["gains"], S["resid"], S["normed2"],
+            pltpu.SemaphoreType.DMA((6, 6)), pltpu.SemaphoreType.DMA((6, 4)),
+            pltpu.SemaphoreType.DMA((5, 8)), pltpu.SemaphoreType.DMA((5, 8)),
+            pltpu.SemaphoreType.DMA((5,)), pltpu.SemaphoreType.DMA((13,)),
+        ],
+        name="front",
+        compiler_params=pltpu.CompilerParams(
+            collective_id=0, has_side_effects=True, vmem_limit_bytes=VMEM_LIMIT
+        ),
+    )(hid, cot, tile, wpack, wo, near_cos, near_sin, shift)
+    return dict(zip(shapes, outs))
+
 
 QUERY_HEADS = 16
 KEY_VALUE_HEADS = 8
 HEAD_DIMENSION = 96
-
-
-EPSILON = 1e-05
-ROPE_BASE = 100000.0
-MASKED = -1e30
 
 
 def angle_tables(pos_rows, head_size):
@@ -293,6 +747,124 @@
     )
 
 
+def rest_of_layer(hidden, gain_one_rows, o, w_gate, w_up, w_down):
+    rows, width = hidden.shape
+    seq = 4 * rows
+    gain_one, gain_two = o["gains"][0:1], o["gains"][1:2]
+    resid, normed_two = o["resid"], o["normed2"]
+    grad_all = o["cot"]
+    t = lax.axis_index("tensor")
+    grad_float = lax.dynamic_slice_in_dim(grad_all, t * rows, rows, 0).astype(F32)
+
+    def over_tokens(a):
+        return lax.psum_scatter(
+            a.astype(BF16), "tensor", scatter_dimension=0, tiled=True
+        ).astype(F32)
+
+    def dot(spec, a, b):
+        return jnp.einsum(spec, a, b, preferred_element_type=F32)
+
+    inv_two = lax.rsqrt(jnp.mean(resid * resid, axis=-1, keepdims=True) + EPSILON)
+    rows_all = lax.all_gather(normed_two, "tensor", axis=0, tiled=True)
+    gate = dot("sd,df->sf", rows_all, w_gate)
+    up = dot("sd,df->sf", rows_all, w_up)
+    sig = jax.nn.sigmoid(gate)
+    silu = gate * sig
+    act = (silu * up).astype(BF16)
+    g_act = dot("sd,fd->sf", grad_all, w_down)
+    g_gate = (g_act * up * sig * (1.0 + gate * (1.0 - sig))).astype(BF16)
+    g_up = (g_act * silu).astype(BF16)
+    g_norm_two = over_tokens(dot("sf,df->sd", g_gate, w_gate) + dot("sf,df->sd", g_up, w_up))
+    layer_out = (resid + over_tokens(dot("sf,fd->sd", act, w_down))).astype(BF16)
+    scaled = gain_two * g_norm_two
+    g_resid = (
+        grad_float
+        + inv_two * scaled
+        - resid * inv_two**3 * jnp.mean(scaled * resid, axis=-1, keepdims=True)
+    )
+    g_resid_low = g_resid.astype(BF16)
+    gain_two_grad = jnp.sum(g_norm_two * resid * inv_two, axis=0)
+    grad_out = dot("tc,td->cd", o["rows"], g_resid_low)
+    g_att = dot("td,cd->tc", g_resid_low, o["wo"]).astype(BF16)
+    g_att = lax.all_to_all(g_att, "tensor", split_axis=1, concat_axis=0, tiled=True)
+    g_heads = g_att.reshape(seq, 4, HEAD).transpose(1, 0, 2)
+    q = o["heads"][0:4, :, :HEAD]
+    k = jnp.repeat(o["heads"][4:6, :, :HEAD], 2, axis=0)
+    v = jnp.repeat(o["heads"][6:8, :, :HEAD], 2, axis=0)
+    scale = 1.0 / math.sqrt(HEAD)
+    index = jnp.arange(seq, dtype=jnp.int32)
+    first = o["start"][0].astype(jnp.int32)
+    visible = (index[None, :] <= index[:, None]) & (index[None, :] >= first[:, None])
+    scores = jnp.where(visible[None], dot("hqd,hkd->hqk", q, k) * scale, MASKED)
+    probs = jnp.exp(scores - o["lse"][:, 0, :, None])
+    g_probs = dot("hqd,hkd->hqk", g_heads, v)
+    g_scores = (probs * (g_probs - jnp.sum(probs * g_probs, axis=-1, keepdims=True))).astype(BF16)
+    g_rq = dot("hqk,hkd->hqd", g_scores, k) * scale
+    g_rk = dot("hqk,hqd->hkd", g_scores, q) * scale
+    g_v = dot("hqk,hqd->hkd", probs.astype(BF16), g_heads)
+    g_rk = g_rk.reshape(2, 2, seq, HEAD).sum(1)
+    g_v = g_v.reshape(2, 2, seq, HEAD).sum(1)
+    rates = ROPE_BASE ** (-(jnp.arange(HEAD // 2, dtype=F32) * 2.0) / HEAD)
+    turned = index.astype(F32)[:, None] * rates[None, :]
+    cosine, sine = jnp.cos(turned), jnp.sin(turned)
+
+    def turn_back(u):
+        a, b = u[..., : HEAD // 2], u[..., HEAD // 2 :]
+        return jnp.concatenate([a * cosine + b * sine, b * cosine - a * sine], axis=-1)
+
+    g = jnp.concatenate([turn_back(g_rq), turn_back(g_rk), g_v], axis=0).astype(BF16)
+    g = g.transpose(1, 0, 2).reshape(seq, 8 * HEAD)
+    grad_w = dot("sc,sd->cd", o["normed"], g)
+    g_norm_one = over_tokens(dot("sd,cd->sc", g, o["w"]))
+    x = hidden.astype(F32)
+    inv_one = lax.rsqrt(jnp.mean(x * x, axis=-1, keepdims=True) + EPSILON)
+    scaled = gain_one * g_norm_one
+    grad_input = (
+        g_resid + inv_one * scaled - x * inv_one**3 * jnp.mean(scaled * x, axis=-1, keepdims=True)
+    )
+    gain_one_grad = jnp.sum(g_norm_one * x * inv_one, axis=0)
+    gains = lax.psum_scatter(
+        jnp.stack([gain_one_grad, gain_two_grad], axis=1),
+        ("dp", "tensor"), scatter_dimension=0, tiled=True,
+    )
+    grad_w = lax.psum_scatter(grad_w.astype(BF16), "dp", scatter_dimension=0, tiled=True)
+    wrows = grad_w.shape[0] // 4
+    grad_w = lax.all_to_all(
+        grad_w.reshape(4, wrows, 8 * HEAD), "tensor", split_axis=0, concat_axis=0, tiled=True
+    )
+    grad_w = grad_w.astype(F32).transpose(1, 0, 2)
+    query = grad_w[:, :, : 4 * HEAD].reshape(wrows, 16 * HEAD)
+    key = grad_w[:, :, 4 * HEAD : 6 * HEAD].reshape(wrows, 8 * HEAD)
+    value = grad_w[:, :, 6 * HEAD :].reshape(wrows, 8 * HEAD)
+    out = lax.psum_scatter(
+        grad_out.astype(BF16), ("dp", "tensor"), scatter_dimension=0, tiled=True
+    ).astype(F32)
+
+    def owners(a, dim):
+        return lax.psum_scatter(
+            a.astype(BF16), "dp", scatter_dimension=dim, tiled=True
+        ).astype(F32)
+
+    gate_sum = owners(dot("sd,sf->df", rows_all, g_gate), 0)
+    up_sum = owners(dot("sd,sf->df", rows_all, g_up), 0)
+    down_sum = owners(dot("sf,sd->fd", act, grad_all), 1)
+    return (
+        layer_out, grad_input, gains[:, 0], query, key, value, out, gains[:, 1],
+        gate_sum, up_sum, down_sum,
+    )
+
+
+def fast_shards(
+    hidden_in, positions, gain_attn, w_query, key_matrix, value_matrix, w_output, gain_mlp,
+    w_gate, w_up, w_down, cotangent,
+):
+    o = front(
+        hidden_in, cotangent, positions, gain_attn, gain_mlp, w_query, key_matrix, value_matrix,
+        w_output,
+    )
+    return rest_of_layer(hidden_in, gain_attn, o, w_gate, w_up, w_down)
+
+
 def solution(mesh):
     placed = (
         P(("dp", "tensor"), None),
@@ -308,8 +880,9 @@
         P("tensor", None),
         P(("dp", "tensor"), None),
     )
+    fits = mesh.shape["dp"] == 8 and mesh.shape["tensor"] == 4
     return jax.shard_map(
-        shards,
+        fast_shards if fits else shards,
         mesh=mesh,
         in_specs=placed,
         out_specs=(

time: 883 us -> 722 us (0.82)
  blocking collectives: 123 us -> 0 us
  matrix products: 155 us -> 57.6 us
  Pallas kernels: 0 us -> 88.4 us
  local copies, waits for them, and re-layouts: 80.7 us -> 16.5 us
  waiting for transfers between devices: 468 us -> 514 us
  other arithmetic: 35.5 us -> 19.4 us
    reduce_scatter x5 -> x8, waiting for transfers between devices: 130 us -> 364 us  [the longest x3 137 us: owners(): lax.psum_scatter(a.astype(BF16), 'dp', scatter_dimension=dim, tiled=True)]
    all_gather x6 -> x1, waiting for transfers between devices: 153 us -> 47.7 us  [rest_of_layer(): rows_all = lax.all_gather(normed_two, 'tensor', axis=0, tiled=True)]
    dot_general x77 -> x18, matrix products: 155 us -> 57.6 us  [dot(): return jnp.einsum(spec, a, b, preferred_element_type=F32)]
    unnamed x17 -> x11, waiting for transfers between devices: 184 us -> 95.8 us
    pallas_call x0 -> x1, Pallas kernels: none -> 88.4 us  [front(): pl.pallas_call(front_kernel, out_shape=[sds(*v) for v in shapes.values()]...]
    unnamed x2 -> x0, blocking collectives: 82.6 us -> none
    all_gather x2 -> x0, blocking collectives: 40.7 us -> none  [the longest x1 21.3 us: shards(): lax.all_gather(value_rows_lowered, 'tensor', axis=0, tiled=True)]
    unnamed x76 -> x49, local copies, waits for them, and re-layouts: 44.9 us -> 6.14 us
  transfers between devices with their start and end apart: 14 -> 12, of which waited for: 12 -> 11; matrix products, arithmetic and copies ran while one was open for 19% -> 7% of each run, Pallas kernels for 0% -> 0%
where the time goes in v2:
time: 722 us; the launch traced here: 719 us
  waiting for transfers between devices  514 us (71%)
  Pallas kernels  88.4 us (12%)
  matrix products  57.6 us (8%)
  other arithmetic  19.4 us (3%)
  local copies, waits for them, and re-layouts  16.5 us (2%)
  between operations  14.6 us (2%)
  starting transfers between devices  8.88 us (1%)
    reduce_scatter x3, waiting for transfers between devices, owners(): lax.psum_scatter(a.astype(BF16), 'dp', scatter_dimension=dim, tiled=True)  137 us
    reduce_scatter x1, waiting for transfers between devices, rest_of_layer(): lax.psum_scatter(grad_out.astype(BF16), ('dp', 'tensor'), scatter_dimensi...  107 us
    unnamed x11, waiting for transfers between devices  95.8 us
    pallas_call x1, Pallas kernels, front(): pl.pallas_call(front_kernel, out_shape=[sds(*v) for v in shapes.values()]...  88.4 us
    reduce_scatter x3, waiting for transfers between devices, over_tokens(): lax.psum_scatter(a.astype(BF16), 'tensor', scatter_dimension=0, tiled=True)  76.2 us
    dot_general x18, matrix products, dot(): return jnp.einsum(spec, a, b, preferred_element_type=F32)  57.6 us
    all_gather x1, waiting for transfers between devices, rest_of_layer(): rows_all = lax.all_gather(normed_two, 'tensor', axis=0, tiled=True)  47.7 us
    reduce_scatter x1, waiting for transfers between devices, rest_of_layer(): lax.psum_scatter(grad_w.astype(BF16), 'dp', scatter_dimension=0, tiled=True)  43.8 us
  transfers between devices with their start and end apart: 12, of which 11 were waited for; matrix products, arithmetic and copies ran while one was open for 7% of the time, Pallas kernels for 0%

profile of v2, /device:TPU:4, one launch (start us, length us, event | category | flops | bytes accessed | tf_op | source)
XLA Modules:
  0.0 719.3 jit_solution(740701140360268716)
XLA Ops:
  13.0 88.4 %front.1 = (bf16[512,1536]{1,0:T(8,128)(2,1)}, bf16[1536,768]{1,0:T(8,128)(2,1)}, bf16[1536,1536]{1,0:T(8,128)(2,1)}, bf16[8,512,128]{2,1,0:T(8,128)(2,1)}, f32[...) custom-call(bf16[128,1536]{1,0:T(8,128)(2,1)} %hid.1, ...), custom_call_target="tpu_custom_call" | custom-call | tf_op jit(solution)/shard_map/front/pallas_call | solution.py:440
  101.5 47.7 %all-gather.2.cloned.1.call-done = bf16[512,1536]{1,0:T(8,128)(2,1)} async-done(((bf16[128,1536]{1,0:T(8,128)(2,1)}), bf16[512,1536]{1,0:T(8,128)(2,1)}) %all-gather.2.cloned.1.call-update) | async-done | bytes 1572880 | tf_op jit(solution)/shard_map/all_gather | solution.py:768
  149.2 4.3 fusion.42
  155.8 3.5 multiply_convert_fusion.1
  165.3 5.3 convolution_convert_fusion.6
  171.7 27.7 %reduce-scatter.14.cloned.1.call-done = bf16[128,1536]{1,0:T(8,128)(2,1)} async-done(((bf16[512,1536]{1,0:T(8,128)(2,1)}), bf16[128,1536]{1,0:T(8,128)(2,1)}) %reduce-scatter.14.cloned.1.call-update) | async-done | bytes 393232 | tf_op jit(solution)/shard_map/reduce_scatter | solution.py:760
  201.3 34.8 %reduce-scatter.12.cloned.1.call-done = bf16[128,1536]{1,0:T(8,128)(2,1)} async-done(((bf16[512,1536]{1,0:T(8,128)(2,1)}), bf16[128,1536]{1,0:T(8,128)(2,1)}) %reduce-scatter.12.cloned.1.call-update) | async-done | bytes 393232 | tf_op jit(solution)/shard_map/reduce_scatter | solution.py:760
  238.4 4.0 convolution_convert_fusion.7
  243.2 3.5 all-to-all-start
  251.7 6.5 all-to-all-done
  258.6 3.6 bitcast_reduce_fusion
  270.5 4.7 convolution_convert_fusion.1
  276.8 4.8 convolution_convert_fusion.2
  281.7 4.8 convolution_convert_fusion.3
  286.6 4.3 convolution_convert_fusion.4
  291.2 13.7 %reduce-scatter.16.cloned.1.call-done = bf16[128,1536]{1,0:T(8,128)(2,1)} async-done(((bf16[512,1536]{1,0:T(8,128)(2,1)}), bf16[128,1536]{1,0:T(8,128)(2,1)}) %reduce-scatter.16.cloned.1.call-update) | async-done | bytes 393232 | tf_op jit(solution)/shard_map/reduce_scatter | solution.py:760
  307.5 3.5 convolution_convert_fusion
  311.0 42.0 %reduce-scatter.26.cloned.1.call-done = bf16[1024,192]{0,1:T(8,128)(2,1)} async-done(((bf16[1024,1536]{0,1:T(8,128)(2,1)}), bf16[1024,192]{0,1:T(8,128)(2,1)}) %reduce-scatter.26.cloned.1.call-update) | async-done | bytes 393232 | tf_op jit(solution)/shard_map/reduce_scatter | solution.py:844
  355.0 47.4 %reduce-scatter.24.cloned.1.call-done = bf16[192,1024]{1,0:T(8,128)(2,1)} async-done(((bf16[1536,1024]{1,0:T(8,128)(2,1)}), bf16[192,1024]{1,0:T(8,128)(2,1)}) %reduce-scatter.24.cloned.1.call-update) | async-done | bytes 393232 | tf_op jit(solution)/shard_map/reduce_scatter | solution.py:844
  404.3 47.5 %reduce-scatter.22.cloned.1.call-done = bf16[192,1024]{1,0:T(8,128)(2,1)} async-done(((bf16[1536,1024]{1,0:T(8,128)(2,1)}), bf16[192,1024]{1,0:T(8,128)(2,1)}) %reduce-scatter.22.cloned.1.call-update) | async-done | bytes 393232 | tf_op jit(solution)/shard_map/reduce_scatter | solution.py:844
  453.8 43.8 %reduce-scatter.18.cloned.1.call-done = bf16[192,768]{1,0:T(8,128)(2,1)} async-done(((bf16[1536,768]{1,0:T(8,128)(2,1)}), bf16[192,768]{1,0:T(8,128)(2,1)}) %reduce-scatter.18.cloned.1.call-update) | async-done | bytes 294928 | tf_op jit(solution)/shard_map/reduce_scatter | solution.py:830
  497.6 4.6 all-to-all-start.1
  503.3 95.6 %reduce-scatter.28.cloned.1.call-done = f32[48,2]{1,0:T(8,128)} async-done(((f32[1536,2]{1,0:T(8,128)}), f32[48,2]{1,0:T(8,128)}) %reduce-scatter.28.cloned.1.call-update) | async-done | bytes 400
  603.8 107.0 %reduce-scatter.20.cloned.1.call-done = bf16[48,1536]{1,0:T(8,128)(2,1)} async-done(((bf16[1536,1536]{1,0:T(8,128)(2,1)}), bf16[48,1536]{1,0:T(8,128)(2,1)}) %reduce-scatter.20.cloned.1.call-update) | async-done | bytes 147472 | tf_op jit(solution)/shard_map/reduce_scatter | solution.py:839
  (131 shorter events, 51.7 us)
Async XLA Ops:
  7.2 142.0 %all-gather.2.cloned.1.call-start = ((), (), s32[]{:S(2)}) async-start(), calls=%async_computation.11 | async-start | bytes 1966080 | tf_op jit(solution)/shard_map/all_gather | solution.py:768
  101.5 52.0 %copy-start.14 = (bf16[1536,1024]{1,0:T(8,128)(2,1)S(1)}, bf16[1536,1024]{1,0:T(8,128)(2,1)}, u32[]{:S(2)}) copy-start(bf16[1536,1024]{1,0:T(8,128)(2,1)} %param.23) | copy-start | bytes 9437188
  101.5 98.0 %reduce-scatter.14.cloned.1.call-start = ((), (), s32[]{:S(2)}) async-start(), calls=%async_computation.13 | async-start | bytes 1966080 | tf_op jit(solution)/shard_map/reduce_scatter | solution.py:760
  149.2 4.3 copy-start.18
  165.0 71.1 %reduce-scatter.12.cloned.1.call-start = ((), (), s32[]{:S(2)}) async-start(), calls=%async_computation.12 | async-start | bytes 1966080 | tf_op jit(solution)/shard_map/reduce_scatter | solution.py:760
  165.3 6.3 copy-start.1
  165.3 6.4 copy-start.5
  238.4 9.4 %copy-start.13 = (f32[1,512]{1,0:T(1,128)S(1)}, f32[1,512]{1,0:T(1,128)}, u32[]{:S(2)}) copy-start(f32[1,512]{1,0:T(1,128)} %get-tuple-element.26) | copy-start | bytes 6148
  238.4 9.4 %copy-start.12 = (f32[4,1,512]{2,1,0:T(1,128)S(1)}, f32[4,1,512]{2,1,0:T(1,128)}, u32[]{:S(2)}) copy-start(f32[4,1,512]{2,1,0:T(1,128)} %get-tuple-element.28) | copy-start | bytes 24580
  243.2 15.0 %all-to-all-start = ((bf16[128,4,384]{2,0,1:T(8,128)(2,1)}), bf16[128,4,384]{2,0,1:T(8,128)(2,1)S(1)}, u32[]{:S(2)}, u32[]{:S(2)}) async-start(bf16[128,4,384]{2,0,1:T(8,128)(2,1)} %bitcast.82), calls=%async_computation.2 | async-start | bytes 786432 | tf_op jit(solution)/shard_map/all_to_all | solution.py:789
  246.7 58.2 %reduce-scatter.16.cloned.1.call-start = ((), (), s32[]{:S(2)}) async-start(), calls=%async_computation.14 | async-start | bytes 1966080 | tf_op jit(solution)/shard_map/reduce_scatter | solution.py:760
  258.6 3.6 copy-start.8
  258.6 3.6 copy-start
  270.3 82.8 %reduce-scatter.26.cloned.1.call-start = ((), (), s32[]{:S(2)}) async-start(), calls=%async_computation.19 | async-start | bytes 3538944 | tf_op jit(solution)/shard_map/reduce_scatter | solution.py:844
  275.3 127.1 %reduce-scatter.24.cloned.1.call-start = ((), (), s32[]{:S(2)}) async-start(), calls=%async_computation.18 | async-start | bytes 3538944 | tf_op jit(solution)/shard_map/reduce_scatter | solution.py:844
  281.6 170.2 %reduce-scatter.22.cloned.1.call-start = ((), (), s32[]{:S(2)}) async-start(), calls=%async_computation.17 | async-start | bytes 3538944 | tf_op jit(solution)/shard_map/reduce_scatter | solution.py:844
  286.5 211.1 %reduce-scatter.18.cloned.1.call-start = ((), (), s32[]{:S(2)}) async-start(), calls=%async_computation.15 | async-start | bytes 2654208 | tf_op jit(solution)/shard_map/reduce_scatter | solution.py:830
  286.5 4.4 copy-start.2
  286.5 4.6 copy-start.11
  290.9 16.6 %copy-start.4 = (bf16[128,1536]{1,0:T(8,128)(2,1)S(1)}, bf16[128,1536]{1,0:T(8,128)(2,1)}, u32[]{:S(2)}) copy-start(bf16[128,1536]{1,0:T(8,128)(2,1)} %get-tuple-element.32) | copy-start | bytes 1179652
  290.9 308.0 %reduce-scatter.28.cloned.1.call-start = ((), (), s32[]{:S(2)}) async-start(), calls=%async_computation.20 | async-start | bytes 811008
  307.4 403.5 %reduce-scatter.20.cloned.1.call-start = ((), (), s32[]{:S(2)}) async-start(), calls=%async_computation.16 | async-start | bytes 4866048 | tf_op jit(solution)/shard_map/reduce_scatter | solution.py:839
  311.0 191.1 %copy-start.3 = (bf16[128,1536]{1,0:T(8,128)(2,1)S(1)}, bf16[128,1536]{1,0:T(8,128)(2,1)}, u32[]{:S(2)}) copy-start(bf16[128,1536]{1,0:T(8,128)(2,1)} %reduce-scatter.16.cloned.1.call-done) | copy-start | bytes 1179652
  497.6 103.5 %all-to-all-start.1 = ((bf16[4,48,768]{2,1,0:T(8,128)(2,1)}), bf16[4,48,768]{2,1,0:T(8,128)(2,1)S(1)}, u32[]{:S(2)}, u32[]{:S(2)}) async-start(bf16[4,48,768]{2,1,0:T(8,128)(2,1)} %bitcast.94), calls=%async_computation.5 | async-start | bytes 589824 | tf_op jit(solution)/shard_map/all_to_all | solution.py:832
  (10 other events, 19.3 us)
Sparse Core Ops, SparseCore 0:
  101.6 47.5 all-gather.1
  165.1 34.2 reduce-scatter.13
  201.8 34.2 reduce-scatter.11
  270.4 34.4 reduce-scatter.15
  308.1 44.8 reduce-scatter.25
  356.3 46.0 reduce-scatter.23
  405.7 46.0 reduce-scatter.21
  455.2 42.3 reduce-scatter.17
  502.7 96.2 reduce-scatter.27
  604.3 106.5 reduce-scatter.19

commit v3 on v2

--- a/solution.py
+++ b/solution.py
@@ -461,6 +461,605 @@
             collective_id=0, has_side_effects=True, vmem_limit_bytes=VMEM_LIMIT
         ),
     )(hid, cot, tile, wpack, wo, near_cos, near_sin, shift)
+    return dict(zip(shapes, outs), tables=(near_cos, near_sin, shift))
+
+
+def feed_forward_kernel(
+    nrm, cot, gains, resid, wg, wu, wd, wo,
+    mlp_out, gatt_out, gres_out, low_out, gain_out, dws_out,
+    rows_all, cot_all, gate_w, up_w, down_w, out_w, act, gg, gu, msend, gsend, gown, grecv,
+    gatt, gres, low, gain, part, crecv,
+    tsend, trecv, csend, crsem, local, store,
+):
+    t, d = lax.axis_index("tensor"), lax.axis_index("dp")
+    ln = Links(tsend, trecv, csend, crsem)
+    rows, width = nrm.shape
+    span = width // 4
+    half = span // 2
+    core = lax.rem(d, 2)
+    N, G = range(2)
+
+    def at_shard(ref, shard):
+        return ref.at[pl.ds(pl.multiple_of(shard * rows, rows), rows), :]
+
+    def ds_of(shard):
+        return pl.ds(pl.multiple_of(shard * rows, rows), rows)
+
+    rows_of = functools.partial(at_shard, rows_all)
+    loads = [
+        pltpu.make_async_copy(a, b, local.at[i])
+        for i, (a, b) in enumerate(
+            [(nrm, rows_of(t)), (wg, gate_w), (wu, up_w), (cot, cot_all), (wd, down_w), (wo, out_w)]
+        )
+    ]
+    for c in loads:
+        c.start()
+    ln.barrier((1, 2, 3), (1,))
+    ln.gather_start(N, nrm, rows_of)
+    for c in loads[:5]:
+        c.wait()
+
+    def to_owner(shard, m):
+        return pltpu.make_async_remote_copy(
+            src_ref=gsend.at[shard],
+            dst_ref=grecv.at[m - 1],
+            send_sem=tsend.at[G, m],
+            recv_sem=trecv.at[G, m],
+            device_id={"dp": d, "tensor": shard},
+            device_id_type=MESH,
+        )
+
+    def one_shard(i, carry):
+        shard, m = ln.shard_at(i)
+
+        @pl.when(i > 0)
+        def _():
+            ln.gather_take(N, i, rows_of)
+
+        at = ds_of(shard)
+        r = rows_all[at, :]
+        gate = mm(r, gate_w[...])
+        up = mm(r, up_w[...])
+        sig = 1.0 / (1.0 + jnp.exp(-gate))
+        silu = gate * sig
+        act[at, :] = (silu * up).astype(BF16)
+        g_act = mm(cot_all[at, :], down_w[...], NT)
+        gg[at, :] = (g_act * up * sig * (1.0 + gate * (1.0 - sig))).astype(BF16)
+        gu[at, :] = (g_act * silu).astype(BF16)
+        g = mm(gg[at, :], gate_w[...], NT) + mm(gu[at, :], up_w[...], NT)
+
+        @pl.when(i == 0)
+        def _():
+            gown[...] = g
+
+        @pl.when(i > 0)
+        def _():
+            gsend[shard] = g.astype(BF16)
+            to_owner(shard, m).start()
+
+        msend[shard] = mm(act[at, :], down_w[...]).astype(BF16)
+        return carry
+
+    lax.fori_loop(0, 4, one_shard, 0)
+
+    def block(ref, k, j, side):
+        return ref.at[k, pl.ds(pl.multiple_of(j * span + side * half, half), half), :]
+
+    def to_core(k, j):
+        return pltpu.make_async_remote_copy(
+            src_ref=block(part, k, j, 1 - core),
+            dst_ref=crecv.at[j, k],
+            send_sem=csend.at[k, j],
+            recv_sem=crsem.at[k, j],
+            device_id={"dp": dp_peer(d, 1), "tensor": t},
+            device_id_type=MESH,
+        )
+
+    def weights(j, carry):
+        cols = pl.ds(pl.multiple_of(j * span, 128), span)
+        for k, (a, b) in enumerate(((rows_all, gg), (rows_all, gu), (cot_all, act))):
+            part[k, cols, :] = mm(a[:, cols], b[...], TN).astype(BF16)
+            to_core(k, j).start()
+        return carry
+
+    lax.fori_loop(0, 4, weights, 0)
+    stores = [pltpu.make_async_copy(msend, mlp_out, store.at[0])]
+    stores[0].start()
+
+    def chip_sums(j, carry):
+        for k in range(3):
+            to_core(k, j).wait_recv()
+            mine = pl.ds(pl.multiple_of(j * span + core * half, half), half)
+            crecv[j, k] = (part[k, mine, :].astype(F32) + crecv[j, k].astype(F32)).astype(BF16)
+        return carry
+
+    lax.fori_loop(0, 4, chip_sums, 0)
+    stores.append(pltpu.make_async_copy(crecv, dws_out, store.at[1]))
+    stores[1].start()
+    loads[5].wait()
+    for m in (1, 2, 3):
+        ln.landed_tensor(G, m, grecv.at[m - 1])
+    g = gown[...]
+    for m in (1, 2, 3):
+        g = g + grecv[m - 1].astype(F32)
+    r = resid[...]
+    inv = lax.rsqrt(jnp.mean(r * r, axis=1, keepdims=True) + EPSILON)
+    gain[0] = jnp.sum(g * r * inv, axis=0, keepdims=True)
+    scaled = g * gains[1:2, :]
+    gr = (
+        cot_all[ds_of(t), :].astype(F32)
+        + inv * scaled
+        - r * (inv * inv * inv) * jnp.mean(scaled * r, axis=1, keepdims=True)
+    )
+    gres[...] = gr
+    low[...] = gr.astype(BF16)
+    for s in range(4):
+        gatt[s] = mm(low[...], out_w[s * span : (s + 1) * span, :], NT).astype(BF16)
+    for i, (a, b) in enumerate(((gatt, gatt_out), (gres, gres_out), (low, low_out), (gain, gain_out))):
+        stores.append(pltpu.make_async_copy(a, b, store.at[2 + i]))
+        stores[-1].start()
+    ln.gather_end(N, nrm, rows_of)
+    for m in (1, 2, 3):
+        to_owner(tensor_peer(t, m), m).wait_send()
+
+    def sent(j, carry):
+        for k in range(3):
+            to_core(k, j).wait_send()
+        return carry
+
+    lax.fori_loop(0, 4, sent, 0)
+    for c in stores:
+        c.wait()
+
+
+def feed_forward(o, w_gate, w_up, w_down):
+    rows, width = o["normed2"].shape
+    units = w_gate.shape[1]
+    span = width // 4
+    seq = 4 * rows
+    hbm = pl.BlockSpec(memory_space=pl.ANY)
+    vmem = pl.BlockSpec(memory_space=pltpu.VMEM)
+    shapes = dict(
+        mlp=((4, rows, width), BF16), g_att=((4, rows, span), BF16), g_resid=((rows, width), F32),
+        low=((rows, width), BF16), gain=((1, 1, width), F32),
+        grads=((4, 3, span // 2, units), BF16),
+    )
+    S = {k: pltpu.VMEM(*v) for k, v in shapes.items()}
+    wide = pltpu.VMEM((seq, width), BF16)
+    hidden = pltpu.VMEM((seq, units), BF16)
+    weight = pltpu.VMEM((width, units), BF16)
+    outs = pl.pallas_call(
+        feed_forward_kernel,
+        out_shape=[jax.ShapeDtypeStruct(*v) for v in shapes.values()],
+        in_specs=[hbm, hbm, vmem, vmem, hbm, hbm, hbm, hbm],
+        out_specs=[hbm] * len(shapes),
+        scratch_shapes=[
+            wide, wide, weight, weight, pltpu.VMEM((units, width), BF16),
+            pltpu.VMEM((width, width), BF16), hidden, hidden, hidden,
+            S["mlp"], S["mlp"], S["g_resid"], pltpu.VMEM((3, rows, width), BF16),
+            S["g_att"], S["g_resid"], S["low"], S["gain"],
+            pltpu.VMEM((3, width, units), BF16), S["grads"],
+            pltpu.SemaphoreType.DMA((2, 6)), pltpu.SemaphoreType.DMA((2, 4)),
+            pltpu.SemaphoreType.DMA((3, 4)), pltpu.SemaphoreType.DMA((3, 4)),
+            pltpu.SemaphoreType.DMA((6,)), pltpu.SemaphoreType.DMA((6,)),
+        ],
+        name="feed_forward",
+        compiler_params=pltpu.CompilerParams(
+            collective_id=1, has_side_effects=True, vmem_limit_bytes=VMEM_LIMIT
+        ),
+    )(o["normed2"], o["cot"], o["gains"], o["resid"], w_gate, w_up, w_down, o["wo"])
+    return dict(zip(shapes, outs))
+
+
+class LineSum:
+    def __init__(self, ln, kind, src, recv):
+        self.ln, self.kind, self.src, self.recv = ln, kind, src, recv
+        t = ln.t
+        self.near, self.two, self.three = (tensor_peer(t, m) for m in (1, 2, 3))
+
+    def copy(self, src, to, slot, sem):
+        ln, kind = self.ln, self.kind
+        return pltpu.make_async_remote_copy(
+            src_ref=src,
+            dst_ref=self.recv.at[slot],
+            send_sem=ln.tsend.at[kind, sem],
+            recv_sem=ln.trecv.at[kind, slot],
+            device_id={"dp": ln.d, "tensor": to},
+            device_id_type=MESH,
+        )
+
+    def first(self, i, shard):
+        c = self.copy(self.src.at[shard], self.near, i, i)
+        if isinstance(i, int):
+            if i == 2:
+                c.start()
+            else:
+                pl.when(self.ln.mid == 0)(c.start)
+        else:
+            pl.when((i == 2) | ((self.ln.mid == 0) & (i < 2)))(c.start)
+
+    def start(self):
+        for i, shard in enumerate((self.three, self.two, self.near)):
+            self.first(i, shard)
+
+    def hand_on(self):
+        @pl.when(self.ln.mid == 1)
+        def _():
+            for i, shard in enumerate((self.two, self.three)):
+                self.ln.landed_tensor(self.kind, i, self.recv.at[i])
+                self.recv[i] = (
+                    self.recv[i].astype(F32) + self.src[shard].astype(F32)
+                ).astype(BF16)
+                self.copy(self.recv.at[i], shard, 3, i).start()
+
+    def take(self):
+        for i in (2, 3):
+            self.ln.landed_tensor(self.kind, i, self.recv.at[i])
+        return self.recv[2].astype(F32) + self.recv[3].astype(F32)
+
+    def end(self):
+        for i in range(3):
+            pltpu.make_async_copy(
+                self.src.at[0], self.src.at[0], self.ln.tsend.at[self.kind, i]
+            ).wait()
+
+
+class PlaneSum:
+    def __init__(self, ln, kind, src, recv):
+        self.ln, self.kind, self.src, self.recv = ln, kind, src, recv
+        j = lax.div(ln.d, 2)
+        self.j = j
+        self.x = j + 1 - 2 * lax.rem(j, 2)
+        self.y = lax.rem(j + 2, 4)
+        self.diag = lax.rem(self.x + 2, 4)
+        self.lanes = src.shape[-1] // 2
+
+    def half(self, ref, h):
+        spot = [slice(None)] * (len(ref.shape) - 1) + [pl.ds(h * self.lanes, self.lanes)]
+        return ref.at[tuple(spot)]
+
+    def copy(self, src, m, i):
+        return self.ln.over_dp(self.kind, i, src, self.recv.at[i], to=m)
+
+    def plan(self):
+        return (
+            (self.half(self.src.at[self.diag], 0), 2, 0),
+            (self.half(self.src.at[self.diag], 1), 4, 2),
+            (self.half(self.src.at[self.x], 0), 2, 1),
+            (self.half(self.src.at[self.y], 1), 4, 3),
+        )
+
+    def start(self):
+        for src, m, i in self.plan():
+            self.copy(src, m, i).start()
+
+    def hand_on(self):
+        for i, h, block, m in ((0, 0, self.y, 4), (2, 1, self.x, 2)):
+            self.ln.landed_dp(self.kind, i, self.recv.at[i])
+            self.recv[i] = (
+                self.recv[i].astype(F32) + self.half(self.src.at[block], h)[...].astype(F32)
+            ).astype(BF16)
+            self.copy_on(i, h, m).start()
+
+    def copy_on(self, i, h, m):
+        return self.ln.over_dp(self.kind, 4 + h, self.recv.at[i], self.recv.at[4 + h], to=m)
+
+    def take(self, h):
+        for i in (1 + 2 * h, 4 + h):
+            self.ln.landed_dp(self.kind, i, self.recv.at[i])
+        own = self.half(self.src.at[self.j], h)[...].astype(F32)
+        return own + self.recv[1 + 2 * h].astype(F32) + self.recv[4 + h].astype(F32)
+
+    def end(self):
+        for src, m, i in self.plan():
+            self.copy(src, m, i).wait_send()
+        for i, h, m in ((0, 0, 4), (2, 1, 2)):
+            self.copy_on(i, h, m).wait_send()
+
+
+class CoreSum:
+    def __init__(self, ln, kind, src, recv):
+        self.ln, self.kind, self.src, self.recv = ln, kind, src, recv
+        self.half = recv.shape[1]
+        self.core = lax.rem(ln.d, 2)
+
+    def side(self, which):
+        return pl.ds(pl.multiple_of(which * self.half, self.half), self.half)
+
+    def copy(self, j):
+        ln = self.ln
+        return pltpu.make_async_remote_copy(
+            src_ref=self.src.at[j, self.side(1 - self.core), :],
+            dst_ref=self.recv.at[j],
+            send_sem=ln.dsend.at[self.kind, j],
+            recv_sem=ln.drecv.at[self.kind, j],
+            device_id={"dp": dp_peer(ln.d, 1), "tensor": ln.t},
+            device_id_type=MESH,
+        )
+
+    def take(self):
+        def one(j, carry):
+            self.copy(j).wait_recv()
+            self.recv[j] = (
+                self.recv[j].astype(F32) + self.src[j, self.side(self.core), :].astype(F32)
+            ).astype(BF16)
+            return carry
+
+        lax.fori_loop(0, 4, one, 0)
+
+    def end(self):
+        def one(j, carry):
+            self.copy(j).wait_send()
+            return carry
+
+        lax.fori_loop(0, 4, one, 0)
+
+
+def back_kernel(
+    gatt, mlp, heads, lse, start, normed, w, hid, gres, resid, gains, arow, low, grads, gain,
+    near_cos, near_sin, shift,
+    layer_out, gin_out, gain_out, wqkv_out, wo_out, mlpw_out,
+    gall, gh, hd, gq, gk, gv, gqkv, nall, wv, mlp_src, mlp_in, gn_src, gn_in,
+    ff, ff_in, wo_part, wo_core, wo_in, wo_src, wo_line, wq_part, wq_core, wq_in, wq_src, wq_all,
+    rows_in, line_in, layer, gin, gsum, wqkv, wof, ffw,
+    tsend, trecv, dsend, drecv, local, store,
+):
+    ln = Links(tsend, trecv, dsend, drecv)
+    t, d = ln.t, ln.d
+    rows, width = hid.shape
+    span = width // 4
+    A, M, B, O, W, R = range(6)
+    DF, DR, CO, DO, CW, DW = range(6)
+
+    def ds_of(shard):
+        return pl.ds(pl.multiple_of(shard * rows, rows), rows)
+
+    loads = [
+        pltpu.make_async_copy(a, b, local.at[i])
+        for i, (a, b) in enumerate(
+            [
+                (grads, ff), (gatt.at[t], gall.at[ds_of(t), :]), (mlp, mlp_src), (heads, hd),
+                (w, wv), (normed, nall), (gain, rows_in.at[pl.ds(d, 1)]),
+            ]
+        )
+    ]
+    for c in loads:
+        c.start()
+    ln.barrier((1, 2, 3), (1, 2, 3, 4, 5, 6, 7))
+    for m in (3, 2, 1):
+        ln.over_tensor(A, m, gatt.at[tensor_peer(t, m)], gall.at[ds_of(t), :]).start()
+    ff_sum = PlaneSum(ln, DF, ff, ff_in)
+    loads[0].wait()
+    ff_sum.start()
+    for m in range(1, 8):
+        ln.over_dp(DR, m, gain.at[0], rows_in.at[d]).start()
+    layer_sum = LineSum(ln, M, mlp_src, mlp_in)
+    loads[2].wait()
+    layer_sum.start()
+
+    wo_pair = CoreSum(ln, CO, wo_part, wo_core)
+
+    def output_weights(j, carry):
+        cols = pl.ds(pl.multiple_of(j * span, 128), span)
+        wo_part[j] = mm(arow[:, cols], low[...], TN).astype(BF16)
+        wo_pair.copy(j).start()
+        return carry
+
+    lax.fori_loop(0, 4, output_weights, 0)
+
+    for c in (loads[1], loads[3]):
+        c.wait()
+    for m in (1, 2, 3):
+        ln.landed_tensor(A, m, gall.at[ds_of(tensor_peer(t, m)), :])
+    keep = lax.broadcasted_iota(jnp.int32, (rows, 128), 1) < HEAD
+
+    def split(b, carry):
+        u = gall[ds_of(b), :].astype(F32)
+        for h in range(4):
+            gh[h, ds_of(b), :] = jnp.where(keep, lane_roll(u, -HEAD * h)[:, :128], 0.0).astype(BF16)
+        return carry
+
+    lax.fori_loop(0, 4, split, 0)
+    gk[...] = jnp.zeros_like(gk)
+    gv[...] = jnp.zeros_like(gv)
+    scale = 1.0 / math.sqrt(HEAD)
+
+    def attend_back(h, carry):
+        c = lax.div(h, 2)
+        for b in range(4):
+            far = (b + 1) * rows
+            here = slice(b * rows, far)
+            k, v, q, g = hd[4 + c, :far, :], hd[6 + c, :far, :], hd[h, here, :], gh[h, here, :]
+            sc = mm(k, q, NT) * scale
+            key = lax.broadcasted_iota(jnp.int32, sc.shape, 0)
+            query = lax.broadcasted_iota(jnp.int32, sc.shape, 1) + b * rows
+            first = start[:, here].astype(jnp.int32)
+            sc = jnp.where((key <= query) & (key >= first), sc, MASKED)
+            p = jnp.exp(sc - lse[h, :, here])
+            gp = mm(v, g, NT)
+            gs = (p * (gp - jnp.sum(p * gp, axis=0, keepdims=True))).astype(BF16)
+            gq[h, here, :] = mm(gs, k, TN) * scale
+            gk[c, :far, :] += mm(gs, q) * scale
+            gv[c, :far, :] += mm(p.astype(BF16), g)
+        return carry
+
+    lax.fori_loop(0, 4, attend_back, 0)
+
+    def gather_heads(b, carry):
+        at = ds_of(b)
+        cosine, sine = turn_tables(near_cos, near_sin, shift, b)
+        cosine, sine = cosine[:, :128], sine[:, :128]
+
+        def placed(u, h):
+            u = jnp.concatenate(
+                [jnp.where(keep, u, 0.0), jnp.zeros((rows, 4 * HEAD - 128), F32)], axis=1
+            )
+            return lane_roll(u, HEAD * h)
+
+        def turned(u):
+            return u * cosine - swap_halves(u) * sine
+
+        left = sum(placed(turned(gq[h, at, :]), h) for h in range(4))
+        right = sum(placed(turned(gk[c, at, :]), c) for c in range(2))
+        right = right + sum(placed(gv[c, at, :], c + 2) for c in range(2))
+        gqkv[at, : 4 * HEAD] = left.astype(BF16)
+        gqkv[at, 4 * HEAD :] = right.astype(BF16)
+        return carry
+
+    lax.fori_loop(0, 4, gather_heads, 0)
+    for c in (loads[4], loads[5]):
+        c.wait()
+    gn_sum = LineSum(ln, B, gn_src, gn_in)
+
+    def norm_grads(i, carry):
+        shard, _ = ln.shard_at(3 - i)
+        gn_src[shard] = mm(gqkv[ds_of(shard), :], wv[...], NT).astype(BF16)
+        gn_sum.first(i, shard)
+        return carry
+
+    layer_sum.hand_on()
+    lax.fori_loop(0, 4, norm_grads, 0)
+    wo_pair.take()
+    wo_sum = PlaneSum(ln, DO, wo_core, wo_in)
+    wo_sum.start()
+    wq_pair = CoreSum(ln, CW, wq_part, wq_core)
+
+    def head_weights(j, carry):
+        cols = pl.ds(pl.multiple_of(j * span, 128), span)
+        wq_part[j] = mm(nall[:, cols], gqkv[...], TN).astype(BF16)
+        wq_pair.copy(j).start()
+        return carry
+
+    lax.fori_loop(0, 4, head_weights, 0)
+    ff_sum.hand_on()
+    gn_sum.hand_on()
+    wq_pair.take()
+    wq_sum = PlaneSum(ln, DW, wq_core, wq_in)
+    wq_sum.start()
+    wo_sum.hand_on()
+
+    loads[6].wait()
+    for m in range(1, 8):
+        ln.landed_dp(DR, m, rows_in.at[dp_peer(d, m)])
+    gsum[0] = sum(rows_in[i] for i in range(8))
+    for m in (1, 2, 3):
+        ln.over_tensor(R, m, gsum.at[0], line_in.at[m]).start()
+
+    stores = []
+
+    def out(a, b):
+        c = pltpu.make_async_copy(a, b, store.at[len(stores)])
+        c.start()
+        stores.append(c)
+
+    layer[...] = (resid[...] + mlp_src[t].astype(F32) + layer_sum.take()).astype(BF16)
+    out(layer, layer_out)
+    lanes = ff_sum.lanes
+    for h in range(2):
+        ffw[:, :, h * lanes : (h + 1) * lanes] = ff_sum.take(h)
+    out(ffw, mlpw_out)
+    wq_sum.hand_on()
+    x = hid[...].astype(F32)
+    inv = lax.rsqrt(jnp.mean(x * x, axis=1, keepdims=True) + EPSILON)
+    scaled = (gn_src[t].astype(F32) + gn_sum.take()) * gains[0:1, :]
+    gin[...] = (
+        gres[...]
+        + inv * scaled
+        - x * (inv * inv * inv) * jnp.mean(scaled * x, axis=1, keepdims=True)
+    )
+    out(gin, gin_out)
+    wrows = wo_src.shape[1]
+    lanes = wo_sum.lanes
+    for h in range(2):
+        u = wo_sum.take(h).astype(BF16)
+        for s in range(4):
+            wo_src[s, :, h * lanes : (h + 1) * lanes] = u[s * wrows : (s + 1) * wrows, :]
+    wo_line_sum = LineSum(ln, O, wo_src, wo_line)
+    wo_line_sum.start()
+    total = gsum[0]
+    for m in (1, 2, 3):
+        ln.landed_tensor(R, m, line_in.at[m])
+        total = total + line_in[m]
+    line_in[0] = total
+    out(line_in.at[0], gain_out)
+    lanes = wq_sum.lanes
+    for h in range(2):
+        u = wq_sum.take(h).astype(BF16)
+        for s in range(4):
+            wq_src[s, :, h * lanes : (h + 1) * lanes] = u[s * wrows : (s + 1) * wrows, :]
+    for m in (3, 2, 1):
+        ln.over_tensor(W, m, wq_src.at[tensor_peer(t, m)], wq_all.at[m]).start()
+    wqkv[pl.ds(t, 1)] = wq_src[pl.ds(t, 1)].astype(F32)
+    wo_line_sum.hand_on()
+    for m in (1, 2, 3):
+        ln.landed_tensor(W, m, wq_all.at[m])
+        wqkv[pl.ds(tensor_peer(t, m), 1)] = wq_all[pl.ds(m, 1)].astype(F32)
+    out(wqkv, wqkv_out)
+    wof[...] = wo_src[t].astype(F32) + wo_line_sum.take()
+    out(wof, wo_out)
+
+    for m in (1, 2, 3):
+        ln.over_tensor(A, m, gatt.at[tensor_peer(t, m)], gall.at[ds_of(t), :]).wait_send()
+        ln.over_tensor(R, m, gsum.at[0], line_in.at[m]).wait_send()
+        ln.over_tensor(W, m, wq_src.at[tensor_peer(t, m)], wq_all.at[m]).wait_send()
+    for m in range(1, 8):
+        ln.over_dp(DR, m, gain.at[0], rows_in.at[d]).wait_send()
+    for s in (layer_sum, gn_sum, wo_line_sum, ff_sum, wo_sum, wq_sum, wo_pair, wq_pair):
+        s.end()
+    for c in stores:
+        c.wait()
+
+
+def back(o, f, hid, tables):
+    rows, width = hid.shape
+    seq = 4 * rows
+    span = width // 4
+    wrows = span // 8
+    units = f["grads"].shape[-1]
+    hbm = pl.BlockSpec(memory_space=pl.ANY)
+    vmem = pl.BlockSpec(memory_space=pltpu.VMEM)
+    V = pltpu.VMEM
+    shapes = dict(
+        layer=((rows, width), BF16), gin=((rows, width), F32), gain=((1, width), F32),
+        wqkv=((4, wrows, 8 * HEAD), F32), wo=((wrows, width), F32),
+        mlp=((3, span // 2, units), F32),
+    )
+    operands = [
+        (f["g_att"], hbm), (f["mlp"], hbm), (o["heads"], hbm), (o["lse"], vmem), (o["start"], vmem),
+        (o["normed"], hbm), (o["w"], hbm), (hid, vmem), (f["g_resid"], vmem), (o["resid"], vmem),
+        (o["gains"], vmem), (o["rows"], vmem), (f["low"], vmem), (f["grads"], hbm),
+        (f["gain"], hbm), (tables[0], vmem), (tables[1], vmem), (tables[2], vmem),
+    ]
+    half = span // 2
+    four = V((4, rows, width), BF16)
+    outs = pl.pallas_call(
+        back_kernel,
+        out_shape=[jax.ShapeDtypeStruct(*v) for v in shapes.values()],
+        in_specs=[s for _, s in operands],
+        out_specs=[hbm] * len(shapes),
+        scratch_shapes=[
+            V((seq, span), BF16), V((4, seq, 128), BF16), V((8, seq, 128), BF16),
+            V((4, seq, 128), F32), V((2, seq, 128), F32), V((2, seq, 128), F32),
+            V((seq, 8 * HEAD), BF16), V((seq, width), BF16), V((width, 8 * HEAD), BF16),
+            four, four, four, four,
+            V((4, 3, half, units), BF16), V((6, 3, half, units // 2), BF16),
+            V((4, span, width), BF16), V((4, half, width), BF16), V((6, half, width // 2), BF16),
+            V((4, wrows, width), BF16), V((4, wrows, width), BF16),
+            V((4, span, 8 * HEAD), BF16), V((4, half, 8 * HEAD), BF16),
+            V((6, half, 4 * HEAD), BF16), V((4, wrows, 8 * HEAD), BF16),
+            V((4, wrows, 8 * HEAD), BF16),
+            V((8, 1, width), F32), V((4, 1, width), F32),
+            V((rows, width), BF16), V((rows, width), F32), V((1, 1, width), F32),
+            V((4, wrows, 8 * HEAD), F32), V((wrows, width), F32), V((3, half, units), F32),
+            pltpu.SemaphoreType.DMA((6, 4)), pltpu.SemaphoreType.DMA((6, 4)),
+            pltpu.SemaphoreType.DMA((6, 8)), pltpu.SemaphoreType.DMA((6, 8)),
+            pltpu.SemaphoreType.DMA((7,)), pltpu.SemaphoreType.DMA((6,)),
+        ],
+        name="back",
+        compiler_params=pltpu.CompilerParams(
+            collective_id=2, has_side_effects=True, vmem_limit_bytes=VMEM_LIMIT
+        ),
+    )(*[a for a, _ in operands])
     return dict(zip(shapes, outs))
 
 
@@ -747,113 +1346,6 @@
     )
 
 
-def rest_of_layer(hidden, gain_one_rows, o, w_gate, w_up, w_down):
-    rows, width = hidden.shape
-    seq = 4 * rows
-    gain_one, gain_two = o["gains"][0:1], o["gains"][1:2]
-    resid, normed_two = o["resid"], o["normed2"]
-    grad_all = o["cot"]
-    t = lax.axis_index("tensor")
-    grad_float = lax.dynamic_slice_in_dim(grad_all, t * rows, rows, 0).astype(F32)
-
-    def over_tokens(a):
-        return lax.psum_scatter(
-            a.astype(BF16), "tensor", scatter_dimension=0, tiled=True
-        ).astype(F32)
-
-    def dot(spec, a, b):
-        return jnp.einsum(spec, a, b, preferred_element_type=F32)
-
-    inv_two = lax.rsqrt(jnp.mean(resid * resid, axis=-1, keepdims=True) + EPSILON)
-    rows_all = lax.all_gather(normed_two, "tensor", axis=0, tiled=True)
-    gate = dot("sd,df->sf", rows_all, w_gate)
-    up = dot("sd,df->sf", rows_all, w_up)
-    sig = jax.nn.sigmoid(gate)
-    silu = gate * sig
-    act = (silu * up).astype(BF16)
-    g_act = dot("sd,fd->sf", grad_all, w_down)
-    g_gate = (g_act * up * sig * (1.0 + gate * (1.0 - sig))).astype(BF16)
-    g_up = (g_act * silu).astype(BF16)
-    g_norm_two = over_tokens(dot("sf,df->sd", g_gate, w_gate) + dot("sf,df->sd", g_up, w_up))
-    layer_out = (resid + over_tokens(dot("sf,fd->sd", act, w_down))).astype(BF16)
-    scaled = gain_two * g_norm_two
-    g_resid = (
-        grad_float
-        + inv_two * scaled
-        - resid * inv_two**3 * jnp.mean(scaled * resid, axis=-1, keepdims=True)
-    )
-    g_resid_low = g_resid.astype(BF16)
-    gain_two_grad = jnp.sum(g_norm_two * resid * inv_two, axis=0)
-    grad_out = dot("tc,td->cd", o["rows"], g_resid_low)
-    g_att = dot("td,cd->tc", g_resid_low, o["wo"]).astype(BF16)
-    g_att = lax.all_to_all(g_att, "tensor", split_axis=1, concat_axis=0, tiled=True)
-    g_heads = g_att.reshape(seq, 4, HEAD).transpose(1, 0, 2)
-    q = o["heads"][0:4, :, :HEAD]
-    k = jnp.repeat(o["heads"][4:6, :, :HEAD], 2, axis=0)
-    v = jnp.repeat(o["heads"][6:8, :, :HEAD], 2, axis=0)
-    scale = 1.0 / math.sqrt(HEAD)
-    index = jnp.arange(seq, dtype=jnp.int32)
-    first = o["start"][0].astype(jnp.int32)
-    visible = (index[None, :] <= index[:, None]) & (index[None, :] >= first[:, None])
-    scores = jnp.where(visible[None], dot("hqd,hkd->hqk", q, k) * scale, MASKED)
-    probs = jnp.exp(scores - o["lse"][:, 0, :, None])
-    g_probs = dot("hqd,hkd->hqk", g_heads, v)
-    g_scores = (probs * (g_probs - jnp.sum(probs * g_probs, axis=-1, keepdims=True))).astype(BF16)
-    g_rq = dot("hqk,hkd->hqd", g_scores, k) * scale
-    g_rk = dot("hqk,hqd->hkd", g_scores, q) * scale
-    g_v = dot("hqk,hqd->hkd", probs.astype(BF16), g_heads)
-    g_rk = g_rk.reshape(2, 2, seq, HEAD).sum(1)
-    g_v = g_v.reshape(2, 2, seq, HEAD).sum(1)
-    rates = ROPE_BASE ** (-(jnp.arange(HEAD // 2, dtype=F32) * 2.0) / HEAD)
-    turned = index.astype(F32)[:, None] * rates[None, :]
-    cosine, sine = jnp.cos(turned), jnp.sin(turned)
-
-    def turn_back(u):
-        a, b = u[..., : HEAD // 2], u[..., HEAD // 2 :]
-        return jnp.concatenate([a * cosine + b * sine, b * cosine - a * sine], axis=-1)
-
-    g = jnp.concatenate([turn_back(g_rq), turn_back(g_rk), g_v], axis=0).astype(BF16)
-    g = g.transpose(1, 0, 2).reshape(seq, 8 * HEAD)
-    grad_w = dot("sc,sd->cd", o["normed"], g)
-    g_norm_one = over_tokens(dot("sd,cd->sc", g, o["w"]))
-    x = hidden.astype(F32)
-    inv_one = lax.rsqrt(jnp.mean(x * x, axis=-1, keepdims=True) + EPSILON)
-    scaled = gain_one * g_norm_one
-    grad_input = (
-        g_resid + inv_one * scaled - x * inv_one**3 * jnp.mean(scaled * x, axis=-1, keepdims=True)
-    )
-    gain_one_grad = jnp.sum(g_norm_one * x * inv_one, axis=0)
-    gains = lax.psum_scatter(
-        jnp.stack([gain_one_grad, gain_two_grad], axis=1),
-        ("dp", "tensor"), scatter_dimension=0, tiled=True,
-    )
-    grad_w = lax.psum_scatter(grad_w.astype(BF16), "dp", scatter_dimension=0, tiled=True)
-    wrows = grad_w.shape[0] // 4
-    grad_w = lax.all_to_all(
-        grad_w.reshape(4, wrows, 8 * HEAD), "tensor", split_axis=0, concat_axis=0, tiled=True
-    )
-    grad_w = grad_w.astype(F32).transpose(1, 0, 2)
-    query = grad_w[:, :, : 4 * HEAD].reshape(wrows, 16 * HEAD)
-    key = grad_w[:, :, 4 * HEAD : 6 * HEAD].reshape(wrows, 8 * HEAD)
-    value = grad_w[:, :, 6 * HEAD :].reshape(wrows, 8 * HEAD)
-    out = lax.psum_scatter(
-        grad_out.astype(BF16), ("dp", "tensor"), scatter_dimension=0, tiled=True
-    ).astype(F32)
-
-    def owners(a, dim):
-        return lax.psum_scatter(
-            a.astype(BF16), "dp", scatter_dimension=dim, tiled=True
-        ).astype(F32)
-
-    gate_sum = owners(dot("sd,sf->df", rows_all, g_gate), 0)
-    up_sum = owners(dot("sd,sf->df", rows_all, g_up), 0)
-    down_sum = owners(dot("sf,sd->fd", act, grad_all), 1)
-    return (
-        layer_out, grad_input, gains[:, 0], query, key, value, out, gains[:, 1],
-        gate_sum, up_sum, down_sum,
-    )
-
-
 def fast_shards(
     hidden_in, positions, gain_attn, w_query, key_matrix, value_matrix, w_output, gain_mlp,
     w_gate, w_up, w_down, cotangent,
@@ -862,7 +1354,26 @@
         hidden_in, cotangent, positions, gain_attn, gain_mlp, w_query, key_matrix, value_matrix,
         w_output,
     )
-    return rest_of_layer(hidden_in, gain_attn, o, w_gate, w_up, w_down)
+    f = feed_forward(o, w_gate, w_up, w_down)
+    b = back(o, f, hidden_in, o["tables"])
+    wrows = w_query.shape[0]
+    parts = b["wqkv"].transpose(1, 0, 2)
+    query = parts[:, :, : 4 * HEAD].reshape(wrows, 16 * HEAD)
+    key = parts[:, :, 4 * HEAD : 6 * HEAD].reshape(wrows, 8 * HEAD)
+    value = parts[:, :, 6 * HEAD :].reshape(wrows, 8 * HEAD)
+
+    def rows_of(w, g):
+        return jnp.sum(w.astype(F32) * g, axis=1)
+
+    gain_one = (
+        rows_of(w_query, query) + rows_of(key_matrix, key) + rows_of(value_matrix, value)
+    ) / gain_attn.astype(F32)
+    mine = lax.axis_index("dp") * lax.axis_size("tensor") + lax.axis_index("tensor")
+    gain_two = lax.dynamic_slice_in_dim(b["gain"][0], mine * wrows, wrows, 0)
+    return (
+        b["layer"], b["gin"], gain_one, query, key, value, b["wo"], gain_two,
+        b["mlp"][0], b["mlp"][1], b["mlp"][2].T,
+    )
 
 
 def solution(mesh):

time: 722 us -> 291 us (0.40)
  waiting for transfers between devices: 514 us -> 0 us
  Pallas kernels: 88.4 us -> 271 us
  matrix products: 57.6 us -> 0 us
  other arithmetic: 19.4 us -> 5.59 us
  between operations: 14.6 us -> 0.79 us
  starting transfers between devices: 8.88 us -> 0 us
    reduce_scatter x8 -> x0, waiting for transfers between devices: 364 us -> none  [the longest x3 137 us: owners(): lax.psum_scatter(a.astype(BF16), 'dp', scatter_dimension=dim, tiled=True)]
    pallas_call x0 -> x2, Pallas kernels: none -> 183 us  [the longest x1 106 us: back(): pl.pallas_call(back_kernel, out_shape=[jax.ShapeDtypeStruct(*v) for v in...]
    unnamed x11 -> x0, waiting for transfers between devices: 95.8 us -> none
    dot_general x18 -> x0, matrix products: 57.6 us -> none  [dot(): return jnp.einsum(spec, a, b, preferred_element_type=F32)]
    all_gather x1 -> x0, waiting for transfers between devices: 47.7 us -> none  [rest_of_layer(): rows_all = lax.all_gather(normed_two, 'tensor', axis=0, tiled=True)]
    convert_element_type x7 -> x1, other arithmetic: 8.8 us -> 0.66 us  [front(): gain_attn.astype(F32)]
    all_to_all x2 -> x0, starting transfers between devices: 8.06 us -> none  [the longest x1 4.6 us: rest_of_layer(): lax.all_to_all(grad_w.reshape(4, wrows, 8 * HEAD), 'tensor', split_axis=0...]
  transfers between devices with their start and end apart: 12 -> 0, of which waited for: 11 -> 0; matrix products, arithmetic and copies ran while one was open for 7% -> 0% of each run, Pallas kernels for 0% -> 0%
where the time goes in v3:
time: 291 us; the launch traced here: 290 us
  Pallas kernels  271 us (93%)
  local copies, waits for them, and re-layouts  12.2 us (4%)
  other arithmetic  5.59 us (2%)
    pallas_call x1, Pallas kernels, back(): pl.pallas_call(back_kernel, out_shape=[jax.ShapeDtypeStruct(*v) for v in...  106 us
    pallas_call x1, Pallas kernels, front(): pl.pallas_call(front_kernel, out_shape=[sds(*v) for v in shapes.values()]...  88.4 us
    pallas_call x1, Pallas kernels, feed_forward(): pl.pallas_call(feed_forward_kernel, out_shape=[jax.ShapeDtypeStruct(*v) f...  76.7 us

profile of v3, /device:TPU:4, one launch (start us, length us, event | category | flops | bytes accessed | tf_op | source)
XLA Modules:
  0.0 289.6 jit_solution(16530966243938589815)
XLA Ops:
  0.7 0.7 convert_bitcast_fusion
  1.3 0.7 bitcast_convert_fusion
  2.0 0.7 convert_element_type.20
  2.6 0.6 stack.23.tile
  3.2 1.0 reshape.42
  4.3 1.0 reshape.43
  5.3 0.9 copy.37
  6.3 0.8 pad_maximum_fusion.wpack
  7.1 88.4 %front.1 = (bf16[512,1536]{1,0:T(8,128)(2,1)}, bf16[1536,768]{1,0:T(8,128)(2,1)}, bf16[1536,1536]{1,0:T(8,128)(2,1)}, bf16[8,512,128]{2,1,0:T(8,128)(2,1)}, f32[...) custom-call(bf16[128,1536]{1,0:T(8,128)(2,1)} %hid.3, ...), custom_call_target="tpu_custom_call" | custom-call | tf_op jit(solution)/shard_map/front/pallas_call | solution.py:440
  95.5 76.7 %feed_forward.1 = (bf16[4,128,1536]{2,1,0:T(8,128)(2,1)}, bf16[4,128,384]{2,1,0:T(8,128)(2,1)}, f32[128,1536]{1,0:T(8,128)}, bf16[128,1536]{1,0:T(8,128)(2,1)}, ...) custom-call(bf16[128,1536]{1,0:T(8,128)(2,1)} %get-tuple-element.34.nrm, ...), custom_call_target="tpu_custom_call" | custom-call | tf_op jit(solution)/shard_map/feed_forward/pallas_call | solution.py:631
  172.3 105.9 %back.1 = (bf16[128,1536]{1,0:T(8,128)(2,1)}, f32[128,1536]{1,0:T(8,128)}, f32[1,1536]{1,0:T(1,128)}, f32[4,48,768]{2,1,0:T(8,128)}, f32[48,1536]{1,0:T(8,128)}, /*index=5*/f32[3,192,1024]{2,1,0:T(8,128)}) custom-call(bf16[4,128,384]{2,1,0:T(8,128)(2,1)} %get-tuple-element.39.gatt, bf16[4,128,1536]{2,1,0:T(8,128)(2,1)} %get-tuple-element.40.mlp, ...), custom_call_target="tpu_custom_call" | custom-call | tf_op jit(solution)/shard_map/back/pallas_call | solution.py:1035
  278.2 1.4 dynamic-slice_bitcast_fusion
  279.6 1.0 slice_bitcast_fusion.3
  280.6 1.1 fusion
  281.9 0.8 reshape.45
  282.7 0.1 multiply_reduce_fusion
  282.8 1.1 multiply_reduce_fusion.2
  284.1 0.1 reshape.46
  284.2 1.1 multiply_reduce_fusion.1
  285.3 0.5 add_divide_fusion
  285.8 1.4 slice_bitcast_fusion
  287.3 0.7 copy.41
  288.0 0.9 copy.42
  288.9 0.7 copy.43
  (23 shorter events, 0.4 us)
Async XLA Ops:
  278.1 4.6 %copy-start.3 = (bf16[48,1536]{1,0:T(8,128)(2,1)S(1)}, bf16[48,1536]{1,0:T(8,128)(2,1)}, u32[]{:S(2)}) copy-start(bf16[48,1536]{1,0:T(8,128)(2,1)} %param.18) | copy-start | bytes 442372
  278.2 7.1 %copy-start.7 = (bf16[48]{0:T(256)(128)(2,1)S(1)}, bf16[48]{0:T(256)(128)(2,1)}, u32[]{:S(2)}) copy-start(bf16[48]{0:T(256)(128)(2,1)} %param.17) | copy-start | bytes 292
  278.2 7.6 %copy-start = (f32[3,192,1024]{2,1,0:T(8,128)S(1)}, f32[3,192,1024]{2,1,0:T(8,128)}, u32[]{:S(2)}) copy-start(f32[3,192,1024]{2,1,0:T(8,128)} %get-tuple-element.56) | copy-start | bytes 7077892
  282.7 4.6 %copy-start.1 = (f32[4,6,8,384]{3,2,0,1:T(8,128)}, f32[4,6,8,384]{3,2,0,1:T(8,128)S(1)}, u32[]{:S(2)}) copy-start(f32[4,6,8,384]{3,2,0,1:T(8,128)S(1)} %copy.33) | copy-start | bytes 884740
  284.2 3.1 %copy-start.4 = (f32[48,768]{1,0:T(8,128)}, f32[48,768]{1,0:T(8,128)S(1)}, u32[]{:S(2)}) copy-start(f32[48,768]{1,0:T(8,128)S(1)} %reshape.46) | copy-start | bytes 442372
  285.8 1.5 copy-start.5
  285.8 2.2 copy-start.2
  287.3 1.6 copy-start.6

commit v4 on v1

--- a/solution.py
+++ b/solution.py
@@ -1,18 +1,939 @@
+import functools
 import math
 
 import jax
 import jax.numpy as jnp
+import numpy as np
 from jax import lax
+from jax.experimental import pallas as pl
+from jax.experimental.pallas import tpu as pltpu
 from jax.sharding import PartitionSpec as P
+
+F32 = jnp.float32
+BF16 = jnp.bfloat16
+MESH = pl.DeviceIdType.MESH
+EPSILON = 1e-05
+ROPE_BASE = 100000.0
+MASKED = -1e30
+HEAD = 96
+VMEM_LIMIT = 64 * 2**20 - 65536
+
+
+def rotary_tables(rows, shards_in_sequence):
+    half = HEAD // 2
+    lanes = np.arange(4 * HEAD) % half
+    rates = ROPE_BASE ** (-(lanes * 2.0) / HEAD)
+    near = np.arange(rows)[:, None] * rates[None, :]
+    far = (np.arange(shards_in_sequence) * rows)[:, None] * rates[None, :]
+    shift = np.concatenate([np.cos(far), np.sin(far)], axis=0)
+    return (
+        np.cos(near).astype(np.float32),
+        np.sin(near).astype(np.float32),
+        shift.astype(np.float32),
+    )
+
+
+def tensor_peer(t, m):
+    if m == 1:
+        return t + 1 - 2 * lax.rem(t, 2)
+    if m == 2:
+        return lax.rem(t + 2, 4)
+    return 3 - t
+
+
+def dp_peer(d, m):
+    if m & 1:
+        d = d + 1 - 2 * lax.rem(d, 2)
+    if m & 2:
+        d = d + 2 - 4 * lax.rem(lax.div(d, 2), 2)
+    if m & 4:
+        d = lax.rem(d + 4, 8)
+    return d
+
+
+class Links:
+    def __init__(self, tsend, trecv, dsend, drecv):
+        self.t = lax.axis_index("tensor")
+        self.d = lax.axis_index("dp")
+        self.mid = lax.rem(lax.div(self.t + 1, 2), 2)
+        self.tsend, self.trecv, self.dsend, self.drecv = tsend, trecv, dsend, drecv
+
+    def shard_at(self, i):
+        t, mid = self.t, self.mid
+        near, two, three = (tensor_peer(t, m) for m in (1, 2, 3))
+        if isinstance(i, int):
+            if i == 0:
+                return t, 0
+            if i == 1:
+                return near, 1
+            if i == 2:
+                return two + mid * (three - two), 2 + mid
+            return three + mid * (two - three), 3 - mid
+        one_if = [1 - jnp.minimum(jnp.abs(i - k), 1) for k in range(4)]
+        pairs = [self.shard_at(k) for k in range(4)]
+        return (
+            sum(f * p[0] for f, p in zip(one_if, pairs)),
+            sum(f * p[1] for f, p in zip(one_if, pairs)),
+        )
+
+    def over_tensor(self, kind, m, src, dst, recv=None):
+        peer = tensor_peer(self.t, m)
+        return pltpu.make_async_remote_copy(
+            src_ref=src,
+            dst_ref=dst,
+            send_sem=self.tsend.at[kind, m],
+            recv_sem=self.trecv.at[kind, m if recv is None else recv],
+            device_id={"dp": self.d, "tensor": peer},
+            device_id_type=MESH,
+        )
+
+    def over_dp(self, kind, m, src, dst, to=None):
+        peer = dp_peer(self.d, m if to is None else to)
+        return pltpu.make_async_remote_copy(
+            src_ref=src,
+            dst_ref=dst,
+            send_sem=self.dsend.at[kind, m],
+            recv_sem=self.drecv.at[kind, m],
+            device_id={"dp": peer, "tensor": self.t},
+            device_id_type=MESH,
+        )
+
+    def landed_tensor(self, kind, m, ref):
+        pltpu.make_async_copy(ref, ref, self.trecv.at[kind, m]).wait()
+
+    def landed_dp(self, kind, m, ref):
+        pltpu.make_async_copy(ref, ref, self.drecv.at[kind, m]).wait()
+
+    def gather_start(self, kind, src, at):
+        own = at(self.t)
+        self.over_tensor(kind, 1, src, own).start()
+
+        @pl.when(self.mid == 0)
+        def _():
+            self.over_tensor(kind, 2, src, own).start()
+
+        @pl.when(self.mid == 1)
+        def _():
+            self.over_tensor(kind, 3, src, own).start()
+
+    def gather_take(self, kind, i, at):
+        shard, m = self.shard_at(i)
+        block = at(shard)
+        self.landed_tensor(kind, m, block)
+
+        def hand_on():
+            pltpu.make_async_remote_copy(
+                src_ref=block,
+                dst_ref=block,
+                send_sem=self.tsend.at[kind, 2 + i],
+                recv_sem=self.trecv.at[kind, 5 - m],
+                device_id={"dp": self.d, "tensor": tensor_peer(self.t, 1)},
+                device_id_type=MESH,
+            ).start()
+
+        if isinstance(i, int):
+            if i >= 2:
+                pl.when(self.mid == 1)(hand_on)
+        else:
+            pl.when((self.mid == 1) & (i >= 2))(hand_on)
+
+    def gather_end(self, kind, src, at):
+        own = at(self.t)
+        self.over_tensor(kind, 1, src, own).wait_send()
+
+        @pl.when(self.mid == 0)
+        def _():
+            self.over_tensor(kind, 2, src, own).wait_send()
+
+        @pl.when(self.mid == 1)
+        def _():
+            self.over_tensor(kind, 3, src, own).wait_send()
+            for i in (2, 3):
+                shard, m = self.shard_at(i)
+                pltpu.make_async_copy(at(shard), at(shard), self.tsend.at[kind, 2 + i]).wait()
+
+    def barrier(self, tensor_peers, dp_peers):
+        sem = pltpu.get_barrier_semaphore()
+        for m in tensor_peers:
+            pl.semaphore_signal(
+                sem,
+                inc=1,
+                device_id={"dp": self.d, "tensor": tensor_peer(self.t, m)},
+                device_id_type=MESH,
+            )
+        for m in dp_peers:
+            pl.semaphore_signal(
+                sem,
+                inc=1,
+                device_id={"dp": dp_peer(self.d, m), "tensor": self.t},
+                device_id_type=MESH,
+            )
+        pl.semaphore_wait(sem, len(tensor_peers) + len(dp_peers))
+
+
+def mm(a, b, dims=((1,), (0,))):
+    return lax.dot_general(a, b, (dims, ((), ())), preferred_element_type=F32)
+
+
+NN = ((1,), (0,))
+NT = ((1,), (1,))
+TN = ((0,), (0,))
+
+
+def lane_roll(u, by):
+    return pltpu.roll(u, by % u.shape[-1], u.ndim - 1)
+
+
+def swap_halves(u):
+    lane = lax.broadcasted_iota(jnp.int32, u.shape, 1)
+    low = lax.rem(lane, HEAD) < HEAD // 2
+    return jnp.where(low, -lane_roll(u, -(HEAD // 2)), lane_roll(u, HEAD // 2))
+
+
+def turn_tables(near_cos, near_sin, shift, shard):
+    c = shift[pl.ds(shard, 1), :]
+    s = shift[pl.ds(shard + 4, 1), :]
+    a, b = near_cos[...], near_sin[...]
+    return a * c - b * s, b * c + a * s
+
+
+class LineSum:
+    def __init__(self, ln, kind, src, recv):
+        self.ln, self.kind, self.src, self.recv = ln, kind, src, recv
+        t = ln.t
+        self.near, self.two, self.three = (tensor_peer(t, m) for m in (1, 2, 3))
+
+    def copy(self, src, to, slot, sem):
+        ln, kind = self.ln, self.kind
+        return pltpu.make_async_remote_copy(
+            src_ref=src,
+            dst_ref=self.recv.at[slot],
+            send_sem=ln.tsend.at[kind, sem],
+            recv_sem=ln.trecv.at[kind, slot],
+            device_id={"dp": ln.d, "tensor": to},
+            device_id_type=MESH,
+        )
+
+    def first(self, i, shard):
+        c = self.copy(self.src.at[shard], self.near, i, i)
+        if isinstance(i, int):
+            if i == 2:
+                c.start()
+            else:
+                pl.when(self.ln.mid == 0)(c.start)
+        else:
+            pl.when((i == 2) | ((self.ln.mid == 0) & (i < 2)))(c.start)
+
+    def start(self):
+        for i, shard in enumerate((self.three, self.two, self.near)):
+            self.first(i, shard)
+
+    def hand_on(self):
+        @pl.when(self.ln.mid == 1)
+        def _():
+            for i, shard in enumerate((self.two, self.three)):
+                self.ln.landed_tensor(self.kind, i, self.recv.at[i])
+                self.recv[i] = (
+                    self.recv[i].astype(F32) + self.src[shard].astype(F32)
+                ).astype(BF16)
+                self.copy(self.recv.at[i], shard, 3, i).start()
+
+    def take(self):
+        for i in (2, 3):
+            self.ln.landed_tensor(self.kind, i, self.recv.at[i])
+        return self.recv[2].astype(F32) + self.recv[3].astype(F32)
+
+    def end(self):
+        for i in range(3):
+            pltpu.make_async_copy(
+                self.src.at[0], self.src.at[0], self.ln.tsend.at[self.kind, i]
+            ).wait()
+
+
+class PlaneSum:
+    def __init__(self, ln, kind, src, recv):
+        self.ln, self.kind, self.src, self.recv = ln, kind, src, recv
+        j = lax.div(ln.d, 2)
+        self.j = j
+        self.x = j + 1 - 2 * lax.rem(j, 2)
+        self.y = lax.rem(j + 2, 4)
+        self.diag = lax.rem(self.x + 2, 4)
+        self.lanes = src.shape[-1] // 2
+
+    def half(self, ref, h):
+        spot = [slice(None)] * (len(ref.shape) - 1) + [pl.ds(h * self.lanes, self.lanes)]
+        return ref.at[tuple(spot)]
+
+    def copy(self, src, m, i):
+        return self.ln.over_dp(self.kind, i, src, self.recv.at[i], to=m)
+
+    def plan(self):
+        return (
+            (self.half(self.src.at[self.diag], 0), 2, 0),
+            (self.half(self.src.at[self.diag], 1), 4, 2),
+            (self.half(self.src.at[self.x], 0), 2, 1),
+            (self.half(self.src.at[self.y], 1), 4, 3),
+        )
+
+    def start(self):
+        for src, m, i in self.plan():
+            self.copy(src, m, i).start()
+
+    def hand_on(self):
+        for i, h, block, m in ((0, 0, self.y, 4), (2, 1, self.x, 2)):
+            self.ln.landed_dp(self.kind, i, self.recv.at[i])
+            self.recv[i] = (
+                self.recv[i].astype(F32) + self.half(self.src.at[block], h)[...].astype(F32)
+            ).astype(BF16)
+            self.copy_on(i, h, m).start()
+
+    def copy_on(self, i, h, m):
+        return self.ln.over_dp(self.kind, 4 + h, self.recv.at[i], self.recv.at[4 + h], to=m)
+
+    def take(self, h):
+        for i in (1 + 2 * h, 4 + h):
+            self.ln.landed_dp(self.kind, i, self.recv.at[i])
+        own = self.half(self.src.at[self.j], h)[...].astype(F32)
+        return own + self.recv[1 + 2 * h].astype(F32) + self.recv[4 + h].astype(F32)
+
+    def end(self):
+        for src, m, i in self.plan():
+            self.copy(src, m, i).wait_send()
+        for i, h, m in ((0, 0, 4), (2, 1, 2)):
+            self.copy_on(i, h, m).wait_send()
+
+
+class CoreSum:
+    def __init__(self, ln, kind, src, recv):
+        self.ln, self.kind, self.src, self.recv = ln, kind, src, recv
+        self.half = recv.shape[1]
+        self.core = lax.rem(ln.d, 2)
+
+    def side(self, which):
+        return pl.ds(pl.multiple_of(which * self.half, self.half), self.half)
+
+    def copy(self, j):
+        ln = self.ln
+        return pltpu.make_async_remote_copy(
+            src_ref=self.src.at[j, self.side(1 - self.core), :],
+            dst_ref=self.recv.at[j],
+            send_sem=ln.dsend.at[self.kind, j],
+            recv_sem=ln.drecv.at[self.kind, j],
+            device_id={"dp": dp_peer(ln.d, 1), "tensor": ln.t},
+            device_id_type=MESH,
+        )
+
+    def take(self):
+        def one(j, carry):
+            self.copy(j).wait_recv()
+            self.recv[j] = (
+                self.recv[j].astype(F32) + self.src[j, self.side(self.core), :].astype(F32)
+            ).astype(BF16)
+            return carry
+
+        lax.fori_loop(0, 4, one, 0)
+
+    def end(self):
+        def one(j, carry):
+            self.copy(j).wait_send()
+            return carry
+
+        lax.fori_loop(0, 4, one, 0)
+
+
+def layer_kernel(
+    hid, cot, tile, wpack, wo, wg, wu, wd, near_cos, near_sin, shift,
+    layer_out, gin_out, gain_out, wqkv_out, wo_out, mlpw_out,
+    xall, nall, call, w, wof, tiles, qh, kh, vh, att, arow, lse, start, gains, resid, normed2,
+    grecv, ff, msend, gatt, gres, low, gain,
+    gall, mlp_in, ff_in, wo_core, wo_in, wo_src, wo_line, wq_core, wq_in, wq_src, wq_all,
+    rows_in, line_in, gsum,
+    tsend, trecv, dsend, drecv, local, store,
+):
+    ln = Links(tsend, trecv, dsend, drecv)
+    t, d = ln.t, ln.d
+    rows, width = hid.shape
+    units = wg.shape[1]
+    seq = 4 * rows
+    span = width // 4
+    half = span // 2
+    core = lax.rem(d, 2)
+    wrows = wo.shape[0]
+    srows = 4 * wrows
+    TILE, W, X, O, C, A, N, G, GA, M, B, OL, WL, R = range(14)
+    DT, DW, FW, DO, FO, DF, DR, CO, DOS, CW, DWS, CK = range(12)
+    V = pltpu.VMEM
+
+    def ds_of(shard):
+        return pl.ds(pl.multiple_of(shard * rows, rows), rows)
+
+    def rows_at(ref, shard):
+        return ref.at[ds_of(shard), :]
+
+    def w_at(ref, dd, tt=None):
+        if tt is None:
+            return ref.at[pl.ds(pl.multiple_of(dd * srows, 16), srows), :]
+        return ref.at[pl.ds(pl.multiple_of(dd * srows + tt * wrows, 16), wrows), :]
+
+    x_of = functools.partial(rows_at, xall)
+    c_of = functools.partial(rows_at, call)
+
+    def wo_of(tt):
+        return w_at(wof, d, tt)
+
+    def columns(tt):
+        return arow.at[:, pl.ds(pl.multiple_of(tt * span, 128), span)]
+
+    at_own = ds_of(t)
+    scale = 1.0 / math.sqrt(HEAD)
+    layer_sum = LineSum(ln, M, msend, mlp_in)
+    ff_sum = PlaneSum(ln, DF, ff, ff_in)
+
+    def visible(shape, b):
+        key = lax.broadcasted_iota(jnp.int32, shape, 0)
+        query = lax.broadcasted_iota(jnp.int32, shape, 1) + b * rows
+        first = start[:, b * rows : (b + 1) * rows].astype(jnp.int32)
+        return (key <= query) & (key >= first)
+
+    def front(outh):
+        mine = [
+            pltpu.make_async_copy(a, b, local.at[i])
+            for i, (a, b) in enumerate(
+                [(tile, tiles.at[d, t]), (wpack.at[t], w_at(w, d, t)), (wo, wo_of(t)),
+                 (hid, x_of(t)), (cot, c_of(t))]
+            )
+        ]
+        for c in mine:
+            c.start()
+        ln.barrier((1, 2, 3), (1, 2, 3, 4, 5, 6, 7))
+        for m in (1, 2, 3):
+            ln.over_tensor(TILE, m, tile, tiles.at[d, t]).start()
+        for m in (1, 2, 3):
+            ln.over_tensor(W, m, wpack.at[tensor_peer(t, m)], w_at(w, d, t)).start()
+        ln.gather_start(O, wo, wo_of)
+        ln.gather_start(X, hid, x_of)
+        mine[0].wait()
+        for m in (1, 2, 3):
+            ln.landed_tensor(TILE, m, tiles.at[d, tensor_peer(t, m)])
+        for m in range(1, 8):
+            ln.over_dp(DT, m, tiles.at[d], tiles.at[d]).start()
+        mine[1].wait()
+        for m in (1, 2, 3):
+            ln.landed_tensor(W, m, w_at(w, d, tensor_peer(t, m)))
+        for m in (2, 4, 6, 1):
+            ln.over_dp(DW, m, w_at(w, d), w_at(w, d)).start()
+        mine[2].wait()
+        for i in (1, 2, 3):
+            ln.gather_take(O, i, wo_of)
+        for m in (2, 4, 6, 1):
+            ln.over_dp(DO, m, w_at(wof, d), w_at(wof, d)).start()
+        for m in range(1, 8):
+            ln.landed_dp(DT, m, tiles.at[dp_peer(d, m)])
+        for m in (2, 4, 6):
+            dd = dp_peer(d, m)
+            ln.landed_dp(DW, m, w_at(w, dd))
+            ln.over_dp(FW, m, w_at(w, dd), w_at(w, dd), to=1).start()
+        for g in range(4):
+            acc = jnp.zeros((8, 8 * wrows), F32)
+            for j in range(8):
+                r = 8 * g + j
+                piece = jnp.concatenate(
+                    [tiles[r // 4, r % 4], jnp.zeros((8, 8 * wrows - 128), F32)], axis=1
+                )
+                acc = acc + lane_roll(piece, wrows * j)
+            gains[:, g * 8 * wrows : (g + 1) * 8 * wrows] = acc
+        for s in range(4):
+            start[:, s * rows : (s + 1) * rows] = tiles[d, s, 2:3, :]
+        mine[3].wait()
+        for i in (1, 2, 3):
+            ln.gather_take(X, i, x_of)
+        mine[4].wait()
+        ln.gather_start(C, cot, c_of)
+        ln.landed_dp(DW, 1, w_at(w, dp_peer(d, 1)))
+        for m in (2, 4, 6):
+            ln.landed_dp(FW, m, w_at(w, dp_peer(d, m ^ 1)))
+
+        def project(s, carry):
+            at = ds_of(s)
+            x = xall[at, :].astype(F32)
+            inv = lax.rsqrt(jnp.mean(x * x, axis=1, keepdims=True) + EPSILON)
+            normed = (x * inv * gains[0:1, :]).astype(BF16)
+            nall[at, :] = normed
+            cosine, sine = turn_tables(near_cos, near_sin, shift, s)
+            q = mm(normed, w[:, : 4 * HEAD])
+            q = q * cosine + swap_halves(q) * sine
+            kv = mm(normed, w[:, 4 * HEAD :])
+            lane = lax.broadcasted_iota(jnp.int32, kv.shape, 1)
+            kv = jnp.where(lane < 2 * HEAD, kv * cosine + swap_halves(kv) * sine, kv)
+            keep = lax.broadcasted_iota(jnp.int32, (rows, 128), 1) < HEAD
+
+            def head(u, h):
+                return jnp.where(keep, lane_roll(u, -HEAD * h)[:, :128], 0.0).astype(BF16)
+
+            for h in range(4):
+                qh[h, at, :] = head(q, h)
+            for c in range(2):
+                kh[c, at, :] = head(kv, c)
+                vh[c, at, :] = head(kv, c + 2)
+            return carry
+
+        lax.fori_loop(0, 4, project, 0)
+
+        def attend(h, carry):
+            @pl.when((h == 1) | (h == 3))
+            def _():
+                ln.gather_take(C, lax.div(h + 1, 2), c_of)
+
+            c = lax.div(h, 2)
+            for b in range(4):
+                far = (b + 1) * rows
+                here = slice(b * rows, far)
+                sc = mm(kh[c, :far, :], qh[h, here, :], NT) * scale
+                sc = jnp.where(visible(sc.shape, b), sc, MASKED)
+                peak = jnp.max(sc, axis=0, keepdims=True)
+                e = jnp.exp(sc - peak)
+                total = jnp.sum(e, axis=0, keepdims=True)
+                p = (e * (1.0 / total)).astype(BF16)
+                outh[h, here, :] = mm(p, vh[c, :far, :], TN)
+                lse[h, :, here] = peak + jnp.log(total)
+            return carry
+
+        lax.fori_loop(0, 4, attend, 0)
+
+        def pack(b, carry):
+            acc = jnp.zeros((rows, 4 * HEAD), F32)
+            for h in range(4):
+                piece = jnp.concatenate(
+                    [outh[h, ds_of(b), :], jnp.zeros((rows, 4 * HEAD - 128), F32)], axis=1
+                )
+                acc = acc + lane_roll(piece, HEAD * h)
+            att[b] = acc.astype(BF16)
+            return carry
+
+        lax.fori_loop(0, 4, pack, 0)
+        ln.gather_end(X, hid, x_of)
+        for m in (3, 2, 1):
+            ln.over_tensor(A, m, att.at[tensor_peer(t, m)], columns(t)).start()
+        own = pltpu.make_async_copy(att.at[t], columns(t), local.at[0])
+        own.start()
+        ln.gather_take(C, 3, c_of)
+        for m in (2, 4, 6):
+            dd = dp_peer(d, m)
+            ln.landed_dp(DO, m, w_at(wof, dd))
+            ln.over_dp(FO, m, w_at(wof, dd), w_at(wof, dd), to=1).start()
+        ln.landed_dp(DO, 1, w_at(wof, dp_peer(d, 1)))
+        for m in (2, 4, 6):
+            ln.landed_dp(FO, m, w_at(wof, dp_peer(d, m ^ 1)))
+        own.wait()
+        for m in (1, 2, 3):
+            ln.landed_tensor(A, m, columns(tensor_peer(t, m)))
+        third = width // 3
+
+        def project_out(n, carry):
+            cols = pl.ds(pl.multiple_of(n * third, 128), third)
+            resid[:, cols] = xall[at_own, cols].astype(F32) + mm(arow[...], wof[:, cols])
+            return carry
+
+        lax.fori_loop(0, 3, project_out, 0)
+        r = resid[...]
+        inv = lax.rsqrt(jnp.mean(r * r, axis=1, keepdims=True) + EPSILON)
+        normed2[...] = (r * inv * gains[1:2, :]).astype(BF16)
+        ln.gather_start(N, normed2, x_of)
+        xall[at_own, :] = normed2[...]
+
+    def feed(loads, gate_w, up_w, down_w, act, gg, gu, gsend, gown, part):
+        for c in loads:
+            c.wait()
+
+        def to_owner(shard, m):
+            return pltpu.make_async_remote_copy(
+                src_ref=gsend.at[shard],
+                dst_ref=grecv.at[m - 1],
+                send_sem=tsend.at[G, m],
+                recv_sem=trecv.at[G, m],
+                device_id={"dp": d, "tensor": shard},
+                device_id_type=MESH,
+            )
+
+        def one_shard(i, carry):
+            shard, m = ln.shard_at(i)
+
+            @pl.when(i > 0)
+            def _():
+                ln.gather_take(N, i, x_of)
+
+            at = ds_of(shard)
+            r = xall[at, :]
+            gate = mm(r, gate_w[...])
+            up = mm(r, up_w[...])
+            sig = 1.0 / (1.0 + jnp.exp(-gate))
+            silu = gate * sig
+            act[at, :] = (silu * up).astype(BF16)
+            g_act = mm(call[at, :], down_w[...], NT)
+            gg[at, :] = (g_act * up * sig * (1.0 + gate * (1.0 - sig))).astype(BF16)
+            gu[at, :] = (g_act * silu).astype(BF16)
+            g = mm(gg[at, :], gate_w[...], NT) + mm(gu[at, :], up_w[...], NT)
+
+            @pl.when(i == 0)
+            def _():
+                gown[...] = g
+
+            @pl.when(i > 0)
+            def _():
+                gsend[shard] = g.astype(BF16)
+                to_owner(shard, m).start()
+
+            msend[shard] = mm(act[at, :], down_w[...]).astype(BF16)
+            return carry
+
+        lax.fori_loop(0, 4, one_shard, 0)
+        layer_sum.first(0, layer_sum.three)
+        layer_sum.first(1, layer_sum.two)
+
+        def side(which):
+            return pl.ds(pl.multiple_of(which * half, half), half)
+
+        def to_core(k, j):
+            return pltpu.make_async_remote_copy(
+                src_ref=part.at[lax.rem(j, 2), k, side(1 - core), :],
+                dst_ref=ff.at[j, k],
+                send_sem=dsend.at[CK + k, j],
+                recv_sem=drecv.at[CK + k, j],
+                device_id={"dp": dp_peer(d, 1), "tensor": t},
+                device_id_type=MESH,
+            )
+
+        def chip_sum(j):
+            for k in range(3):
+                to_core(k, j).wait_recv()
+                ff[j, k] = (
+                    part[lax.rem(j, 2), k, side(core), :].astype(F32) + ff[j, k].astype(F32)
+                ).astype(BF16)
+                to_core(k, j).wait_send()
+
+        def weights(j, carry):
+            cols = pl.ds(pl.multiple_of(j * span, 128), span)
+            for k, (a, b) in enumerate(((xall, gg), (xall, gu), (call, act))):
+                part[lax.rem(j, 2), k] = mm(a[:, cols], b[...], TN).astype(BF16)
+                to_core(k, j).start()
+
+            @pl.when(j > 0)
+            def _():
+                chip_sum(j - 1)
+
+            return carry
+
+        lax.fori_loop(0, 4, weights, 0)
+        chip_sum(3)
+        ff_sum.start()
+        for m in (1, 2, 3):
+            ln.landed_tensor(G, m, grecv.at[m - 1])
+        g = gown[...]
+        for m in (1, 2, 3):
+            g = g + grecv[m - 1].astype(F32)
+        r = resid[...]
+        inv = lax.rsqrt(jnp.mean(r * r, axis=1, keepdims=True) + EPSILON)
+        gain[0] = jnp.sum(g * r * inv, axis=0, keepdims=True)
+        scaled = g * gains[1:2, :]
+        gr = (
+            call[at_own, :].astype(F32)
+            + inv * scaled
+            - r * (inv * inv * inv) * jnp.mean(scaled * r, axis=1, keepdims=True)
+        )
+        gres[...] = gr
+        low[...] = gr.astype(BF16)
+        for s in range(4):
+            gatt[s] = mm(low[...], wof[s * span : (s + 1) * span, :], NT).astype(BF16)
+        for m in (1, 2, 3):
+            to_owner(tensor_peer(t, m), m).wait_send()
+
+    def forward(gate_w, up_w, down_w):
+        loads = [
+            pltpu.make_async_copy(a, b, local.at[5 + i])
+            for i, (a, b) in enumerate(((wg, gate_w), (wu, up_w), (wd, down_w)))
+        ]
+        for c in loads:
+            c.start()
+        pl.run_scoped(front, V((4, seq, 128), F32))
+        hidden = V((seq, units), BF16)
+        pl.run_scoped(
+            functools.partial(feed, loads, gate_w, up_w, down_w),
+            hidden, hidden, hidden, V((4, rows, width), BF16), V((rows, width), F32),
+            V((2, 3, span, units), BF16),
+        )
+
+    pl.run_scoped(
+        forward, V((width, units), BF16), V((width, units), BF16), V((units, width), BF16)
+    )
+
+    def backward(gh, gq, gk, gv, gqkv, gn_src, wo_part, wq_part, layer, gin, wqkv, wo_full, ffw):
+        for m in (3, 2, 1):
+            ln.over_tensor(GA, m, gatt.at[tensor_peer(t, m)], rows_at(gall, t)).start()
+        own = [
+            pltpu.make_async_copy(gatt.at[t], rows_at(gall, t), local.at[0]),
+            pltpu.make_async_copy(gain, rows_in.at[pl.ds(d, 1)], local.at[1]),
+        ]
+        for c in own:
+            c.start()
+        for m in range(1, 8):
+            ln.over_dp(DR, m, gain.at[0], rows_in.at[d]).start()
+        layer_sum.first(2, layer_sum.near)
+        wo_pair = CoreSum(ln, CO, wo_part, wo_core)
+
+        def output_weights(j, carry):
+            cols = pl.ds(pl.multiple_of(j * span, 128), span)
+            wo_part[j] = mm(arow[:, cols], low[...], TN).astype(BF16)
+            wo_pair.copy(j).start()
+            return carry
+
+        lax.fori_loop(0, 4, output_weights, 0)
+        layer_sum.hand_on()
+        own[0].wait()
+        for m in (1, 2, 3):
+            ln.landed_tensor(GA, m, rows_at(gall, tensor_peer(t, m)))
+        keep = lax.broadcasted_iota(jnp.int32, (rows, 128), 1) < HEAD
+
+        def split(b, carry):
+            u = gall[ds_of(b), :].astype(F32)
+            for h in range(4):
+                gh[h, ds_of(b), :] = jnp.where(
+                    keep, lane_roll(u, -HEAD * h)[:, :128], 0.0
+                ).astype(BF16)
+            return carry
+
+        lax.fori_loop(0, 4, split, 0)
+        gk[...] = jnp.zeros_like(gk)
+        gv[...] = jnp.zeros_like(gv)
+        wo_pair.take()
+        wo_sum = PlaneSum(ln, DOS, wo_core, wo_in)
+        wo_sum.start()
+
+        def attend_back(h, carry):
+            c = lax.div(h, 2)
+            for b in range(4):
+                far = (b + 1) * rows
+                here = slice(b * rows, far)
+                k, v, q, g = kh[c, :far, :], vh[c, :far, :], qh[h, here, :], gh[h, here, :]
+                sc = mm(k, q, NT) * scale
+                sc = jnp.where(visible(sc.shape, b), sc, MASKED)
+                p = jnp.exp(sc - lse[h, :, here])
+                gp = mm(v, g, NT)
+                gs = (p * (gp - jnp.sum(p * gp, axis=0, keepdims=True))).astype(BF16)
+                gq[h, here, :] = mm(gs, k, TN) * scale
+                gk[c, :far, :] += mm(gs, q) * scale
+                gv[c, :far, :] += mm(p.astype(BF16), g)
+            return carry
+
+        lax.fori_loop(0, 4, attend_back, 0)
+
+        def gather_heads(b, carry):
+            at = ds_of(b)
+            cosine, sine = turn_tables(near_cos, near_sin, shift, b)
+            cosine, sine = cosine[:, :128], sine[:, :128]
+
+            def placed(u, h):
+                u = jnp.concatenate(
+                    [jnp.where(keep, u, 0.0), jnp.zeros((rows, 4 * HEAD - 128), F32)], axis=1
+                )
+                return lane_roll(u, HEAD * h)
+
+            def turned(u):
+                return u * cosine - swap_halves(u) * sine
+
+            left = sum(placed(turned(gq[h, at, :]), h) for h in range(4))
+            right = sum(placed(turned(gk[c, at, :]), c) for c in range(2))
+            right = right + sum(placed(gv[c, at, :], c + 2) for c in range(2))
+            gqkv[at, : 4 * HEAD] = left.astype(BF16)
+            gqkv[at, 4 * HEAD :] = right.astype(BF16)
+            return carry
+
+        lax.fori_loop(0, 4, gather_heads, 0)
+        gn_sum = LineSum(ln, B, gn_src, grecv)
+
+        def norm_grads(i, carry):
+            shard, _ = ln.shard_at(3 - i)
+            gn_src[shard] = mm(gqkv[ds_of(shard), :], w[...], NT).astype(BF16)
+            gn_sum.first(i, shard)
+            return carry
+
+        lax.fori_loop(0, 4, norm_grads, 0)
+        wq_pair = CoreSum(ln, CW, wq_part, wq_core)
+
+        def head_weights(j, carry):
+            cols = pl.ds(pl.multiple_of(j * span, 128), span)
+            wq_part[j] = mm(nall[:, cols], gqkv[...], TN).astype(BF16)
+            wq_pair.copy(j).start()
+            return carry
+
+        ff_sum.hand_on()
+        lax.fori_loop(0, 4, head_weights, 0)
+        wq_pair.take()
+        wq_sum = PlaneSum(ln, DWS, wq_core, wq_in)
+        wq_sum.start()
+        gn_sum.hand_on()
+        wo_sum.hand_on()
+
+        own[1].wait()
+        for m in range(1, 8):
+            ln.landed_dp(DR, m, rows_in.at[dp_peer(d, m)])
+        gsum[0] = sum(rows_in[i] for i in range(8))
+        for m in (1, 2, 3):
+            ln.over_tensor(R, m, gsum.at[0], line_in.at[m]).start()
+
+        stores = []
+
+        def out(a, b):
+            c = pltpu.make_async_copy(a, b, store.at[len(stores)])
+            c.start()
+            stores.append(c)
+
+        layer[...] = (resid[...] + msend[t].astype(F32) + layer_sum.take()).astype(BF16)
+        out(layer, layer_out)
+        lanes = ff_sum.lanes
+        for h in range(2):
+            ffw[:, :, h * lanes : (h + 1) * lanes] = ff_sum.take(h)
+        out(ffw, mlpw_out)
+        wq_sum.hand_on()
+        x = hid[...].astype(F32)
+        inv = lax.rsqrt(jnp.mean(x * x, axis=1, keepdims=True) + EPSILON)
+        scaled = (gn_src[t].astype(F32) + gn_sum.take()) * gains[0:1, :]
+        gin[...] = (
+            gres[...]
+            + inv * scaled
+            - x * (inv * inv * inv) * jnp.mean(scaled * x, axis=1, keepdims=True)
+        )
+        out(gin, gin_out)
+        lanes = wo_sum.lanes
+        for h in range(2):
+            u = wo_sum.take(h).astype(BF16)
+            for s in range(4):
+                wo_src[s, :, h * lanes : (h + 1) * lanes] = u[s * wrows : (s + 1) * wrows, :]
+        wo_line_sum = LineSum(ln, OL, wo_src, wo_line)
+        wo_line_sum.start()
+        total = gsum[0]
+        for m in (1, 2, 3):
+            ln.landed_tensor(R, m, line_in.at[m])
+            total = total + line_in[m]
+        line_in[0] = total
+        out(line_in.at[0], gain_out)
+        lanes = wq_sum.lanes
+        for h in range(2):
+            u = wq_sum.take(h).astype(BF16)
+            for s in range(4):
+                wq_src[s, :, h * lanes : (h + 1) * lanes] = u[s * wrows : (s + 1) * wrows, :]
+        for m in (3, 2, 1):
+            ln.over_tensor(WL, m, wq_src.at[tensor_peer(t, m)], wq_all.at[m]).start()
+        wqkv[pl.ds(t, 1)] = wq_src[pl.ds(t, 1)].astype(F32)
+        wo_line_sum.hand_on()
+        for m in (1, 2, 3):
+            ln.landed_tensor(WL, m, wq_all.at[m])
+            wqkv[pl.ds(tensor_peer(t, m), 1)] = wq_all[pl.ds(m, 1)].astype(F32)
+        out(wqkv, wqkv_out)
+        wo_full[...] = wo_src[t].astype(F32) + wo_line_sum.take()
+        out(wo_full, wo_out)
+
+        for m in (1, 2, 3):
+            ln.over_tensor(TILE, m, tile, tiles.at[d, t]).wait_send()
+            ln.over_tensor(W, m, wpack.at[tensor_peer(t, m)], w_at(w, d, t)).wait_send()
+            ln.over_tensor(A, m, att.at[tensor_peer(t, m)], columns(t)).wait_send()
+            ln.over_tensor(GA, m, gatt.at[tensor_peer(t, m)], rows_at(gall, t)).wait_send()
+            ln.over_tensor(R, m, gsum.at[0], line_in.at[m]).wait_send()
+            ln.over_tensor(WL, m, wq_src.at[tensor_peer(t, m)], wq_all.at[m]).wait_send()
+        ln.gather_end(O, wo, wo_of)
+        ln.gather_end(C, cot, c_of)
+        ln.gather_end(N, normed2, x_of)
+        for m in range(1, 8):
+            ln.over_dp(DT, m, tiles.at[d], tiles.at[d]).wait_send()
+            ln.over_dp(DR, m, gain.at[0], rows_in.at[d]).wait_send()
+        for m in (2, 4, 6, 1):
+            ln.over_dp(DW, m, w_at(w, d), w_at(w, d)).wait_send()
+            ln.over_dp(DO, m, w_at(wof, d), w_at(wof, d)).wait_send()
+        for m in (2, 4, 6):
+            dd = dp_peer(d, m)
+            ln.over_dp(FW, m, w_at(w, dd), w_at(w, dd), to=1).wait_send()
+            ln.over_dp(FO, m, w_at(wof, dd), w_at(wof, dd), to=1).wait_send()
+        for s in (layer_sum, gn_sum, wo_line_sum, ff_sum, wo_sum, wq_sum, wo_pair, wq_pair):
+            s.end()
+        for c in stores:
+            c.wait()
+
+    pl.run_scoped(
+        backward,
+        V((4, seq, 128), BF16), V((4, seq, 128), F32), V((2, seq, 128), F32),
+        V((2, seq, 128), F32), V((seq, 8 * HEAD), BF16), V((4, rows, width), BF16),
+        V((4, span, width), BF16), V((4, span, 8 * HEAD), BF16),
+        V((rows, width), BF16), V((rows, width), F32), V((4, wrows, 8 * HEAD), F32),
+        V((wrows, width), F32), V((3, half, units), F32),
+    )
+
+
+def layer(hid, cot, positions, gain_attn, gain_mlp, wq, wk, wv, wo, wg, wu, wd):
+    rows, width = hid.shape
+    wrows = wq.shape[0]
+    units = wg.shape[1]
+    seq = 4 * rows
+    span = width // 4
+    half = span // 2
+    t = lax.axis_index("tensor")
+    index = t * rows + jnp.arange(rows, dtype=jnp.int32)
+    pad = (0, 128 - wrows)
+    tile = jnp.stack(
+        [
+            jnp.pad(gain_attn.astype(F32), pad),
+            jnp.pad(gain_mlp.astype(F32), pad),
+            (index - positions).astype(F32),
+        ]
+        + [jnp.zeros((128,), F32)] * 5
+    )
+    wpack = jnp.concatenate(
+        [a.reshape(wrows, 4, a.shape[1] // 4).transpose(1, 0, 2) for a in (wq, wk, wv)], axis=2
+    )
+    near_cos, near_sin, shift = rotary_tables(rows, 4)
+    hbm = pl.BlockSpec(memory_space=pl.ANY)
+    vmem = pl.BlockSpec(memory_space=pltpu.VMEM)
+    V = pltpu.VMEM
+    shapes = dict(
+        layer=((rows, width), BF16), gin=((rows, width), F32), gain=((1, width), F32),
+        wqkv=((4, wrows, 8 * HEAD), F32), wo=((wrows, width), F32),
+        mlp=((3, half, units), F32),
+    )
+    wide = V((seq, width), BF16)
+    thin, thin_f = V((rows, width), BF16), V((rows, width), F32)
+    four = V((4, rows, width), BF16)
+    pair = V((2, seq, 128), BF16)
+    outs = pl.pallas_call(
+        layer_kernel,
+        out_shape=[jax.ShapeDtypeStruct(*v) for v in shapes.values()],
+        in_specs=[vmem] + [hbm] * 7 + [vmem] * 3,
+        out_specs=[hbm] * len(shapes),
+        scratch_shapes=[
+            wide, wide, wide, V((width, 8 * HEAD), BF16), V((width, width), BF16),
+            V((8, 4, 8, 128), F32), V((4, seq, 128), BF16), pair, pair,
+            V((4, rows, span), BF16), thin, V((4, 1, seq), F32), V((1, seq), F32),
+            V((8, width), F32), thin_f, thin,
+            four, V((4, 3, half, units), BF16), four, V((4, rows, span), BF16), thin_f, thin,
+            V((1, 1, width), F32),
+            V((seq, span), BF16), four, V((6, 3, half, units // 2), BF16),
+            V((4, half, width), BF16), V((6, half, width // 2), BF16),
+            V((4, wrows, width), BF16), V((4, wrows, width), BF16),
+            V((4, half, 8 * HEAD), BF16), V((6, half, 4 * HEAD), BF16),
+            V((4, wrows, 8 * HEAD), BF16), V((4, wrows, 8 * HEAD), BF16),
+            V((8, 1, width), F32), V((4, 1, width), F32), V((1, 1, width), F32),
+            pltpu.SemaphoreType.DMA((14, 6)), pltpu.SemaphoreType.DMA((14, 4)),
+            pltpu.SemaphoreType.DMA((14, 8)), pltpu.SemaphoreType.DMA((14, 8)),
+            pltpu.SemaphoreType.DMA((8,)), pltpu.SemaphoreType.DMA((6,)),
+        ],
+        name="layer",
+        compiler_params=pltpu.CompilerParams(
+            collective_id=0, has_side_effects=True, vmem_limit_bytes=VMEM_LIMIT
+        ),
+    )(hid, cot, tile, wpack, wo, wg, wu, wd, near_cos, near_sin, shift)
+    return dict(zip(shapes, outs))
+
 
 QUERY_HEADS = 16
 KEY_VALUE_HEADS = 8
 HEAD_DIMENSION = 96
-
-
-EPSILON = 1e-05
-ROPE_BASE = 100000.0
-MASKED = -1e30
 
 
 def angle_tables(pos_rows, head_size):
@@ -293,6 +1214,34 @@
     )
 
 
+def fast_shards(
+    hidden_in, positions, gain_attn, w_query, key_matrix, value_matrix, w_output, gain_mlp,
+    w_gate, w_up, w_down, cotangent,
+):
+    b = layer(
+        hidden_in, cotangent, positions, gain_attn, gain_mlp, w_query, key_matrix, value_matrix,
+        w_output, w_gate, w_up, w_down,
+    )
+    wrows = w_query.shape[0]
+    parts = b["wqkv"].transpose(1, 0, 2)
+    query = parts[:, :, : 4 * HEAD].reshape(wrows, 16 * HEAD)
+    key = parts[:, :, 4 * HEAD : 6 * HEAD].reshape(wrows, 8 * HEAD)
+    value = parts[:, :, 6 * HEAD :].reshape(wrows, 8 * HEAD)
+
+    def rows_of(w, g):
+        return jnp.sum(w.astype(F32) * g, axis=1)
+
+    gain_one = (
+        rows_of(w_query, query) + rows_of(key_matrix, key) + rows_of(value_matrix, value)
+    ) / gain_attn.astype(F32)
+    mine = lax.axis_index("dp") * lax.axis_size("tensor") + lax.axis_index("tensor")
+    gain_two = lax.dynamic_slice_in_dim(b["gain"][0], mine * wrows, wrows, 0)
+    return (
+        b["layer"], b["gin"], gain_one, query, key, value, b["wo"], gain_two,
+        b["mlp"][0], b["mlp"][1], b["mlp"][2].T,
+    )
+
+
 def solution(mesh):
     placed = (
         P(("dp", "tensor"), None),
@@ -308,8 +1257,9 @@
         P("tensor", None),
         P(("dp", "tensor"), None),
     )
+    fits = mesh.shape["dp"] == 8 and mesh.shape["tensor"] == 4
     return jax.shard_map(
-        shards,
+        fast_shards if fits else shards,
         mesh=mesh,
         in_specs=placed,
         out_specs=(

time: 883 us -> 277 us (0.31)
  waiting for transfers between devices: 468 us -> 0 us
  Pallas kernels: 0 us -> 254 us
  matrix products: 155 us -> 0 us
  blocking collectives: 123 us -> 0 us
  local copies, waits for them, and re-layouts: 80.7 us -> 15.5 us
  other arithmetic: 35.5 us -> 5.68 us
  between operations: 14.3 us -> 0.77 us
    pallas_call x0 -> x1, Pallas kernels: none -> 254 us  [layer(): pl.pallas_call(layer_kernel, out_shape=[jax.ShapeDtypeStruct(*v) for v in...]
    unnamed x17 -> x0, waiting for transfers between devices: 184 us -> none
    dot_general x77 -> x0, matrix products: 155 us -> none  [the longest x8 14.8 us: attend(): jnp.einsum('qk,kd->qd', probs.astype(jnp.bfloat16), v_block, preferred_el...]
    all_gather x6 -> x0, waiting for transfers between devices: 153 us -> none  [the longest x1 38.4 us: shards(): lax.all_gather(w_query, ('dp', 'tensor'), axis=0, tiled=True)]
    reduce_scatter x5 -> x0, waiting for transfers between devices: 130 us -> none  [the longest x1 47.5 us: shards(): lax.psum_scatter(grad_gate.astype(jnp.bfloat16), 'dp', scatter_dimension=...]
    unnamed x2 -> x0, blocking collectives: 82.6 us -> none
    unnamed x76 -> x22, local copies, waits for them, and re-layouts: 44.9 us -> 3.36 us
    all_gather x2 -> x0, blocking collectives: 40.7 us -> none  [the longest x1 21.3 us: shards(): lax.all_gather(value_rows_lowered, 'tensor', axis=0, tiled=True)]
  transfers between devices with their start and end apart: 14 -> 0, of which waited for: 12 -> 0; matrix products, arithmetic and copies ran while one was open for 19% -> 0% of each run, Pallas kernels for 0% -> 0%
where the time goes in v4:
time: 277 us; the launch traced here: 276 us
  Pallas kernels  254 us (92%)
  local copies, waits for them, and re-layouts  15.5 us (6%)
  other arithmetic  5.68 us (2%)
    pallas_call x1, Pallas kernels, layer(): pl.pallas_call(layer_kernel, out_shape=[jax.ShapeDtypeStruct(*v) for v in...  254 us

profile of v4, /device:TPU:4, one launch (start us, length us, event | category | flops | bytes accessed | tf_op | source)
XLA Modules:
  0.0 276.2 jit_solution(10402532957882808002)
XLA Ops:
  0.7 0.7 convert_bitcast_fusion
  1.3 0.7 bitcast_convert_fusion
  2.0 0.7 convert_element_type.20
  2.6 0.6 stack.23.tile
  3.2 1.0 reshape.42
  4.3 1.0 reshape.43
  5.3 0.9 copy.37
  6.3 0.8 pad_maximum_fusion.wpack
  7.1 254.2 %layer.1 = (bf16[128,1536]{1,0:T(8,128)(2,1)}, f32[128,1536]{1,0:T(8,128)}, f32[1,1536]{1,0:T(1,128)}, f32[4,48,768]{2,1,0:T(8,128)}, f32[48,1536]{1,0:T(8,128)}, /*index=5*/f32[3,192,1024]{2,1,0:T(8,128)}) custom-call(bf16[128,1536]{1,0:T(8,128)(2,1)} %hid.1, bf16[128,1536]{1,0:T(8,128)(2,1)} %cot.1, f32[8,128]{1,0:T(8,128)} %stack.23.tile, ...), custom_call_target="tpu_custom_call" | custom-call | tf_op jit(solution)/shard_map/layer/pallas_call | solution.py:904
  261.4 1.4 dynamic-slice_bitcast_fusion
  262.8 1.0 slice_bitcast_fusion.3
  263.8 1.8 fusion
  265.6 0.1 copy.30
  265.7 0.1 reshape.45
  265.9 1.2 multiply_reduce_fusion
  267.1 0.1 multiply_reduce_fusion.2
  267.2 1.8 copy.31
  269.0 1.7 reshape.46
  270.8 1.1 multiply_reduce_fusion.1
  271.9 0.5 add_divide_fusion
  272.4 1.4 slice_bitcast_fusion
  273.8 0.7 copy.41
  274.6 0.9 copy.42
  275.5 0.7 copy.43
  (23 shorter events, 0.1 us)
Async XLA Ops:
  261.3 5.8 %copy-start.6 = (bf16[48,768]{1,0:T(8,128)(2,1)S(1)}, bf16[48,768]{1,0:T(8,128)(2,1)}, u32[]{:S(2)}) copy-start(bf16[48,768]{1,0:T(8,128)(2,1)} %param.19) | copy-start | bytes 221188
  261.3 9.4 %copy-start.7 = (bf16[48,768]{1,0:T(8,128)(2,1)S(1)}, bf16[48,768]{1,0:T(8,128)(2,1)}, u32[]{:S(2)}) copy-start(bf16[48,768]{1,0:T(8,128)(2,1)} %param.20) | copy-start | bytes 221188
  261.3 10.5 %copy-start.8 = (bf16[48]{0:T(256)(128)(2,1)S(1)}, bf16[48]{0:T(256)(128)(2,1)}, u32[]{:S(2)}) copy-start(bf16[48]{0:T(256)(128)(2,1)} %param.17) | copy-start | bytes 292
  261.4 11.0 %copy-start = (f32[3,192,1024]{2,1,0:T(8,128)S(1)}, f32[3,192,1024]{2,1,0:T(8,128)}, u32[]{:S(2)}) copy-start(f32[3,192,1024]{2,1,0:T(8,128)} %get-tuple-element.22) | copy-start | bytes 7077892
  265.9 1.2 copy-start.3
  265.9 7.9 %copy-start.1 = (f32[4,6,8,384]{3,2,0,1:T(8,128)}, f32[4,6,8,384]{3,2,0,1:T(8,128)S(1)}, u32[]{:S(2)}) copy-start(f32[4,6,8,384]{3,2,0,1:T(8,128)S(1)} %copy.33) | copy-start | bytes 884740
  267.2 7.4 %copy-start.2 = (f32[128,1536]{1,0:T(8,128)S(1)}, f32[128,1536]{1,0:T(8,128)}, u32[]{:S(2)}) copy-start(f32[128,1536]{1,0:T(8,128)} %get-tuple-element.42) | copy-start | bytes 2359300
  270.8 3.1 %copy-start.4 = (bf16[128,1536]{1,0:T(8,128)(2,1)S(1)}, bf16[128,1536]{1,0:T(8,128)(2,1)}, u32[]{:S(2)}) copy-start(bf16[128,1536]{1,0:T(8,128)(2,1)} %get-tuple-element.41) | copy-start | bytes 1179652
  272.4 3.1 %copy-start.5 = (f32[48,1536]{1,0:T(8,128)S(1)}, f32[48,1536]{1,0:T(8,128)}, u32[]{:S(2)}) copy-start(f32[48,1536]{1,0:T(8,128)} %get-tuple-element.47) | copy-start | bytes 884740

commit v5 on v4

--- a/solution.py
+++ b/solution.py
@@ -342,12 +342,12 @@
 
 
 def layer_kernel(
-    hid, cot, tile, wpack, wo, wg, wu, wd, near_cos, near_sin, shift,
+    hid, cot, pos, gain_one, gain_two, wq, wk, wv, wo, wg, wu, wd, near_cos, near_sin, shift,
     layer_out, gin_out, gain_out, wqkv_out, wo_out, mlpw_out,
     xall, nall, call, w, wof, tiles, qh, kh, vh, att, arow, lse, start, gains, resid, normed2,
     grecv, ff, msend, gatt, gres, low, gain,
     gall, mlp_in, ff_in, wo_core, wo_in, wo_src, wo_line, wq_core, wq_in, wq_src, wq_all,
-    rows_in, line_in, gsum,
+    rows_in, line_in, gsum, tile, wpack, gown_row,
     tsend, trecv, dsend, drecv, local, store,
 ):
     ln = Links(tsend, trecv, dsend, drecv)
@@ -361,7 +361,7 @@
     wrows = wo.shape[0]
     srows = 4 * wrows
     TILE, W, X, O, C, A, N, G, GA, M, B, OL, WL, R = range(14)
-    DT, DW, FW, DO, FO, DF, DR, CO, DOS, CW, DWS, CK = range(12)
+    DT, DW, FW, DO, FO, DR, CO, DOS, CW, DWS, CK, DF = (*range(11), 13)
     V = pltpu.VMEM
 
     def ds_of(shard):
@@ -387,7 +387,9 @@
     at_own = ds_of(t)
     scale = 1.0 / math.sqrt(HEAD)
     layer_sum = LineSum(ln, M, msend, mlp_in)
-    ff_sum = PlaneSum(ln, DF, ff, ff_in)
+    ff_sums = [
+        PlaneSum(ln, DF + k, ff.at[:, k], ff_in.at[:, k]) for k in range(3)
+    ]
 
     def visible(shape, b):
         key = lax.broadcasted_iota(jnp.int32, shape, 0)
@@ -396,6 +398,21 @@
         return (key <= query) & (key >= first)
 
     def front(outh):
+        tile[...] = jnp.zeros_like(tile)
+        tile[0:1, :wrows] = gain_one[...].astype(F32)
+        tile[1:2, :wrows] = gain_two[...].astype(F32)
+        index = t * rows + lax.broadcasted_iota(jnp.int32, (1, rows), 1)
+        tile[2:3, :] = (index - pos[...]).astype(F32)
+        keys, values = wk[...].astype(F32), wv[...].astype(F32)
+        pair = 2 * HEAD
+        lane = lax.broadcasted_iota(jnp.int32, (wrows, span), 1)
+        for s in range(4):
+            wpack[s, :, :span] = wq[:, s * span : (s + 1) * span]
+            wpack[s, :, span:] = jnp.where(
+                lane < pair,
+                lane_roll(keys, -pair * s)[:, :span],
+                lane_roll(values, pair - pair * s)[:, :span],
+            ).astype(BF16)
         mine = [
             pltpu.make_async_copy(a, b, local.at[i])
             for i, (a, b) in enumerate(
@@ -480,10 +497,6 @@
         lax.fori_loop(0, 4, project, 0)
 
         def attend(h, carry):
-            @pl.when((h == 1) | (h == 3))
-            def _():
-                ln.gather_take(C, lax.div(h + 1, 2), c_of)
-
             c = lax.div(h, 2)
             for b in range(4):
                 far = (b + 1) * rows
@@ -516,7 +529,12 @@
             ln.over_tensor(A, m, att.at[tensor_peer(t, m)], columns(t)).start()
         own = pltpu.make_async_copy(att.at[t], columns(t), local.at[0])
         own.start()
-        ln.gather_take(C, 3, c_of)
+
+        @pl.when(ln.mid == 1)
+        def _():
+            for i in (1, 2, 3):
+                ln.gather_take(C, i, c_of)
+
         for m in (2, 4, 6):
             dd = dp_peer(d, m)
             ln.landed_dp(DO, m, w_at(wof, dd))
@@ -541,7 +559,7 @@
         ln.gather_start(N, normed2, x_of)
         xall[at_own, :] = normed2[...]
 
-    def feed(loads, gate_w, up_w, down_w, act, gg, gu, gsend, gown, part):
+    def feed(loads, gate_w, up_w, down_w, act, gg, gu, gsend, gown, part, gact):
         for c in loads:
             c.wait()
 
@@ -555,6 +573,20 @@
                 device_id_type=MESH,
             )
 
+        @pl.when(ln.mid == 0)
+        def _():
+            for i in (1, 2, 3):
+                ln.gather_take(C, i, c_of)
+
+        piece = units // 4
+
+        def act_grads(c, carry):
+            cols = pl.ds(pl.multiple_of(c * piece, 128), piece)
+            gact[:, cols] = mm(call[...], down_w[cols, :], NT)
+            return carry
+
+        lax.fori_loop(0, 4, act_grads, 0)
+
         def one_shard(i, carry):
             shard, m = ln.shard_at(i)
 
@@ -564,14 +596,16 @@
 
             at = ds_of(shard)
             r = xall[at, :]
-            gate = mm(r, gate_w[...])
-            up = mm(r, up_w[...])
-            sig = 1.0 / (1.0 + jnp.exp(-gate))
-            silu = gate * sig
-            act[at, :] = (silu * up).astype(BF16)
-            g_act = mm(call[at, :], down_w[...], NT)
-            gg[at, :] = (g_act * up * sig * (1.0 + gate * (1.0 - sig))).astype(BF16)
-            gu[at, :] = (g_act * silu).astype(BF16)
+            for c in range(4):
+                cols = slice(c * piece, (c + 1) * piece)
+                gate = mm(r, gate_w[:, cols])
+                up = mm(r, up_w[:, cols])
+                sig = 1.0 / (1.0 + jnp.exp(-gate))
+                silu = gate * sig
+                act[at, cols] = (silu * up).astype(BF16)
+                g_act = gact[at, cols]
+                gg[at, cols] = (g_act * up * sig * (1.0 + gate * (1.0 - sig))).astype(BF16)
+                gu[at, cols] = (g_act * silu).astype(BF16)
             g = mm(gg[at, :], gate_w[...], NT) + mm(gu[at, :], up_w[...], NT)
 
             @pl.when(i == 0)
@@ -583,19 +617,16 @@
                 gsend[shard] = g.astype(BF16)
                 to_owner(shard, m).start()
 
-            msend[shard] = mm(act[at, :], down_w[...]).astype(BF16)
             return carry
 
         lax.fori_loop(0, 4, one_shard, 0)
-        layer_sum.first(0, layer_sum.three)
-        layer_sum.first(1, layer_sum.two)
 
         def side(which):
             return pl.ds(pl.multiple_of(which * half, half), half)
 
         def to_core(k, j):
             return pltpu.make_async_remote_copy(
-                src_ref=part.at[lax.rem(j, 2), k, side(1 - core), :],
+                src_ref=part.at[j, side(1 - core), :],
                 dst_ref=ff.at[j, k],
                 send_sem=dsend.at[CK + k, j],
                 recv_sem=drecv.at[CK + k, j],
@@ -603,29 +634,44 @@
                 device_id_type=MESH,
             )
 
-        def chip_sum(j):
-            for k in range(3):
-                to_core(k, j).wait_recv()
-                ff[j, k] = (
-                    part[lax.rem(j, 2), k, side(core), :].astype(F32) + ff[j, k].astype(F32)
-                ).astype(BF16)
-                to_core(k, j).wait_send()
-
-        def weights(j, carry):
-            cols = pl.ds(pl.multiple_of(j * span, 128), span)
-            for k, (a, b) in enumerate(((xall, gg), (xall, gu), (call, act))):
-                part[lax.rem(j, 2), k] = mm(a[:, cols], b[...], TN).astype(BF16)
+        def chip_sum(k, j):
+            to_core(k, j).wait_recv()
+            ff[j, k] = (
+                part[j, side(core), :].astype(F32) + ff[j, k].astype(F32)
+            ).astype(BF16)
+            to_core(k, j).wait_send()
+
+        for k, (a, b) in enumerate(((xall, gg), (xall, gu), (call, act))):
+
+            def weights(j, carry, k=k, a=a, b=b):
+                cols = pl.ds(pl.multiple_of(j * span, 128), span)
+                if k > 0:
+
+                    @pl.when(j == 2)
+                    def _():
+                        chip_sum(k - 1, 3)
+                        ff_sums[k - 1].start()
+
+                part[j] = mm(a[:, cols], b[...], TN).astype(BF16)
                 to_core(k, j).start()
 
-            @pl.when(j > 0)
-            def _():
-                chip_sum(j - 1)
-
-            return carry
-
-        lax.fori_loop(0, 4, weights, 0)
-        chip_sum(3)
-        ff_sum.start()
+                @pl.when(j > 0)
+                def _():
+                    chip_sum(k, j - 1)
+
+                return carry
+
+            lax.fori_loop(0, 4, weights, 0)
+        chip_sum(2, 3)
+        ff_sums[2].start()
+
+        def feed_sums(n, carry):
+            third = width // 3
+            cols = pl.ds(pl.multiple_of(n * third, 128), third)
+            msend[:, :, cols] = mm(act[...], down_w[:, cols]).astype(BF16).reshape(4, rows, third)
+            return carry
+
+        lax.fori_loop(0, 3, feed_sums, 0)
         for m in (1, 2, 3):
             ln.landed_tensor(G, m, grecv.at[m - 1])
         g = gown[...]
@@ -659,7 +705,7 @@
         pl.run_scoped(
             functools.partial(feed, loads, gate_w, up_w, down_w),
             hidden, hidden, hidden, V((4, rows, width), BF16), V((rows, width), F32),
-            V((2, 3, span, units), BF16),
+            V((4, span, units), BF16), V((seq, units), F32),
         )
 
     pl.run_scoped(
@@ -677,7 +723,7 @@
             c.start()
         for m in range(1, 8):
             ln.over_dp(DR, m, gain.at[0], rows_in.at[d]).start()
-        layer_sum.first(2, layer_sum.near)
+        layer_sum.start()
         wo_pair = CoreSum(ln, CO, wo_part, wo_core)
 
         def output_weights(j, carry):
@@ -687,7 +733,8 @@
             return carry
 
         lax.fori_loop(0, 4, output_weights, 0)
-        layer_sum.hand_on()
+        for k in range(2):
+            ff_sums[k].hand_on()
         own[0].wait()
         for m in (1, 2, 3):
             ln.landed_tensor(GA, m, rows_at(gall, tensor_peer(t, m)))
@@ -765,13 +812,12 @@
             wq_pair.copy(j).start()
             return carry
 
-        ff_sum.hand_on()
+        ff_sums[2].hand_on()
+        wo_sum.hand_on()
         lax.fori_loop(0, 4, head_weights, 0)
         wq_pair.take()
         wq_sum = PlaneSum(ln, DWS, wq_core, wq_in)
         wq_sum.start()
-        gn_sum.hand_on()
-        wo_sum.hand_on()
 
         own[1].wait()
         for m in range(1, 8):
@@ -779,7 +825,7 @@
         gsum[0] = sum(rows_in[i] for i in range(8))
         for m in (1, 2, 3):
             ln.over_tensor(R, m, gsum.at[0], line_in.at[m]).start()
-
+        layer_sum.hand_on()
         stores = []
 
         def out(a, b):
@@ -787,13 +833,41 @@
             c.start()
             stores.append(c)
 
+        def to_rows(total, dst):
+            lanes = total.lanes
+            for h in range(2):
+                u = total.take(h).astype(BF16)
+                for s in range(4):
+                    dst[s, :, h * lanes : (h + 1) * lanes] = u[s * wrows : (s + 1) * wrows, :]
+
+        def feed_weights(k):
+            lanes = units // 2
+            for h in range(2):
+                ffw[k, :, h * lanes : (h + 1) * lanes] = ff_sums[k].take(h)
+            out(ffw.at[k], mlpw_out.at[k])
+
+        to_rows(wo_sum, wo_src)
+        wo_line_sum = LineSum(ln, OL, wo_src, wo_line)
+        wo_line_sum.start()
+        gn_sum.hand_on()
+        wq_sum.hand_on()
         layer[...] = (resid[...] + msend[t].astype(F32) + layer_sum.take()).astype(BF16)
         out(layer, layer_out)
-        lanes = ff_sum.lanes
-        for h in range(2):
-            ffw[:, :, h * lanes : (h + 1) * lanes] = ff_sum.take(h)
-        out(ffw, mlpw_out)
-        wq_sum.hand_on()
+        for k in range(3):
+            feed_weights(k)
+        to_rows(wq_sum, wq_src)
+        for m in (3, 2, 1):
+            ln.over_tensor(WL, m, wq_src.at[tensor_peer(t, m)], wq_all.at[m]).start()
+        wqkv[pl.ds(t, 1)] = wq_src[pl.ds(t, 1)].astype(F32)
+        wo_line_sum.hand_on()
+        total = gsum[0]
+        for m in (1, 2, 3):
+            ln.landed_tensor(R, m, line_in.at[m])
+            total = total + line_in[m]
+        mine = (d * 4 + t) * wrows
+        turned = pltpu.roll(jnp.broadcast_to(total, (8, width)), lax.rem(width - mine, width), 1)
+        gown_row[...] = turned[:, :128]
+        out(gown_row, gain_out)
         x = hid[...].astype(F32)
         inv = lax.rsqrt(jnp.mean(x * x, axis=1, keepdims=True) + EPSILON)
         scaled = (gn_src[t].astype(F32) + gn_sum.take()) * gains[0:1, :]
@@ -803,34 +877,12 @@
             - x * (inv * inv * inv) * jnp.mean(scaled * x, axis=1, keepdims=True)
         )
         out(gin, gin_out)
-        lanes = wo_sum.lanes
-        for h in range(2):
-            u = wo_sum.take(h).astype(BF16)
-            for s in range(4):
-                wo_src[s, :, h * lanes : (h + 1) * lanes] = u[s * wrows : (s + 1) * wrows, :]
-        wo_line_sum = LineSum(ln, OL, wo_src, wo_line)
-        wo_line_sum.start()
-        total = gsum[0]
-        for m in (1, 2, 3):
-            ln.landed_tensor(R, m, line_in.at[m])
-            total = total + line_in[m]
-        line_in[0] = total
-        out(line_in.at[0], gain_out)
-        lanes = wq_sum.lanes
-        for h in range(2):
-            u = wq_sum.take(h).astype(BF16)
-            for s in range(4):
-                wq_src[s, :, h * lanes : (h + 1) * lanes] = u[s * wrows : (s + 1) * wrows, :]
-        for m in (3, 2, 1):
-            ln.over_tensor(WL, m, wq_src.at[tensor_peer(t, m)], wq_all.at[m]).start()
-        wqkv[pl.ds(t, 1)] = wq_src[pl.ds(t, 1)].astype(F32)
-        wo_line_sum.hand_on()
+        wo_full[...] = wo_src[t].astype(F32) + wo_line_sum.take()
+        out(wo_full, wo_out)
         for m in (1, 2, 3):
             ln.landed_tensor(WL, m, wq_all.at[m])
             wqkv[pl.ds(tensor_peer(t, m), 1)] = wq_all[pl.ds(m, 1)].astype(F32)
         out(wqkv, wqkv_out)
-        wo_full[...] = wo_src[t].astype(F32) + wo_line_sum.take()
-        out(wo_full, wo_out)
 
         for m in (1, 2, 3):
             ln.over_tensor(TILE, m, tile, tiles.at[d, t]).wait_send()
@@ -852,7 +904,7 @@
             dd = dp_peer(d, m)
             ln.over_dp(FW, m, w_at(w, dd), w_at(w, dd), to=1).wait_send()
             ln.over_dp(FO, m, w_at(wof, dd), w_at(wof, dd), to=1).wait_send()
-        for s in (layer_sum, gn_sum, wo_line_sum, ff_sum, wo_sum, wq_sum, wo_pair, wq_pair):
+        for s in (layer_sum, gn_sum, wo_line_sum, *ff_sums, wo_sum, wq_sum, wo_pair, wq_pair):
             s.end()
         for c in stores:
             c.wait()
@@ -874,26 +926,12 @@
     seq = 4 * rows
     span = width // 4
     half = span // 2
-    t = lax.axis_index("tensor")
-    index = t * rows + jnp.arange(rows, dtype=jnp.int32)
-    pad = (0, 128 - wrows)
-    tile = jnp.stack(
-        [
-            jnp.pad(gain_attn.astype(F32), pad),
-            jnp.pad(gain_mlp.astype(F32), pad),
-            (index - positions).astype(F32),
-        ]
-        + [jnp.zeros((128,), F32)] * 5
-    )
-    wpack = jnp.concatenate(
-        [a.reshape(wrows, 4, a.shape[1] // 4).transpose(1, 0, 2) for a in (wq, wk, wv)], axis=2
-    )
     near_cos, near_sin, shift = rotary_tables(rows, 4)
     hbm = pl.BlockSpec(memory_space=pl.ANY)
     vmem = pl.BlockSpec(memory_space=pltpu.VMEM)
     V = pltpu.VMEM
     shapes = dict(
-        layer=((rows, width), BF16), gin=((rows, width), F32), gain=((1, width), F32),
+        layer=((rows, width), BF16), gin=((rows, width), F32), gain=((8, 128), F32),
         wqkv=((4, wrows, 8 * HEAD), F32), wo=((wrows, width), F32),
         mlp=((3, half, units), F32),
     )
@@ -904,7 +942,7 @@
     outs = pl.pallas_call(
         layer_kernel,
         out_shape=[jax.ShapeDtypeStruct(*v) for v in shapes.values()],
-        in_specs=[vmem] + [hbm] * 7 + [vmem] * 3,
+        in_specs=[vmem, hbm] + [vmem] * 6 + [hbm] * 4 + [vmem] * 3,
         out_specs=[hbm] * len(shapes),
         scratch_shapes=[
             wide, wide, wide, V((width, 8 * HEAD), BF16), V((width, width), BF16),
@@ -919,16 +957,111 @@
             V((4, half, 8 * HEAD), BF16), V((6, half, 4 * HEAD), BF16),
             V((4, wrows, 8 * HEAD), BF16), V((4, wrows, 8 * HEAD), BF16),
             V((8, 1, width), F32), V((4, 1, width), F32), V((1, 1, width), F32),
+            V((8, 128), F32), V((4, wrows, 8 * HEAD), BF16), V((8, 128), F32),
             pltpu.SemaphoreType.DMA((14, 6)), pltpu.SemaphoreType.DMA((14, 4)),
-            pltpu.SemaphoreType.DMA((14, 8)), pltpu.SemaphoreType.DMA((14, 8)),
-            pltpu.SemaphoreType.DMA((8,)), pltpu.SemaphoreType.DMA((6,)),
+            pltpu.SemaphoreType.DMA((16, 8)), pltpu.SemaphoreType.DMA((16, 8)),
+            pltpu.SemaphoreType.DMA((8,)), pltpu.SemaphoreType.DMA((8,)),
         ],
         name="layer",
         compiler_params=pltpu.CompilerParams(
             collective_id=0, has_side_effects=True, vmem_limit_bytes=VMEM_LIMIT
         ),
-    )(hid, cot, tile, wpack, wo, wg, wu, wd, near_cos, near_sin, shift)
+    )(
+        hid, cot, positions.reshape(1, rows), gain_attn.reshape(1, wrows),
+        gain_mlp.reshape(1, wrows), wq, wk, wv, wo, wg, wu, wd, near_cos, near_sin, shift,
+    )
     return dict(zip(shapes, outs))
+
+
+def finish_kernel(
+    layer, gin, gain, wqkv, wo, mlp, wq, wk, wv, gain_one,
+    layer_out, gin_out, gain_one_out, query_out, key_out, value_out, wo_out, gain_two_out,
+    gate_out, up_out, down_out,
+    lay, gi, ga, w4, wof, ff, one, query, key, value, two, load, store,
+):
+    moves = [
+        (layer, lay, layer_out), (gin, gi, gin_out), (wo, wof, wo_out),
+        (mlp.at[0], ff.at[0], gate_out), (mlp.at[1], ff.at[1], up_out),
+        (mlp.at[2], ff.at[2], down_out), (wqkv, w4, None), (gain, ga, None),
+    ]
+    loads = [pltpu.make_async_copy(a, b, load.at[i]) for i, (a, b, _) in enumerate(moves)]
+    for i in (6, 7, 0, 1, 2, 3, 4, 5):
+        loads[i].start()
+    stores = []
+
+    def out(a, b):
+        c = pltpu.make_async_copy(a, b, store.at[len(stores)])
+        c.start()
+        stores.append(c)
+
+    wrows, span = query.shape[0], query.shape[1] // 4
+    pair = 2 * HEAD
+    loads[6].wait()
+    lane = lax.broadcasted_iota(jnp.int32, (wrows, 8 * HEAD), 1)
+    keys = jnp.zeros((wrows, 8 * HEAD), F32)
+    values = jnp.zeros((wrows, 8 * HEAD), F32)
+    for s in range(4):
+        query[:, s * span : (s + 1) * span] = w4[s, :, :span]
+        u = jnp.concatenate([w4[s, :, span:], jnp.zeros((wrows, span), F32)], axis=1)
+        here = (lane >= pair * s) & (lane < pair * (s + 1))
+        keys = jnp.where(here, lane_roll(u, pair * s), keys)
+        values = jnp.where(here, lane_roll(u, pair * s - pair), values)
+    key[...] = keys
+    value[...] = values
+    out(query, query_out)
+    out(key, key_out)
+    out(value, value_out)
+    total = (
+        jnp.sum(wq[...].astype(F32) * query[...], axis=1, keepdims=True)
+        + jnp.sum(wk[...].astype(F32) * keys, axis=1, keepdims=True)
+        + jnp.sum(wv[...].astype(F32) * values, axis=1, keepdims=True)
+    )
+    tall = jnp.concatenate(
+        [jnp.broadcast_to(total, (wrows, 128)), jnp.zeros((128 - wrows, 128), F32)], axis=0
+    )
+    one[...] = tall.T[0:1, :wrows] / gain_one[...].astype(F32)
+    out(one, gain_one_out)
+    loads[7].wait()
+    two[...] = ga[0:1, :wrows]
+    out(two, gain_two_out)
+    for i in range(6):
+        loads[i].wait()
+        out(moves[i][1], moves[i][2])
+    for c in stores:
+        c.wait()
+
+
+def finish(b, wq, wk, wv, gain_attn):
+    rows, width = b["layer"].shape
+    wrows, kv = wk.shape
+    half, units = b["mlp"].shape[1:]
+    hbm = pl.BlockSpec(memory_space=pl.ANY)
+    vmem = pl.BlockSpec(memory_space=pltpu.VMEM)
+    V = pltpu.VMEM
+    thin = ((rows, width), F32)
+    row = ((1, wrows), F32)
+    weight, narrow = ((wrows, width), F32), ((wrows, kv), F32)
+    shapes = [
+        ((rows, width), BF16), thin, row, weight, narrow, narrow, weight, row,
+        ((half, units), F32), ((half, units), F32), ((half, units), F32),
+    ]
+    return pl.pallas_call(
+        finish_kernel,
+        out_shape=[jax.ShapeDtypeStruct(*v) for v in shapes],
+        in_specs=[hbm] * 6 + [vmem] * 4,
+        out_specs=[hbm] * len(shapes),
+        scratch_shapes=[
+            V((rows, width), BF16), V(*thin), V((8, 128), F32), V((4, wrows, 8 * HEAD), F32),
+            V(*weight), V((3, half, units), F32), V(*row), V(*weight), V(*narrow), V(*narrow),
+            V(*row),
+            pltpu.SemaphoreType.DMA((8,)), pltpu.SemaphoreType.DMA((11,)),
+        ],
+        name="finish",
+        compiler_params=pltpu.CompilerParams(vmem_limit_bytes=VMEM_LIMIT),
+    )(
+        b["layer"], b["gin"], b["gain"], b["wqkv"], b["wo"], b["mlp"], wq, wk, wv,
+        gain_attn.reshape(1, wrows),
+    )
 
 
 QUERY_HEADS = 16
@@ -1222,23 +1355,10 @@
         hidden_in, cotangent, positions, gain_attn, gain_mlp, w_query, key_matrix, value_matrix,
         w_output, w_gate, w_up, w_down,
     )
+    o = finish(b, w_query, key_matrix, value_matrix, gain_attn)
     wrows = w_query.shape[0]
-    parts = b["wqkv"].transpose(1, 0, 2)
-    query = parts[:, :, : 4 * HEAD].reshape(wrows, 16 * HEAD)
-    key = parts[:, :, 4 * HEAD : 6 * HEAD].reshape(wrows, 8 * HEAD)
-    value = parts[:, :, 6 * HEAD :].reshape(wrows, 8 * HEAD)
-
-    def rows_of(w, g):
-        return jnp.sum(w.astype(F32) * g, axis=1)
-
-    gain_one = (
-        rows_of(w_query, query) + rows_of(key_matrix, key) + rows_of(value_matrix, value)
-    ) / gain_attn.astype(F32)
-    mine = lax.axis_index("dp") * lax.axis_size("tensor") + lax.axis_index("tensor")
-    gain_two = lax.dynamic_slice_in_dim(b["gain"][0], mine * wrows, wrows, 0)
     return (
-        b["layer"], b["gin"], gain_one, query, key, value, b["wo"], gain_two,
-        b["mlp"][0], b["mlp"][1], b["mlp"][2].T,
+        o[0], o[1], o[2].reshape(wrows), o[3], o[4], o[5], o[6], o[7].reshape(wrows), o[8], o[9], o[10].T,
     )
 
 

time: 277 us -> 240 us (0.87)
  Pallas kernels: 254 us -> 237 us
  local copies, waits for them, and re-layouts: 15.5 us -> 0 us
  other arithmetic: 5.68 us -> 0 us
    pallas_call x1, Pallas kernels: 254 us -> 232 us  [layer(): pl.pallas_call(layer_kernel, out_shape=[jax.ShapeDtypeStruct(*v) for v in...]
    reshape x6 -> x0, local copies, waits for them, and re-layouts: 4.87 us -> none  [the longest x3 2.98 us: layer(): a.reshape(wrows, 4, a.shape[1] // 4).transpose(1, 0, 2)]
    pallas_call x0 -> x1, Pallas kernels: none -> 4.81 us  [finish(): pl.pallas_call(finish_kernel, out_shape=[jax.ShapeDtypeStruct(*v) for v i...]
    slice x3 -> x0, local copies, waits for them, and re-layouts: 3.76 us -> none  [the longest x2 1.95 us: fast_shards(): key = parts[:, :, 4 * HEAD:6 * HEAD].reshape(wrows, 8 * HEAD)]
    unnamed x22 -> x0, local copies, waits for them, and re-layouts: 3.36 us -> none
where the time goes in v5:
time: 240 us; the launch traced here: 238 us
  Pallas kernels  237 us (99%)
    pallas_call x1, Pallas kernels, layer(): pl.pallas_call(layer_kernel, out_shape=[jax.ShapeDtypeStruct(*v) for v in...  232 us
    pallas_call x1, Pallas kernels, finish(): pl.pallas_call(finish_kernel, out_shape=[jax.ShapeDtypeStruct(*v) for v i...  4.81 us

profile of v5, /device:TPU:4, one launch (start us, length us, event | category | flops | bytes accessed | tf_op | source)
XLA Modules:
  0.0 237.6 jit_solution(18414959087893220379)
XLA Ops:
  0.6 232.0 %layer.1 = (bf16[128,1536]{1,0:T(8,128)(2,1)}, f32[128,1536]{1,0:T(8,128)}, f32[8,128]{1,0:T(8,128)}, f32[4,48,768]{2,1,0:T(8,128)}, f32[48,1536]{1,0:T(8,128)}, /*index=5*/f32[3,192,1024]{2,1,0:T(8,128)}) custom-call(bf16[128,1536]{1,0:T(8,128)(2,1)} %hid.1, bf16[128,1536]{1,0:T(8,128)(2,1)} %cot.1, s32[1,128]{1,0:T(1,128)} %bitcast.8, ...), custom_call_target="tpu_custom_call" | custom-call | tf_op jit(solution)/shard_map/layer/pallas_call | solution.py:942
  232.6 4.8 %finish.1 = (bf16[128,1536]{1,0:T(8,128)(2,1)}, f32[128,1536]{1,0:T(8,128)}, f32[1,48]{1,0:T(1,128)}, f32[48,1536]{1,0:T(8,128)}, f32[48,768]{1,0:T(8,128)}, /*i...) custom-call(bf16[128,1536]{1,0:T(8,128)(2,1)} %get-tuple-element.28., ...), custom_call_target="tpu_custom_call" | custom-call | tf_op jit(solution)/shard_map/finish/pallas_call | solution.py:1048

commit v6 on v5

--- a/solution.py
+++ b/solution.py
@@ -152,7 +152,7 @@
                 shard, m = self.shard_at(i)
                 pltpu.make_async_copy(at(shard), at(shard), self.tsend.at[kind, 2 + i]).wait()
 
-    def barrier(self, tensor_peers, dp_peers):
+    def greet(self, tensor_peers, dp_peers):
         sem = pltpu.get_barrier_semaphore()
         for m in tensor_peers:
             pl.semaphore_signal(
@@ -168,7 +168,7 @@
                 device_id={"dp": dp_peer(self.d, m), "tensor": self.t},
                 device_id_type=MESH,
             )
-        pl.semaphore_wait(sem, len(tensor_peers) + len(dp_peers))
+        return len(tensor_peers) + len(dp_peers)
 
 
 def mm(a, b, dims=((1,), (0,))):
@@ -251,28 +251,28 @@
 
 
 class PlaneSum:
-    def __init__(self, ln, kind, src, recv):
-        self.ln, self.kind, self.src, self.recv = ln, kind, src, recv
+    def __init__(self, ln, kind, src, slot, width):
+        self.ln, self.kind, self.src, self.slot = ln, kind, src, slot
         j = lax.div(ln.d, 2)
         self.j = j
         self.x = j + 1 - 2 * lax.rem(j, 2)
         self.y = lax.rem(j + 2, 4)
         self.diag = lax.rem(self.x + 2, 4)
-        self.lanes = src.shape[-1] // 2
+        self.lanes = width // 2
 
     def half(self, ref, h):
         spot = [slice(None)] * (len(ref.shape) - 1) + [pl.ds(h * self.lanes, self.lanes)]
         return ref.at[tuple(spot)]
 
     def copy(self, src, m, i):
-        return self.ln.over_dp(self.kind, i, src, self.recv.at[i], to=m)
+        return self.ln.over_dp(self.kind, i, src, self.slot(i), to=m)
 
     def plan(self):
         return (
-            (self.half(self.src.at[self.diag], 0), 2, 0),
-            (self.half(self.src.at[self.diag], 1), 4, 2),
-            (self.half(self.src.at[self.x], 0), 2, 1),
-            (self.half(self.src.at[self.y], 1), 4, 3),
+            (self.half(self.src(self.diag), 0), 2, 0),
+            (self.half(self.src(self.diag), 1), 4, 2),
+            (self.half(self.src(self.x), 0), 2, 1),
+            (self.half(self.src(self.y), 1), 4, 3),
         )
 
     def start(self):
@@ -281,20 +281,20 @@
 
     def hand_on(self):
         for i, h, block, m in ((0, 0, self.y, 4), (2, 1, self.x, 2)):
-            self.ln.landed_dp(self.kind, i, self.recv.at[i])
-            self.recv[i] = (
-                self.recv[i].astype(F32) + self.half(self.src.at[block], h)[...].astype(F32)
+            self.ln.landed_dp(self.kind, i, self.slot(i))
+            self.slot(i)[...] = (
+                self.slot(i)[...].astype(F32) + self.half(self.src(block), h)[...].astype(F32)
             ).astype(BF16)
             self.copy_on(i, h, m).start()
 
     def copy_on(self, i, h, m):
-        return self.ln.over_dp(self.kind, 4 + h, self.recv.at[i], self.recv.at[4 + h], to=m)
+        return self.ln.over_dp(self.kind, 4 + h, self.slot(i), self.slot(4 + h), to=m)
 
     def take(self, h):
         for i in (1 + 2 * h, 4 + h):
-            self.ln.landed_dp(self.kind, i, self.recv.at[i])
-        own = self.half(self.src.at[self.j], h)[...].astype(F32)
-        return own + self.recv[1 + 2 * h].astype(F32) + self.recv[4 + h].astype(F32)
+            self.ln.landed_dp(self.kind, i, self.slot(i))
+        own = self.half(self.src(self.j), h)[...].astype(F32)
+        return own + self.slot(1 + 2 * h)[...].astype(F32) + self.slot(4 + h)[...].astype(F32)
 
     def end(self):
         for src, m, i in self.plan():
@@ -303,10 +303,55 @@
             self.copy_on(i, h, m).wait_send()
 
 
+class PlaneGather:
+    def __init__(self, ln, kind, hand, block, part):
+        self.ln, self.kind, self.hand, self.block, self.part = ln, kind, hand, block, part
+
+    def own(self, m):
+        here = self.block(self.ln.d)
+        return self.ln.over_dp(self.kind, m, here, here)
+
+    def on(self, m):
+        h, to, i = (0, 4, 3) if m == 2 else (1, 2, 5)
+        piece = self.part(dp_peer(self.ln.d, m), h)
+        return self.ln.over_dp(self.kind, i, piece, piece, to=to)
+
+    def core(self, m):
+        block = self.block(dp_peer(self.ln.d, m))
+        return self.ln.over_dp(self.hand, m, block, block, to=1)
+
+    def start(self):
+        for m in (2, 4, 1):
+            self.own(m).start()
+
+    def hand_on(self):
+        for m in (2, 4):
+            self.ln.landed_dp(self.kind, m, self.block(dp_peer(self.ln.d, m)))
+            self.on(m).start()
+            self.core(m).start()
+
+    def take(self):
+        far = dp_peer(self.ln.d, 6)
+        for h, i in ((0, 3), (1, 5)):
+            self.ln.landed_dp(self.kind, i, self.part(far, h))
+        self.core(6).start()
+        self.ln.landed_dp(self.kind, 1, self.block(dp_peer(self.ln.d, 1)))
+        for m in (2, 4, 6):
+            self.ln.landed_dp(self.hand, m, self.block(dp_peer(self.ln.d, m ^ 1)))
+
+    def end(self):
+        for m in (2, 4, 1):
+            self.own(m).wait_send()
+        for m in (2, 4):
+            self.on(m).wait_send()
+        for m in (2, 4, 6):
+            self.core(m).wait_send()
+
+
 class CoreSum:
-    def __init__(self, ln, kind, src, recv):
-        self.ln, self.kind, self.src, self.recv = ln, kind, src, recv
-        self.half = recv.shape[1]
+    def __init__(self, ln, kind, src, slot):
+        self.ln, self.kind, self.src, self.slot = ln, kind, src, slot
+        self.half = src.shape[1] // 2
         self.core = lax.rem(ln.d, 2)
 
     def side(self, which):
@@ -316,7 +361,7 @@
         ln = self.ln
         return pltpu.make_async_remote_copy(
             src_ref=self.src.at[j, self.side(1 - self.core), :],
-            dst_ref=self.recv.at[j],
+            dst_ref=self.slot(j),
             send_sem=ln.dsend.at[self.kind, j],
             recv_sem=ln.drecv.at[self.kind, j],
             device_id={"dp": dp_peer(ln.d, 1), "tensor": ln.t},
@@ -326,8 +371,8 @@
     def take(self):
         def one(j, carry):
             self.copy(j).wait_recv()
-            self.recv[j] = (
-                self.recv[j].astype(F32) + self.src[j, self.side(self.core), :].astype(F32)
+            self.slot(j)[...] = (
+                self.slot(j)[...].astype(F32) + self.src[j, self.side(self.core), :].astype(F32)
             ).astype(BF16)
             return carry
 
@@ -346,8 +391,8 @@
     layer_out, gin_out, gain_out, wqkv_out, wo_out, mlpw_out,
     xall, nall, call, w, wof, tiles, qh, kh, vh, att, arow, lse, start, gains, resid, normed2,
     grecv, ff, msend, gatt, gres, low, gain,
-    gall, mlp_in, ff_in, wo_core, wo_in, wo_src, wo_line, wq_core, wq_in, wq_src, wq_all,
-    rows_in, line_in, gsum, tile, wpack, gown_row,
+    gall, mlp_in, ff_in, wo_core, wo_in, wo_src, wo_line, wq_src, wq_all,
+    rows_in, line_in, gsum, tile, wpack, gown_row, bias,
     tsend, trecv, dsend, drecv, local, store,
 ):
     ln = Links(tsend, trecv, dsend, drecv)
@@ -357,6 +402,7 @@
     seq = 4 * rows
     span = width // 4
     half = span // 2
+    wide = 2 * span
     core = lax.rem(d, 2)
     wrows = wo.shape[0]
     srows = 4 * wrows
@@ -382,13 +428,53 @@
         return w_at(wof, d, tt)
 
     def columns(tt):
-        return arow.at[:, pl.ds(pl.multiple_of(tt * span, 128), span)]
+        return arow.at[:, pl.ds(pl.multiple_of((tt - 1) * wide, 128), wide)]
 
     at_own = ds_of(t)
+    near, two, three = (tensor_peer(t, m) for m in (1, 2, 3))
+    inner, outer = pl.when(ln.mid == 1), pl.when(ln.mid == 0)
+
+    def to_inner(kind, src, dst, act):
+        @outer
+        def _():
+            act(ln.over_tensor(kind, 1, src(near - 1), dst))
+            act(ln.over_tensor(kind, 2, src(two - 1), dst))
+
+        @inner
+        def _():
+            act(ln.over_tensor(kind, 3, src(three - 1), dst))
+
+    def go(c):
+        c.start()
+
+    def gone(c):
+        c.wait_send()
+
+    def from_inner(kind, take):
+        def one(m):
+            take(kind, m, tensor_peer(t, m))
+
+        @outer
+        def _():
+            one(1)
+            one(2)
+
+        @inner
+        def _():
+            one(3)
+
+    def part_rows(ref, dd, h):
+        return ref.at[pl.ds(pl.multiple_of(dd * srows + h * (srows // 2), 16), srows // 2), :]
+
+    w_plane = PlaneGather(ln, DW, FW, lambda dd: w_at(w, dd), functools.partial(part_rows, w))
+    o_plane = PlaneGather(ln, DO, FO, lambda dd: w_at(wof, dd), functools.partial(part_rows, wof))
     scale = 1.0 / math.sqrt(HEAD)
     layer_sum = LineSum(ln, M, msend, mlp_in)
     ff_sums = [
-        PlaneSum(ln, DF + k, ff.at[:, k], ff_in.at[:, k]) for k in range(3)
+        PlaneSum(
+            ln, DF + k, lambda j, k=k: ff.at[j, k], lambda i, k=k: ff_in.at[i, k], units
+        )
+        for k in range(3)
     ]
 
     def visible(shape, b):
@@ -398,58 +484,55 @@
         return (key <= query) & (key >= first)
 
     def front(outh):
+        greeted = ln.greet((1, 2, 3), (1, 2, 3, 4, 5, 6, 7))
         tile[...] = jnp.zeros_like(tile)
         tile[0:1, :wrows] = gain_one[...].astype(F32)
         tile[1:2, :wrows] = gain_two[...].astype(F32)
         index = t * rows + lax.broadcasted_iota(jnp.int32, (1, rows), 1)
         tile[2:3, :] = (index - pos[...]).astype(F32)
-        keys, values = wk[...].astype(F32), wv[...].astype(F32)
-        pair = 2 * HEAD
-        lane = lax.broadcasted_iota(jnp.int32, (wrows, span), 1)
-        for s in range(4):
-            wpack[s, :, :span] = wq[:, s * span : (s + 1) * span]
-            wpack[s, :, span:] = jnp.where(
-                lane < pair,
-                lane_roll(keys, -pair * s)[:, :span],
-                lane_roll(values, pair - pair * s)[:, :span],
-            ).astype(BF16)
+        for g in range(2):
+            wpack[g, :, :wide] = wq[:, g * wide : (g + 1) * wide]
+            wpack[g, :, wide : wide + span] = wk[:, g * span : (g + 1) * span]
+            wpack[g, :, wide + span :] = wv[:, g * span : (g + 1) * span]
         mine = [
             pltpu.make_async_copy(a, b, local.at[i])
             for i, (a, b) in enumerate(
-                [(tile, tiles.at[d, t]), (wpack.at[t], w_at(w, d, t)), (wo, wo_of(t)),
-                 (hid, x_of(t)), (cot, c_of(t))]
+                [(tile, tiles.at[d, t]), (wo, wo_of(t)), (hid, x_of(t)), (cot, c_of(t))]
             )
         ]
         for c in mine:
             c.start()
-        ln.barrier((1, 2, 3), (1, 2, 3, 4, 5, 6, 7))
+        own_w = pltpu.make_async_copy(wpack.at[t - 1], w_at(w, d, t), local.at[4])
+        inner(own_w.start)
+        pl.semaphore_wait(pltpu.get_barrier_semaphore(), greeted)
         for m in (1, 2, 3):
             ln.over_tensor(TILE, m, tile, tiles.at[d, t]).start()
-        for m in (1, 2, 3):
-            ln.over_tensor(W, m, wpack.at[tensor_peer(t, m)], w_at(w, d, t)).start()
+        to_inner(W, lambda g: wpack.at[g], w_at(w, d, t), go)
         ln.gather_start(O, wo, wo_of)
-        ln.gather_start(X, hid, x_of)
+        inner(ln.over_tensor(C, 1, cot, c_of(t)).start)
+        to_inner(X, lambda g: hid, x_of(t), go)
         mine[0].wait()
         for m in (1, 2, 3):
             ln.landed_tensor(TILE, m, tiles.at[d, tensor_peer(t, m)])
         for m in range(1, 8):
             ln.over_dp(DT, m, tiles.at[d], tiles.at[d]).start()
+
+        @inner
+        def _():
+            own_w.wait()
+            for m in (1, 2, 3):
+                ln.landed_tensor(W, m, w_at(w, d, tensor_peer(t, m)))
+            w_plane.start()
+
         mine[1].wait()
-        for m in (1, 2, 3):
-            ln.landed_tensor(W, m, w_at(w, d, tensor_peer(t, m)))
-        for m in (2, 4, 6, 1):
-            ln.over_dp(DW, m, w_at(w, d), w_at(w, d)).start()
-        mine[2].wait()
         for i in (1, 2, 3):
             ln.gather_take(O, i, wo_of)
-        for m in (2, 4, 6, 1):
-            ln.over_dp(DO, m, w_at(wof, d), w_at(wof, d)).start()
+        o_plane.start()
+        mine[3].wait()
+        inner(ln.over_tensor(C, 3, cot, c_of(t)).start)
+        outer(lambda: ln.gather_start(C, cot, c_of))
         for m in range(1, 8):
             ln.landed_dp(DT, m, tiles.at[dp_peer(d, m)])
-        for m in (2, 4, 6):
-            dd = dp_peer(d, m)
-            ln.landed_dp(DW, m, w_at(w, dd))
-            ln.over_dp(FW, m, w_at(w, dd), w_at(w, dd), to=1).start()
         for g in range(4):
             acc = jnp.zeros((8, 8 * wrows), F32)
             for j in range(8):
@@ -461,14 +544,7 @@
             gains[:, g * 8 * wrows : (g + 1) * 8 * wrows] = acc
         for s in range(4):
             start[:, s * rows : (s + 1) * rows] = tiles[d, s, 2:3, :]
-        mine[3].wait()
-        for i in (1, 2, 3):
-            ln.gather_take(X, i, x_of)
-        mine[4].wait()
-        ln.gather_start(C, cot, c_of)
-        ln.landed_dp(DW, 1, w_at(w, dp_peer(d, 1)))
-        for m in (2, 4, 6):
-            ln.landed_dp(FW, m, w_at(w, dp_peer(d, m ^ 1)))
+        mine[2].wait()
 
         def project(s, carry):
             at = ds_of(s)
@@ -477,32 +553,35 @@
             normed = (x * inv * gains[0:1, :]).astype(BF16)
             nall[at, :] = normed
             cosine, sine = turn_tables(near_cos, near_sin, shift, s)
-            q = mm(normed, w[:, : 4 * HEAD])
-            q = q * cosine + swap_halves(q) * sine
-            kv = mm(normed, w[:, 4 * HEAD :])
-            lane = lax.broadcasted_iota(jnp.int32, kv.shape, 1)
-            kv = jnp.where(lane < 2 * HEAD, kv * cosine + swap_halves(kv) * sine, kv)
             keep = lax.broadcasted_iota(jnp.int32, (rows, 128), 1) < HEAD
 
             def head(u, h):
                 return jnp.where(keep, lane_roll(u, -HEAD * h)[:, :128], 0.0).astype(BF16)
 
-            for h in range(4):
-                qh[h, at, :] = head(q, h)
-            for c in range(2):
-                kh[c, at, :] = head(kv, c)
-                vh[c, at, :] = head(kv, c + 2)
+            for g in range(4):
+                u = mm(normed, w[:, g * span : (g + 1) * span])
+                if g < 3:
+                    u = u * cosine + swap_halves(u) * sine
+                for h in range(4):
+                    if g < 2:
+                        qh[4 * g + h, at, :] = head(u, h)
+                    elif g == 2:
+                        kh[h, at, :] = head(u, h)
+                    else:
+                        vh[h, at, :] = head(u, h)
             return carry
 
-        lax.fori_loop(0, 4, project, 0)
-
         def attend(h, carry):
+            @pl.when(h == 0)
+            def _():
+                for i in (1, 2):
+                    ln.gather_take(C, i, c_of)
+
             c = lax.div(h, 2)
             for b in range(4):
                 far = (b + 1) * rows
                 here = slice(b * rows, far)
-                sc = mm(kh[c, :far, :], qh[h, here, :], NT) * scale
-                sc = jnp.where(visible(sc.shape, b), sc, MASKED)
+                sc = mm(kh[c, :far, :], qh[h, here, :], NT) * scale + bias[:far, here]
                 peak = jnp.max(sc, axis=0, keepdims=True)
                 e = jnp.exp(sc - peak)
                 total = jnp.sum(e, axis=0, keepdims=True)
@@ -511,40 +590,45 @@
                 lse[h, :, here] = peak + jnp.log(total)
             return carry
 
-        lax.fori_loop(0, 4, attend, 0)
 
         def pack(b, carry):
-            acc = jnp.zeros((rows, 4 * HEAD), F32)
-            for h in range(4):
-                piece = jnp.concatenate(
-                    [outh[h, ds_of(b), :], jnp.zeros((rows, 4 * HEAD - 128), F32)], axis=1
-                )
-                acc = acc + lane_roll(piece, HEAD * h)
-            att[b] = acc.astype(BF16)
+            for g in range(2):
+                acc = jnp.zeros((rows, span), F32)
+                for h in range(4):
+                    piece = jnp.concatenate(
+                        [outh[4 * g + h, ds_of(b), :], jnp.zeros((rows, span - 128), F32)], axis=1
+                    )
+                    acc = acc + lane_roll(piece, HEAD * h)
+                att[b, :, g * span : (g + 1) * span] = acc.astype(BF16)
             return carry
 
-        lax.fori_loop(0, 4, pack, 0)
-        ln.gather_end(X, hid, x_of)
-        for m in (3, 2, 1):
-            ln.over_tensor(A, m, att.at[tensor_peer(t, m)], columns(t)).start()
         own = pltpu.make_async_copy(att.at[t], columns(t), local.at[0])
-        own.start()
-
-        @pl.when(ln.mid == 1)
-        def _():
-            for i in (1, 2, 3):
-                ln.gather_take(C, i, c_of)
-
-        for m in (2, 4, 6):
-            dd = dp_peer(d, m)
-            ln.landed_dp(DO, m, w_at(wof, dd))
-            ln.over_dp(FO, m, w_at(wof, dd), w_at(wof, dd), to=1).start()
-        ln.landed_dp(DO, 1, w_at(wof, dp_peer(d, 1)))
-        for m in (2, 4, 6):
-            ln.landed_dp(FO, m, w_at(wof, dp_peer(d, m ^ 1)))
-        own.wait()
-        for m in (1, 2, 3):
-            ln.landed_tensor(A, m, columns(tensor_peer(t, m)))
+
+        @inner
+        def _():
+            for b in range(4):
+                far = (b + 1) * rows
+                bias[:far, b * rows : far] = jnp.where(visible((far, rows), b), 0.0, MASKED)
+            w_plane.hand_on()
+            w_plane.take()
+            for m in (1, 2, 3):
+                ln.landed_tensor(X, m, x_of(tensor_peer(t, m)))
+            lax.fori_loop(0, 4, project, 0)
+
+        o_plane.hand_on()
+
+        @inner
+        def _():
+            lax.fori_loop(0, 8, attend, 0)
+            lax.fori_loop(0, 4, pack, 0)
+            for m in (2, 1, 3):
+                ln.over_tensor(A, m, att.at[tensor_peer(t, m)], columns(t)).start()
+            own.start()
+            ln.gather_take(C, 3, c_of)
+            own.wait()
+
+        o_plane.take()
+        from_inner(A, lambda kind, m, p: ln.landed_tensor(kind, m, columns(p)))
         third = width // 3
 
         def project_out(n, carry):
@@ -580,21 +664,15 @@
 
         piece = units // 4
 
-        def act_grads(c, carry):
-            cols = pl.ds(pl.multiple_of(c * piece, 128), piece)
-            gact[:, cols] = mm(call[...], down_w[cols, :], NT)
-            return carry
-
-        lax.fori_loop(0, 4, act_grads, 0)
-
         def one_shard(i, carry):
             shard, m = ln.shard_at(i)
+            at = ds_of(shard)
+            gact[...] = mm(call[at, :], down_w[...], NT)
 
             @pl.when(i > 0)
             def _():
                 ln.gather_take(N, i, x_of)
 
-            at = ds_of(shard)
             r = xall[at, :]
             for c in range(4):
                 cols = slice(c * piece, (c + 1) * piece)
@@ -603,7 +681,7 @@
                 sig = 1.0 / (1.0 + jnp.exp(-gate))
                 silu = gate * sig
                 act[at, cols] = (silu * up).astype(BF16)
-                g_act = gact[at, cols]
+                g_act = gact[:, cols]
                 gg[at, cols] = (g_act * up * sig * (1.0 + gate * (1.0 - sig))).astype(BF16)
                 gu[at, cols] = (g_act * silu).astype(BF16)
             g = mm(gg[at, :], gate_w[...], NT) + mm(gu[at, :], up_w[...], NT)
@@ -688,8 +766,8 @@
         )
         gres[...] = gr
         low[...] = gr.astype(BF16)
-        for s in range(4):
-            gatt[s] = mm(low[...], wof[s * span : (s + 1) * span, :], NT).astype(BF16)
+        for g in range(2):
+            gatt[g] = mm(low[...], wof[g * wide : (g + 1) * wide, :], NT).astype(BF16)
         for m in (1, 2, 3):
             to_owner(tensor_peer(t, m), m).wait_send()
 
@@ -700,31 +778,32 @@
         ]
         for c in loads:
             c.start()
-        pl.run_scoped(front, V((4, seq, 128), F32))
+        pl.run_scoped(front, V((8, seq, 128), F32))
         hidden = V((seq, units), BF16)
         pl.run_scoped(
             functools.partial(feed, loads, gate_w, up_w, down_w),
             hidden, hidden, hidden, V((4, rows, width), BF16), V((rows, width), F32),
-            V((4, span, units), BF16), V((seq, units), F32),
+            V((4, span, units), BF16), V((rows, units), F32),
         )
 
     pl.run_scoped(
         forward, V((width, units), BF16), V((width, units), BF16), V((units, width), BF16)
     )
 
-    def backward(gh, gq, gk, gv, gqkv, gn_src, wo_part, wq_part, layer, gin, wqkv, wo_full, ffw):
-        for m in (3, 2, 1):
-            ln.over_tensor(GA, m, gatt.at[tensor_peer(t, m)], rows_at(gall, t)).start()
+    def backward(gh, gq, gk, gv, gqkv, gn_src, wo_part, layer, gin, wqkv, wo_full, ffw):
+        to_inner(GA, lambda g: gatt.at[g], rows_at(gall, t), go)
         own = [
-            pltpu.make_async_copy(gatt.at[t], rows_at(gall, t), local.at[0]),
+            pltpu.make_async_copy(gatt.at[t - 1], rows_at(gall, t), local.at[0]),
             pltpu.make_async_copy(gain, rows_in.at[pl.ds(d, 1)], local.at[1]),
         ]
-        for c in own:
-            c.start()
+        inner(own[0].start)
+        own[1].start()
         for m in range(1, 8):
             ln.over_dp(DR, m, gain.at[0], rows_in.at[d]).start()
         layer_sum.start()
-        wo_pair = CoreSum(ln, CO, wo_part, wo_core)
+        ln.gather_end(O, wo, wo_of)
+        o_plane.end()
+        wo_pair = CoreSum(ln, CO, wo_part, lambda j: wo_core.at[j])
 
         def output_weights(j, carry):
             cols = pl.ds(pl.multiple_of(j * span, 128), span)
@@ -735,25 +814,19 @@
         lax.fori_loop(0, 4, output_weights, 0)
         for k in range(2):
             ff_sums[k].hand_on()
-        own[0].wait()
-        for m in (1, 2, 3):
-            ln.landed_tensor(GA, m, rows_at(gall, tensor_peer(t, m)))
         keep = lax.broadcasted_iota(jnp.int32, (rows, 128), 1) < HEAD
+        wo_pair.take()
+        wo_sum = PlaneSum(ln, DOS, lambda j: wo_core.at[j], lambda i: wo_in.at[i], width)
+        wo_sum.start()
 
         def split(b, carry):
-            u = gall[ds_of(b), :].astype(F32)
-            for h in range(4):
-                gh[h, ds_of(b), :] = jnp.where(
-                    keep, lane_roll(u, -HEAD * h)[:, :128], 0.0
-                ).astype(BF16)
+            for g in range(2):
+                u = gall[ds_of(b), g * span : (g + 1) * span].astype(F32)
+                for h in range(4):
+                    gh[4 * g + h, ds_of(b), :] = jnp.where(
+                        keep, lane_roll(u, -HEAD * h)[:, :128], 0.0
+                    ).astype(BF16)
             return carry
-
-        lax.fori_loop(0, 4, split, 0)
-        gk[...] = jnp.zeros_like(gk)
-        gv[...] = jnp.zeros_like(gv)
-        wo_pair.take()
-        wo_sum = PlaneSum(ln, DOS, wo_core, wo_in)
-        wo_sum.start()
 
         def attend_back(h, carry):
             c = lax.div(h, 2)
@@ -761,8 +834,7 @@
                 far = (b + 1) * rows
                 here = slice(b * rows, far)
                 k, v, q, g = kh[c, :far, :], vh[c, :far, :], qh[h, here, :], gh[h, here, :]
-                sc = mm(k, q, NT) * scale
-                sc = jnp.where(visible(sc.shape, b), sc, MASKED)
+                sc = mm(k, q, NT) * scale + bias[:far, here]
                 p = jnp.exp(sc - lse[h, :, here])
                 gp = mm(v, g, NT)
                 gs = (p * (gp - jnp.sum(p * gp, axis=0, keepdims=True))).astype(BF16)
@@ -771,7 +843,6 @@
                 gv[c, :far, :] += mm(p.astype(BF16), g)
             return carry
 
-        lax.fori_loop(0, 4, attend_back, 0)
 
         def gather_heads(b, carry):
             at = ds_of(b)
@@ -787,37 +858,74 @@
             def turned(u):
                 return u * cosine - swap_halves(u) * sine
 
-            left = sum(placed(turned(gq[h, at, :]), h) for h in range(4))
-            right = sum(placed(turned(gk[c, at, :]), c) for c in range(2))
-            right = right + sum(placed(gv[c, at, :], c + 2) for c in range(2))
-            gqkv[at, : 4 * HEAD] = left.astype(BF16)
-            gqkv[at, 4 * HEAD :] = right.astype(BF16)
+            parts = [
+                [turned(gq[h, at, :]) for h in range(4)],
+                [turned(gq[4 + h, at, :]) for h in range(4)],
+                [turned(gk[c, at, :]) for c in range(4)],
+                [gv[c, at, :] for c in range(4)],
+            ]
+            for g, heads in enumerate(parts):
+                u = sum(placed(v, h) for h, v in enumerate(heads))
+                gqkv[at, g * span : (g + 1) * span] = u.astype(BF16)
             return carry
 
-        lax.fori_loop(0, 4, gather_heads, 0)
-        gn_sum = LineSum(ln, B, gn_src, grecv)
+        def to_row_owner(shard, m):
+            return pltpu.make_async_remote_copy(
+                src_ref=gn_src.at[shard],
+                dst_ref=grecv.at[m - 1],
+                send_sem=tsend.at[B, m],
+                recv_sem=trecv.at[B, m],
+                device_id={"dp": d, "tensor": shard},
+                device_id_type=MESH,
+            )
 
         def norm_grads(i, carry):
-            shard, _ = ln.shard_at(3 - i)
+            shard, m = ln.shard_at(3 - i)
             gn_src[shard] = mm(gqkv[ds_of(shard), :], w[...], NT).astype(BF16)
-            gn_sum.first(i, shard)
+
+            @pl.when(i < 3)
+            def _():
+                to_row_owner(shard, m).start()
+
             return carry
 
-        lax.fori_loop(0, 4, norm_grads, 0)
-        wq_pair = CoreSum(ln, CW, wq_part, wq_core)
+        @inner
+        def _():
+            own[0].wait()
+            for m in (1, 2, 3):
+                ln.landed_tensor(GA, m, rows_at(gall, tensor_peer(t, m)))
+            lax.fori_loop(0, 4, split, 0)
+            gk[...] = jnp.zeros_like(gk)
+            gv[...] = jnp.zeros_like(gv)
+            lax.fori_loop(0, 8, attend_back, 0)
+            lax.fori_loop(0, 4, gather_heads, 0)
+            wo_sum.hand_on()
+            lax.fori_loop(0, 4, norm_grads, 0)
+
+        outer(wo_sum.hand_on)
+        ff_sums[2].hand_on()
+
+        def in_wo(j):
+            return wof.at[pl.ds(pl.multiple_of(j * half, half), half), :]
+
+        def in_wo_half(i):
+            return wof.at[(4 + i // 2) * half : (5 + i // 2) * half, (i % 2) * wide : (i % 2 + 1) * wide]
+
+        wo_pair.end()
+        wq_pair = CoreSum(ln, CW, wo_part, in_wo)
+        wq_sum = PlaneSum(ln, DWS, in_wo, in_wo_half, width)
 
         def head_weights(j, carry):
             cols = pl.ds(pl.multiple_of(j * span, 128), span)
-            wq_part[j] = mm(nall[:, cols], gqkv[...], TN).astype(BF16)
+            wo_part[j] = mm(nall[:, cols], gqkv[...], TN).astype(BF16)
             wq_pair.copy(j).start()
             return carry
 
-        ff_sums[2].hand_on()
-        wo_sum.hand_on()
-        lax.fori_loop(0, 4, head_weights, 0)
-        wq_pair.take()
-        wq_sum = PlaneSum(ln, DWS, wq_core, wq_in)
-        wq_sum.start()
+        @inner
+        def _():
+            lax.fori_loop(0, 4, head_weights, 0)
+            wq_pair.take()
+            wq_sum.start()
 
         own[1].wait()
         for m in range(1, 8):
@@ -849,16 +957,19 @@
         to_rows(wo_sum, wo_src)
         wo_line_sum = LineSum(ln, OL, wo_src, wo_line)
         wo_line_sum.start()
-        gn_sum.hand_on()
-        wq_sum.hand_on()
+        inner(wq_sum.hand_on)
         layer[...] = (resid[...] + msend[t].astype(F32) + layer_sum.take()).astype(BF16)
         out(layer, layer_out)
         for k in range(3):
             feed_weights(k)
-        to_rows(wq_sum, wq_src)
-        for m in (3, 2, 1):
-            ln.over_tensor(WL, m, wq_src.at[tensor_peer(t, m)], wq_all.at[m]).start()
-        wqkv[pl.ds(t, 1)] = wq_src[pl.ds(t, 1)].astype(F32)
+
+        @inner
+        def _():
+            to_rows(wq_sum, wq_src)
+            for m in (2, 1, 3):
+                ln.over_tensor(WL, m, wq_src.at[tensor_peer(t, m)], wq_all.at[m]).start()
+            wqkv[pl.ds(t - 1, 1)] = wq_src[pl.ds(t, 1)].astype(F32)
+
         wo_line_sum.hand_on()
         total = gsum[0]
         for m in (1, 2, 3):
@@ -870,7 +981,17 @@
         out(gown_row, gain_out)
         x = hid[...].astype(F32)
         inv = lax.rsqrt(jnp.mean(x * x, axis=1, keepdims=True) + EPSILON)
-        scaled = (gn_src[t].astype(F32) + gn_sum.take()) * gains[0:1, :]
+        from_inner(B, lambda kind, m, p: ln.landed_tensor(kind, m, grecv.at[m - 1]))
+
+        @outer
+        def _():
+            gin[...] = grecv[0].astype(F32) + grecv[1].astype(F32)
+
+        @inner
+        def _():
+            gin[...] = grecv[2].astype(F32) + gn_src[t].astype(F32)
+
+        scaled = gin[...] * gains[0:1, :]
         gin[...] = (
             gres[...]
             + inv * scaled
@@ -879,42 +1000,46 @@
         out(gin, gin_out)
         wo_full[...] = wo_src[t].astype(F32) + wo_line_sum.take()
         out(wo_full, wo_out)
-        for m in (1, 2, 3):
-            ln.landed_tensor(WL, m, wq_all.at[m])
-            wqkv[pl.ds(tensor_peer(t, m), 1)] = wq_all[pl.ds(m, 1)].astype(F32)
+
+        def columns_in(kind, m, p):
+            ln.landed_tensor(kind, m, wq_all.at[m])
+            wqkv[pl.ds(p - 1, 1)] = wq_all[pl.ds(m, 1)].astype(F32)
+
+        from_inner(WL, columns_in)
         out(wqkv, wqkv_out)
 
         for m in (1, 2, 3):
             ln.over_tensor(TILE, m, tile, tiles.at[d, t]).wait_send()
-            ln.over_tensor(W, m, wpack.at[tensor_peer(t, m)], w_at(w, d, t)).wait_send()
-            ln.over_tensor(A, m, att.at[tensor_peer(t, m)], columns(t)).wait_send()
-            ln.over_tensor(GA, m, gatt.at[tensor_peer(t, m)], rows_at(gall, t)).wait_send()
             ln.over_tensor(R, m, gsum.at[0], line_in.at[m]).wait_send()
-            ln.over_tensor(WL, m, wq_src.at[tensor_peer(t, m)], wq_all.at[m]).wait_send()
-        ln.gather_end(O, wo, wo_of)
+        to_inner(W, lambda g: wpack.at[g], w_at(w, d, t), gone)
+        to_inner(X, lambda g: hid, x_of(t), gone)
+        to_inner(GA, lambda g: gatt.at[g], rows_at(gall, t), gone)
         ln.gather_end(C, cot, c_of)
         ln.gather_end(N, normed2, x_of)
         for m in range(1, 8):
             ln.over_dp(DT, m, tiles.at[d], tiles.at[d]).wait_send()
             ln.over_dp(DR, m, gain.at[0], rows_in.at[d]).wait_send()
-        for m in (2, 4, 6, 1):
-            ln.over_dp(DW, m, w_at(w, d), w_at(w, d)).wait_send()
-            ln.over_dp(DO, m, w_at(wof, d), w_at(wof, d)).wait_send()
-        for m in (2, 4, 6):
-            dd = dp_peer(d, m)
-            ln.over_dp(FW, m, w_at(w, dd), w_at(w, dd), to=1).wait_send()
-            ln.over_dp(FO, m, w_at(wof, dd), w_at(wof, dd), to=1).wait_send()
-        for s in (layer_sum, gn_sum, wo_line_sum, *ff_sums, wo_sum, wq_sum, wo_pair, wq_pair):
+
+        @inner
+        def _():
+            for m in (1, 2, 3):
+                ln.over_tensor(A, m, att.at[tensor_peer(t, m)], columns(t)).wait_send()
+                ln.over_tensor(WL, m, wq_src.at[tensor_peer(t, m)], wq_all.at[m]).wait_send()
+                to_row_owner(tensor_peer(t, m), m).wait_send()
+            for s in (w_plane, wq_sum, wq_pair):
+                s.end()
+
+        for s in (layer_sum, wo_line_sum, *ff_sums, wo_sum):
             s.end()
         for c in stores:
             c.wait()
 
     pl.run_scoped(
         backward,
-        V((4, seq, 128), BF16), V((4, seq, 128), F32), V((2, seq, 128), F32),
-        V((2, seq, 128), F32), V((seq, 8 * HEAD), BF16), V((4, rows, width), BF16),
-        V((4, span, width), BF16), V((4, span, 8 * HEAD), BF16),
-        V((rows, width), BF16), V((rows, width), F32), V((4, wrows, 8 * HEAD), F32),
+        V((8, seq, 128), BF16), V((8, seq, 128), F32), V((4, seq, 128), F32),
+        V((4, seq, 128), F32), V((seq, width), BF16), V((4, rows, width), BF16),
+        V((4, span, width), BF16),
+        V((rows, width), BF16), V((rows, width), F32), V((2, wrows, width), F32),
         V((wrows, width), F32), V((3, half, units), F32),
     )
 
@@ -932,32 +1057,31 @@
     V = pltpu.VMEM
     shapes = dict(
         layer=((rows, width), BF16), gin=((rows, width), F32), gain=((8, 128), F32),
-        wqkv=((4, wrows, 8 * HEAD), F32), wo=((wrows, width), F32),
+        wqkv=((2, wrows, width), F32), wo=((wrows, width), F32),
         mlp=((3, half, units), F32),
     )
     wide = V((seq, width), BF16)
     thin, thin_f = V((rows, width), BF16), V((rows, width), F32)
     four = V((4, rows, width), BF16)
-    pair = V((2, seq, 128), BF16)
+    pair = V((4, seq, 128), BF16)
     outs = pl.pallas_call(
         layer_kernel,
         out_shape=[jax.ShapeDtypeStruct(*v) for v in shapes.values()],
         in_specs=[vmem, hbm] + [vmem] * 6 + [hbm] * 4 + [vmem] * 3,
         out_specs=[hbm] * len(shapes),
         scratch_shapes=[
-            wide, wide, wide, V((width, 8 * HEAD), BF16), V((width, width), BF16),
-            V((8, 4, 8, 128), F32), V((4, seq, 128), BF16), pair, pair,
-            V((4, rows, span), BF16), thin, V((4, 1, seq), F32), V((1, seq), F32),
+            wide, wide, wide, V((width, width), BF16), V((width, width), BF16),
+            V((8, 4, 8, 128), F32), V((8, seq, 128), BF16), pair, pair,
+            V((4, rows, 2 * span), BF16), thin, V((8, 1, seq), F32), V((1, seq), F32),
             V((8, width), F32), thin_f, thin,
-            four, V((4, 3, half, units), BF16), four, V((4, rows, span), BF16), thin_f, thin,
+            four, V((4, 3, half, units), BF16), four, V((2, rows, 2 * span), BF16), thin_f, thin,
             V((1, 1, width), F32),
-            V((seq, span), BF16), four, V((6, 3, half, units // 2), BF16),
+            V((seq, 2 * span), BF16), four, V((6, 3, half, units // 2), BF16),
             V((4, half, width), BF16), V((6, half, width // 2), BF16),
             V((4, wrows, width), BF16), V((4, wrows, width), BF16),
-            V((4, half, 8 * HEAD), BF16), V((6, half, 4 * HEAD), BF16),
-            V((4, wrows, 8 * HEAD), BF16), V((4, wrows, 8 * HEAD), BF16),
+            V((4, wrows, width), BF16), V((4, wrows, width), BF16),
             V((8, 1, width), F32), V((4, 1, width), F32), V((1, 1, width), F32),
-            V((8, 128), F32), V((4, wrows, 8 * HEAD), BF16), V((8, 128), F32),
+            V((8, 128), F32), V((2, wrows, width), BF16), V((8, 128), F32), V((seq, seq), F32),
             pltpu.SemaphoreType.DMA((14, 6)), pltpu.SemaphoreType.DMA((14, 4)),
             pltpu.SemaphoreType.DMA((16, 8)), pltpu.SemaphoreType.DMA((16, 8)),
             pltpu.SemaphoreType.DMA((8,)), pltpu.SemaphoreType.DMA((8,)),
@@ -995,26 +1119,19 @@
         stores.append(c)
 
     wrows, span = query.shape[0], query.shape[1] // 4
-    pair = 2 * HEAD
+    wide = 2 * span
     loads[6].wait()
-    lane = lax.broadcasted_iota(jnp.int32, (wrows, 8 * HEAD), 1)
-    keys = jnp.zeros((wrows, 8 * HEAD), F32)
-    values = jnp.zeros((wrows, 8 * HEAD), F32)
-    for s in range(4):
-        query[:, s * span : (s + 1) * span] = w4[s, :, :span]
-        u = jnp.concatenate([w4[s, :, span:], jnp.zeros((wrows, span), F32)], axis=1)
-        here = (lane >= pair * s) & (lane < pair * (s + 1))
-        keys = jnp.where(here, lane_roll(u, pair * s), keys)
-        values = jnp.where(here, lane_roll(u, pair * s - pair), values)
-    key[...] = keys
-    value[...] = values
+    for g in range(2):
+        query[:, g * wide : (g + 1) * wide] = w4[g, :, :wide]
+        key[:, g * span : (g + 1) * span] = w4[g, :, wide : wide + span]
+        value[:, g * span : (g + 1) * span] = w4[g, :, wide + span :]
     out(query, query_out)
     out(key, key_out)
     out(value, value_out)
     total = (
         jnp.sum(wq[...].astype(F32) * query[...], axis=1, keepdims=True)
-        + jnp.sum(wk[...].astype(F32) * keys, axis=1, keepdims=True)
-        + jnp.sum(wv[...].astype(F32) * values, axis=1, keepdims=True)
+        + jnp.sum(wk[...].astype(F32) * key[...], axis=1, keepdims=True)
+        + jnp.sum(wv[...].astype(F32) * value[...], axis=1, keepdims=True)
     )
     tall = jnp.concatenate(
         [jnp.broadcast_to(total, (wrows, 128)), jnp.zeros((128 - wrows, 128), F32)], axis=0
@@ -1051,7 +1168,7 @@
         in_specs=[hbm] * 6 + [vmem] * 4,
         out_specs=[hbm] * len(shapes),
         scratch_shapes=[
-            V((rows, width), BF16), V(*thin), V((8, 128), F32), V((4, wrows, 8 * HEAD), F32),
+            V((rows, width), BF16), V(*thin), V((8, 128), F32), V((2, wrows, width), F32),
             V(*weight), V((3, half, units), F32), V(*row), V(*weight), V(*narrow), V(*narrow),
             V(*row),
             pltpu.SemaphoreType.DMA((8,)), pltpu.SemaphoreType.DMA((11,)),

time: 240 us -> 233 us (0.971)
  Pallas kernels: 237 us -> 231 us
    pallas_call x1, Pallas kernels: 232 us -> 226 us  [layer(): pl.pallas_call(layer_kernel, out_shape=[jax.ShapeDtypeStruct(*v) for v in...]
where the time goes in v6:
time: 233 us; the launch traced here: 232 us
  Pallas kernels  231 us (99%)
    pallas_call x1, Pallas kernels, layer(): pl.pallas_call(layer_kernel, out_shape=[jax.ShapeDtypeStruct(*v) for v in...  226 us
    pallas_call x1, Pallas kernels, finish(): pl.pallas_call(finish_kernel, out_shape=[jax.ShapeDtypeStruct(*v) for v i...  4.81 us

profile of v6, /device:TPU:4, one launch (start us, length us, event | category | flops | bytes accessed | tf_op | source)
XLA Modules:
  0.0 231.7 jit_solution(7828182761727288953)
XLA Ops:
  0.6 226.1 %layer.1 = (bf16[128,1536]{1,0:T(8,128)(2,1)}, f32[128,1536]{1,0:T(8,128)}, f32[8,128]{1,0:T(8,128)}, f32[2,48,1536]{2,1,0:T(8,128)}, f32[48,1536]{1,0:T(8,128)}, /*index=5*/f32[3,192,1024]{2,1,0:T(8,128)}) custom-call(bf16[128,1536]{1,0:T(8,128)(2,1)} %hid.1, bf16[128,1536]{1,0:T(8,128)(2,1)} %cot.1, s32[1,128]{1,0:T(1,128)} %bitcast.8, ...), custom_call_target="tpu_custom_call" | custom-call | tf_op jit(solution)/shard_map/layer/pallas_call | solution.py:1067
  226.7 4.8 %finish.1 = (bf16[128,1536]{1,0:T(8,128)(2,1)}, f32[128,1536]{1,0:T(8,128)}, f32[1,48]{1,0:T(1,128)}, f32[48,1536]{1,0:T(8,128)}, f32[48,768]{1,0:T(8,128)}, /*i...) custom-call(bf16[128,1536]{1,0:T(8,128)(2,1)} %get-tuple-element.28., ...), custom_call_target="tpu_custom_call" | custom-call | tf_op jit(solution)/shard_map/finish/pallas_call | solution.py:1165

commit v7 on v6

--- a/solution.py
+++ b/solution.py
@@ -527,7 +527,7 @@
         mine[1].wait()
         for i in (1, 2, 3):
             ln.gather_take(O, i, wo_of)
-        o_plane.start()
+        outer(o_plane.start)
         mine[3].wait()
         inner(ln.over_tensor(C, 3, cot, c_of(t)).start)
         outer(lambda: ln.gather_start(C, cot, c_of))
@@ -610,6 +610,7 @@
                 far = (b + 1) * rows
                 bias[:far, b * rows : far] = jnp.where(visible((far, rows), b), 0.0, MASKED)
             w_plane.hand_on()
+            o_plane.start()
             w_plane.take()
             for m in (1, 2, 3):
                 ln.landed_tensor(X, m, x_of(tensor_peer(t, m)))
@@ -838,8 +839,8 @@
                 p = jnp.exp(sc - lse[h, :, here])
                 gp = mm(v, g, NT)
                 gs = (p * (gp - jnp.sum(p * gp, axis=0, keepdims=True))).astype(BF16)
-                gq[h, here, :] = mm(gs, k, TN) * scale
-                gk[c, :far, :] += mm(gs, q) * scale
+                gq[h, here, :] = mm(gs, k, TN)
+                gk[c, :far, :] += mm(gs, q)
                 gv[c, :far, :] += mm(p.astype(BF16), g)
             return carry
 
@@ -856,6 +857,7 @@
                 return lane_roll(u, HEAD * h)
 
             def turned(u):
+                u = u * scale
                 return u * cosine - swap_halves(u) * sine
 
             parts = [
@@ -924,6 +926,19 @@
         @inner
         def _():
             lax.fori_loop(0, 4, head_weights, 0)
+
+        def to_rows(total, dst):
+            lanes = total.lanes
+            for h in range(2):
+                u = total.take(h).astype(BF16)
+                for s in range(4):
+                    dst[s, :, h * lanes : (h + 1) * lanes] = u[s * wrows : (s + 1) * wrows, :]
+
+        to_rows(wo_sum, wo_src)
+        wo_line_sum = LineSum(ln, OL, wo_src, wo_line)
+        wo_line_sum.start()
+        @inner
+        def _():
             wq_pair.take()
             wq_sum.start()
 
@@ -941,22 +956,12 @@
             c.start()
             stores.append(c)
 
-        def to_rows(total, dst):
-            lanes = total.lanes
-            for h in range(2):
-                u = total.take(h).astype(BF16)
-                for s in range(4):
-                    dst[s, :, h * lanes : (h + 1) * lanes] = u[s * wrows : (s + 1) * wrows, :]
-
         def feed_weights(k):
             lanes = units // 2
             for h in range(2):
                 ffw[k, :, h * lanes : (h + 1) * lanes] = ff_sums[k].take(h)
             out(ffw.at[k], mlpw_out.at[k])
 
-        to_rows(wo_sum, wo_src)
-        wo_line_sum = LineSum(ln, OL, wo_src, wo_line)
-        wo_line_sum.start()
         inner(wq_sum.hand_on)
         layer[...] = (resid[...] + msend[t].astype(F32) + layer_sum.take()).astype(BF16)
         out(layer, layer_out)

time: 233 us -> 226 us (0.970)
  Pallas kernels: 231 us -> 222 us
    pallas_call x1, Pallas kernels: 226 us -> 218 us  [layer(): pl.pallas_call(layer_kernel, out_shape=[jax.ShapeDtypeStruct(*v) for v in...]
where the time goes in v7:
time: 226 us; the launch traced here: 223 us
  Pallas kernels  222 us (98%)
    pallas_call x1, Pallas kernels, layer(): pl.pallas_call(layer_kernel, out_shape=[jax.ShapeDtypeStruct(*v) for v in...  218 us
    pallas_call x1, Pallas kernels, finish(): pl.pallas_call(finish_kernel, out_shape=[jax.ShapeDtypeStruct(*v) for v i...  4.81 us

profile of v7, /device:TPU:4, one launch (start us, length us, event | category | flops | bytes accessed | tf_op | source)
XLA Modules:
  0.0 223.2 jit_solution(15237216529004130926)
XLA Ops:
  0.6 217.6 %layer.1 = (bf16[128,1536]{1,0:T(8,128)(2,1)}, f32[128,1536]{1,0:T(8,128)}, f32[8,128]{1,0:T(8,128)}, f32[2,48,1536]{2,1,0:T(8,128)}, f32[48,1536]{1,0:T(8,128)}, /*index=5*/f32[3,192,1024]{2,1,0:T(8,128)}) custom-call(bf16[128,1536]{1,0:T(8,128)(2,1)} %hid.1, bf16[128,1536]{1,0:T(8,128)(2,1)} %cot.1, s32[1,128]{1,0:T(1,128)} %bitcast.8, ...), custom_call_target="tpu_custom_call" | custom-call | tf_op jit(solution)/shard_map/layer/pallas_call | solution.py:1072
  218.3 4.8 %finish.1 = (bf16[128,1536]{1,0:T(8,128)(2,1)}, f32[128,1536]{1,0:T(8,128)}, f32[1,48]{1,0:T(1,128)}, f32[48,1536]{1,0:T(8,128)}, f32[48,768]{1,0:T(8,128)}, /*i...) custom-call(bf16[128,1536]{1,0:T(8,128)(2,1)} %get-tuple-element.28., ...), custom_call_target="tpu_custom_call" | custom-call | tf_op jit(solution)/shard_map/finish/pallas_call | solution.py:1170
